TPU v7x, 128 devices: a whole 4x4x4 slice. The times are simulated.
128 devices in a mesh: line: 4 (over y), xline: 32 (over z, x, core).
Axes of the slice: x: 4, y: 4, z: 4, core: 2. Of those that a mesh axis runs over, the one named last changes fastest.
Arguments:
- traces: bfloat16 [4, 8192, 1024], P('line', 'xline'), may hold values from -6 to 6
- taper: float32 [128], replicated, may hold values from 0.3 to 1
- ray_param: float32 [64], replicated, may hold values from -0.4 to 0.4
- reach: int32 [4, 8192, 4], P('line', 'xline'), may hold values from 0 to 127, all different within a row; in each aligned block of 256 rows (0 to 255, 256 to 511, ..., all dimensions but the last counted through in order) at most 9 rows name the same one
- landing: int32 [4, 8192, 4], P('line', 'xline'), may hold values from 0 to 127
- travel_time: float32 [64, 1024], P('xline'), may hold values from 2 to 40
- amplitude: float32 [64, 1024], P('xline'), may hold values from 0.3 to 3
Outputs:
- image: float32 [4, 1024, 4096], P('line', None, 'xline')
Inputs may be any that keep to these rules, and one draw needn't show every extreme that they name: `reach`: in the rows of one device no tile is named more than 9 times, a bound that some block reaches.
All inputs are finite; a program needn't handle non-finite values.
Results may differ from a plain program's by a relative error of at most 0.0057.
Values may be sent and summed in bfloat16 or wider, within the bound.
No kernel may reach another device: no remote copies, remote signals or barrier semaphores. Data moves between devices by JAX's collectives and lax.ppermute only.
A program may use at most 64 MiB of HBM per device.

v0:
```python
import math

import jax
import jax.numpy as jnp
from jax import lax
from jax.sharding import PartitionSpec as P

X = 128


def with_halo(array, sides, width):
    for axis, dim in sides:
        size, length = (lax.axis_size(axis), array.shape[dim])
        up = [(i, (i + 1) % size) for i in range(size - 1)]
        down = [(j, i) for i, j in up]
        last = lax.slice_in_dim(array, length - width, length, axis=dim)
        leading = lax.slice_in_dim(array, 0, width, axis=dim)
        before = lax.ppermute(last, axis, up)
        after = lax.ppermute(leading, axis, down)
        array = jnp.concatenate([before, array, after], axis=dim)
    return array


def steering(taper, ray_param, window, freq_count):
    offsets = jnp.arange(window, dtype=jnp.float32) - (window - 1) / 2.0
    angular = (jnp.arange(freq_count, dtype=jnp.float32) + 1.0) * (math.pi / freq_count)
    phase = ray_param[:, None, None] * offsets[None, :, None] * angular[None, None, :]
    weight = taper[None, :, None] / math.sqrt(window)
    return (
        (weight * jnp.cos(phase)).astype(jnp.bfloat16),
        (weight * jnp.sin(phase)).astype(jnp.bfloat16),
    )


def kernel_slab(time_row, amp_row, freq_count, factor):
    angular = (jnp.arange(freq_count, dtype=jnp.float32) + 1.0) * (math.pi / freq_count)
    phase = time_row[..., None] * angular
    weight = amp_row[..., None] * factor
    return jnp.concatenate([weight * jnp.cos(phase), weight * jnp.sin(phase)], axis=-1).astype(
        jnp.bfloat16
    )


def slant_stack(halves, cos_weight, sin_weight, half_window, freq_count):
    lower_half = halves[:-1]
    upper_half = halves[1:]
    real_part = jnp.zeros((lower_half.shape[0], cos_weight.shape[0], freq_count), jnp.float32)
    imag_part = jnp.zeros((lower_half.shape[0], cos_weight.shape[0], freq_count), jnp.float32)
    for section, lower in ((lower_half, 0), (upper_half, half_window)):
        cos_part = cos_weight[:, lower : lower + half_window, :]
        sin_part = sin_weight[:, lower : lower + half_window, :]
        data_real = section[..., :freq_count]
        data_imag = section[..., freq_count:]
        real_part = (
            real_part
            + jnp.einsum("nkf,pkf->npf", data_real, cos_part, preferred_element_type=jnp.float32)
            + jnp.einsum("nkf,pkf->npf", data_imag, sin_part, preferred_element_type=jnp.float32)
        )
        imag_part = (
            imag_part
            + jnp.einsum("nkf,pkf->npf", data_imag, cos_part, preferred_element_type=jnp.float32)
            - jnp.einsum("nkf,pkf->npf", data_real, sin_part, preferred_element_type=jnp.float32)
        )
    return jnp.concatenate([real_part, imag_part], axis=-1).astype(jnp.bfloat16)


def on_device(traces, taper, ray_param, reach, landing, travel_time, amplitude):
    freq_count = traces.shape[2] // 2
    window = taper.shape[0]
    half_window = window // 2
    padded = with_halo(traces, (("xline", 1),), window // 4)
    cos_weight, sin_weight = steering(taper, ray_param, window, freq_count)
    centres = padded.shape[1] // half_window - 1
    halves = padded[0].reshape(centres + 1, half_window, 2 * freq_count)
    beam_block = slant_stack(halves, cos_weight, sin_weight, half_window, freq_count)
    ray_count = beam_block.shape[1]
    reach_count = reach.shape[2]
    depth_count = travel_time.shape[1]
    factor = 1.0 / math.sqrt(2.0 * freq_count * centres * ray_count * reach_count / X)
    empty = jnp.zeros((centres, ray_count, depth_count), jnp.bfloat16)
    time_piece = lax.all_gather(travel_time, "xline", axis=0, tiled=True)
    amp_piece = lax.all_gather(amplitude, "xline", axis=0, tiled=True)
    piece_rows = time_piece.shape[0]
    block_rays = max((d for d in range(1, min(piece_rows, 8) + 1) if piece_rows % d == 0))

    def one_block(index, current):
        start = index * block_rays
        time_rows = lax.dynamic_slice_in_dim(time_piece, start, block_rays, 0)
        amp_rows = lax.dynamic_slice_in_dim(amp_piece, start, block_rays, 0)
        kernel = kernel_slab(time_rows, amp_rows, freq_count, factor)
        beams_here = lax.dynamic_slice_in_dim(beam_block, start, block_rays, 1)
        result = jnp.einsum("cgj,gzj->cgz", beams_here, kernel, preferred_element_type=jnp.float32)
        return lax.dynamic_update_slice_in_dim(current, result.astype(jnp.bfloat16), start, 1)

    projected = lax.fori_loop(0, piece_rows // block_rays, one_block, empty)
    proj_rows = projected.reshape(centres * ray_count, depth_count)
    line_count = lax.axis_size("line")
    xline_count = lax.axis_size("xline")
    devices = line_count * xline_count
    row_count = proj_rows.shape[0]
    capacity = max(2, 9 * row_count * reach_count // (8 * devices))
    target = reach[0].reshape(-1)
    column = landing[0].reshape(-1)
    source = jnp.arange(row_count * reach_count, dtype=jnp.int32) // reach_count
    onehot = (target[:, None] == jnp.arange(devices, dtype=jnp.int32)[None, :]).astype(jnp.int32)
    before = jnp.cumsum(onehot, axis=0) - onehot
    slot_rank = jnp.sum(before * onehot, axis=1)
    slot_index = target * capacity + slot_rank
    outgoing = (
        jnp.zeros((devices * capacity, depth_count), jnp.bfloat16)
        .at[slot_index]
        .set(proj_rows[source])
    )
    out_keys = jnp.full((devices * capacity,), -1, jnp.int32).at[slot_index].set(column)
    incoming, in_keys = (
        lax.all_to_all(outgoing, ("line", "xline"), split_axis=0, concat_axis=0, tiled=True),
        lax.all_to_all(out_keys, ("line", "xline"), split_axis=0, concat_axis=0, tiled=True),
    )
    placing = (jnp.arange(X, dtype=jnp.int32)[:, None] == in_keys[None, :]).astype(jnp.bfloat16)
    image_tile = lax.dot_general(
        incoming, placing, (((0,), (1,)), ((), ())), preferred_element_type=jnp.float32
    )
    return image_tile[None]


def solution(mesh):
    placed = (
        P("line", "xline", None),
        P(),
        P(),
        P("line", "xline", None),
        P("line", "xline", None),
        P("xline", None),
        P("xline", None),
    )
    return jax.shard_map(
        on_device, mesh=mesh, in_specs=placed, out_specs=P("line", None, "xline"), check_vma=False
    )
```

profile of v0, /device:TPU:1, one launch (start us, length us, event | category | flops | bytes accessed | tf_op | source)
XLA Modules:
  0.0 863.0 jit_solution(10866048127415013196)
XLA Ops:
  16.3 10.6 %all-to-all-start.1 = ((s32[128,9,1]{1,2,0:T(1,128)}), s32[128,9,1]{1,2,0:T(1,128)S(1)}, u32[]{:S(2)}, u32[]{:S(2)}) async-start(s32[128,9,1]{1,2,0:T(1,128)} %bitcast.14), calls=%async_computation.1 | async-start | bytes 131072 | tf_op jit(solution)/shard_map/all_to_all | solution.py:117
  28.4 64.1 %fusion.18 = (bf16[64,128,512]{1,0,2:T(8,128)(2,1)}, bf16[64,128,512]{1,0,2:T(8,128)(2,1)}) fusion(f32[512]{0:T(512)S(1)} %add_multiply_fusion.1, f32[64,128]{1,0:T(8,128)S(1)} %broadcast_multiply_fusion, f32[128]{0:T(128)S(1)} %broadcast_multiply_fusion.2), kind=kLoop, calls=%fused_computation.25 | loop fusion | flops 20971520 | bytes 16812544 | tf_op jit(solution)/shard_map/convert_element_type | solution.py:30
  92.5 25.8 %all-gather = f32[32,2,1024]{2,1,0:T(2,128)S(1)} all-gather(f32[1,2,1024]{2,1,0:T(2,128)S(1)} %bitcast.48), channel_id=1, replica_groups=mesh['line'=4,'xline'=32] {'xline'}, dimensions={0}, use_global_device_ids=true | all-gather | bytes 270336 | tf_op jit(solution)/shard_map/all_gather | solution.py:82
  118.5 24.6 %all-gather.1 = f32[32,2,1024]{2,1,0:T(2,128)S(1)} all-gather(f32[1,2,1024]{2,1,0:T(2,128)S(1)} %bitcast.49), channel_id=1, replica_groups=mesh['line'=4,'xline'=32] {'xline'}, dimensions={0}, use_global_device_ids=true | all-gather | bytes 270336 | tf_op jit(solution)/shard_map/all_gather | solution.py:81
  144.8 7.9 fusion.31
  152.8 9.0 %fusion.29 = f32[512,64,4]{1,2,0:T(4,128)} fusion(bf16[4,64,512]{1,0,2:T(4,128)(2,1)S(1)} %copy.39, bf16[64,128,512]{1,0,2:T(8,128)(2,1)} %get-tuple-element.138), kind=kOutput, calls=%fused_computation.36 | convolution fusion | flops 16777216 | bytes 9175040 | tf_op jit(solution)/shard_map/nkf,pkf->npf/dot_general | solution.py:62
  161.8 5.4 fusion.39
  167.2 6.7 fusion.42
  173.9 8.3 fusion.45
  182.2 4.5 fusion.63
  186.8 8.1 fusion.48
  194.9 4.6 fusion.66
  201.1 579.7 %while.13 = (s32[]{:T(128)}, bf16[4,64,1024]{2,1,0:T(8,128)(2,1)S(1)}, f32[64,1024]{1,0:T(8,128)S(1)}, f32[64,1024]{1,0:T(8,128)S(1)}, bf16[4,64,1024]{2,0,1:T(4...) while((s32[]{:T(128)}, bf16[4,64,1024]{2,1,0:T(8,128)(2,1)S(1)}, f32[64,1024]{1,0:T(8,128)S(1)}, ...), condition=%wide.region_4.5_spmd, body=%wide.region_3.4_spmd.sunk | while | flops 121676800 | bytes 34017428 | solution.py:95
  201.2 65.1 %fusion.96 = (bf16[8,1024,512]{2,1,0:T(8,128)(2,1)S(1)}, bf16[8,1024,512]{2,1,0:T(8,128)(2,1)}) fusion(f32[512]{0:T(512)S(1)} %add_multiply_fusion.3, f32[8,1024]{1,0:T(8,128)S(1)} %get-tuple-element.174, f32[8,1024]{1,0:T(8,128)S(1)} %get-tuple-element.175), kind=kLoop, calls=%fused_computation.6.clone.1 | loop fusion | flops 20971520 | bytes 16844800 | tf_op jit(solution)/shard_map/convert
  266.3 7.2 fusion.97
  273.6 65.1 %fusion.96 = (bf16[8,1024,512]{2,1,0:T(8,128)(2,1)S(1)}, bf16[8,1024,512]{2,1,0:T(8,128)(2,1)}) fusion(f32[512]{0:T(512)S(1)} %add_multiply_fusion.3, f32[8,1024]{1,0:T(8,128)S(1)} %get-tuple-element.174, f32[8,1024]{1,0:T(8,128)S(1)} %get-tuple-element.175), kind=kLoop, calls=%fused_computation.6.clone.1 | loop fusion | flops 20971520 | bytes 16844800 | tf_op jit(solution)/shard_map/convert
  338.8 7.2 fusion.97
  346.1 65.1 %fusion.96 = (bf16[8,1024,512]{2,1,0:T(8,128)(2,1)S(1)}, bf16[8,1024,512]{2,1,0:T(8,128)(2,1)}) fusion(f32[512]{0:T(512)S(1)} %add_multiply_fusion.3, f32[8,1024]{1,0:T(8,128)S(1)} %get-tuple-element.174, f32[8,1024]{1,0:T(8,128)S(1)} %get-tuple-element.175), kind=kLoop, calls=%fused_computation.6.clone.1 | loop fusion | flops 20971520 | bytes 16844800 | tf_op jit(solution)/shard_map/convert
  411.2 7.2 fusion.97
  418.6 65.1 %fusion.96 = (bf16[8,1024,512]{2,1,0:T(8,128)(2,1)S(1)}, bf16[8,1024,512]{2,1,0:T(8,128)(2,1)}) fusion(f32[512]{0:T(512)S(1)} %add_multiply_fusion.3, f32[8,1024]{1,0:T(8,128)S(1)} %get-tuple-element.174, f32[8,1024]{1,0:T(8,128)S(1)} %get-tuple-element.175), kind=kLoop, calls=%fused_computation.6.clone.1 | loop fusion | flops 20971520 | bytes 16844800 | tf_op jit(solution)/shard_map/convert
  483.7 7.2 fusion.97
  491.0 65.1 %fusion.96 = (bf16[8,1024,512]{2,1,0:T(8,128)(2,1)S(1)}, bf16[8,1024,512]{2,1,0:T(8,128)(2,1)}) fusion(f32[512]{0:T(512)S(1)} %add_multiply_fusion.3, f32[8,1024]{1,0:T(8,128)S(1)} %get-tuple-element.174, f32[8,1024]{1,0:T(8,128)S(1)} %get-tuple-element.175), kind=kLoop, calls=%fused_computation.6.clone.1 | loop fusion | flops 20971520 | bytes 16844800 | tf_op jit(solution)/shard_map/convert
  556.1 7.2 fusion.97
  563.5 65.1 %fusion.96 = (bf16[8,1024,512]{2,1,0:T(8,128)(2,1)S(1)}, bf16[8,1024,512]{2,1,0:T(8,128)(2,1)}) fusion(f32[512]{0:T(512)S(1)} %add_multiply_fusion.3, f32[8,1024]{1,0:T(8,128)S(1)} %get-tuple-element.174, f32[8,1024]{1,0:T(8,128)S(1)} %get-tuple-element.175), kind=kLoop, calls=%fused_computation.6.clone.1 | loop fusion | flops 20971520 | bytes 16844800 | tf_op jit(solution)/shard_map/convert
  628.6 7.2 fusion.97
  635.9 65.1 %fusion.96 = (bf16[8,1024,512]{2,1,0:T(8,128)(2,1)S(1)}, bf16[8,1024,512]{2,1,0:T(8,128)(2,1)}) fusion(f32[512]{0:T(512)S(1)} %add_multiply_fusion.3, f32[8,1024]{1,0:T(8,128)S(1)} %get-tuple-element.174, f32[8,1024]{1,0:T(8,128)S(1)} %get-tuple-element.175), kind=kLoop, calls=%fused_computation.6.clone.1 | loop fusion | flops 20971520 | bytes 16844800 | tf_op jit(solution)/shard_map/convert
  701.1 7.2 fusion.97
  708.4 65.1 %fusion.96 = (bf16[8,1024,512]{2,1,0:T(8,128)(2,1)S(1)}, bf16[8,1024,512]{2,1,0:T(8,128)(2,1)}) fusion(f32[512]{0:T(512)S(1)} %add_multiply_fusion.3, f32[8,1024]{1,0:T(8,128)S(1)} %get-tuple-element.174, f32[8,1024]{1,0:T(8,128)S(1)} %get-tuple-element.175), kind=kLoop, calls=%fused_computation.6.clone.1 | loop fusion | flops 20971520 | bytes 16844800 | tf_op jit(solution)/shard_map/convert
  773.5 7.2 fusion.97
  780.8 13.6 %scatter_custom_fusion = bf16[1152,1024]{1,0:T(8,128)(2,1)S(1)} fusion(s32[1024]{0:T(1024)S(1)} %bitcast.51, bf16[256,1024]{1,0:T(8,128)(2,1)S(1)} %bitcast.45, s32[1024]{0:T(1024)S(1)} %broadcast_clamp_fusion, bf16[]{:T(256)} %constant.77.clone.1), kind=kCustom, calls=%fused_computation.44 | custom fusion | bytes 2359298 | tf_op jit(solution)/shard_map/scatter | solution.py:112
  797.3 6.8 all-to-all-start
  805.7 51.1 %all-to-all-done = bf16[128,9,1024]{2,1,0:T(8,128)(2,1)} async-done(((bf16[128,9,1024]{2,1,0:T(8,128)(2,1)}), bf16[128,9,1024]{2,1,0:T(8,128)(2,1)}, u32[]{:S(2)}, u32[]{:S(2)}) %all-to-all-start) | async-done | bytes 2359328 | tf_op jit(solution)/shard_map/all_to_all | solution.py:116
  (91 shorter events, 31.7 us)
Async XLA Ops:
  0.9 142.4 %collective-permute-start = (bf16[1,32,1024]{2,1,0:T(8,128)(2,1)S(1)}, bf16[1,32,1024]{2,1,0:T(8,128)(2,1)S(1)}, u32[]{:S(2)}, u32[]{:S(2)}) collective-permute-start(bf16[1,32,1024]{2,1,0:T(8,128)(2,1)S(1)} %get-tuple-element.134), channel_id=1, source_target_pairs={{0,1},{1,2},{2,3},{3,4},{4,5},{5,6},{6,7},{7,8},{8,9},{9,10},{10,1... | collective-permute-start | bytes 196616 | tf_op jit(solution)/shard_map/ppermute | solution.py:18
  5.4 137.9 %collective-permute-start.1 = (bf16[1,32,1024]{2,1,0:T(8,128)(2,1)S(1)}, bf16[1,32,1024]{2,1,0:T(8,128)(2,1)S(1)}, u32[]{:S(2)}, u32[]{:S(2)}) collective-permute-start(bf16[1,32,1024]{2,1,0:T(8,128)(2,1)S(1)} %get-tuple-element.133), channel_id=1, source_target_pairs={{1,0},{2,1},{3,2},{4,3},{5,4},{6,5},{7,6},{8,7},{9,8},{10,9},{11,1... | collective-permute-start | bytes 196616 | tf_op jit(solution)/shard_map/ppermute | solution.py:19
  16.3 781.0 %all-to-all-start.1 = ((s32[128,9,1]{1,2,0:T(1,128)}), s32[128,9,1]{1,2,0:T(1,128)S(1)}, u32[]{:S(2)}, u32[]{:S(2)}) async-start(s32[128,9,1]{1,2,0:T(1,128)} %bitcast.14), calls=%async_computation.1 | async-start | bytes 131072 | tf_op jit(solution)/shard_map/all_to_all | solution.py:117
  28.4 64.1 %copy-start.1 = (f32[2,1024]{1,0:T(2,128)S(1)}, f32[2,1024]{1,0:T(2,128)}, u32[]{:S(2)}) copy-start(f32[2,1024]{1,0:T(2,128)} %param.15) | copy-start | bytes 24580
  28.4 90.1 %copy-start.2 = (f32[2,1024]{1,0:T(2,128)S(1)}, f32[2,1024]{1,0:T(2,128)}, u32[]{:S(2)}) copy-start(f32[2,1024]{1,0:T(2,128)} %param.14) | copy-start | bytes 24580
  28.4 114.9 %copy-start = (bf16[1,256,1024]{2,1,0:T(8,128)(2,1)S(1)}, bf16[1,256,1024]{2,1,0:T(8,128)(2,1)}, u32[]{:S(2)}) copy-start(bf16[1,256,1024]{2,1,0:T(8,128)(2,1)} %param.9) | copy-start | bytes 1572868
  144.8 16.9 %slice-start.2 = ((s8[8388608]{0:T(1024)(128)(4,1)}), s8[4194304]{0:T(1024)(128)(4,1)S(1)}, s32[]{:S(2)}) async-start(s8[8388608]{0:T(1024)(128)(4,1)} %bitcast.41), calls=%async_computation.4 | async-start | bytes 8388608
  152.8 9.0 %slice-start.3 = ((s8[8388608]{0:T(1024)(128)(4,1)}), s8[4194304]{0:T(1024)(128)(4,1)S(1)}, s32[]{:S(2)}) async-start(s8[8388608]{0:T(1024)(128)(4,1)} %bitcast.41), calls=%async_computation.5 | async-start | bytes 8388608
  167.2 15.0 %slice-start = ((s8[8388608]{0:T(1024)(128)(4,1)}), s8[4194304]{0:T(1024)(128)(4,1)S(1)}, s32[]{:S(2)}) async-start(s8[8388608]{0:T(1024)(128)(4,1)} %bitcast.39), calls=%async_computation.2 | async-start | bytes 8388608
  173.9 8.3 slice-start.1
  182.2 4.6 copy-start.3
  797.3 59.5 %all-to-all-start = ((bf16[128,9,1024]{2,1,0:T(8,128)(2,1)}), bf16[128,9,1024]{2,1,0:T(8,128)(2,1)}, u32[]{:S(2)}, u32[]{:S(2)}) async-start(bf16[128,9,1024]{2,1,0:T(8,128)(2,1)} %all_to_all.14), calls=%async_computation | async-start | bytes 8388608 | tf_op jit(solution)/shard_map/all_to_all | solution.py:116
where the time goes:
time: 869 us; the launch traced here: 863 us
  other arithmetic  590 us (68%)
  matrix products  114 us (13%)
  waiting for transfers between devices  51.1 us (6%)
  blocking collectives  50.4 us (6%)
  local copies, waits for them, and re-layouts  32.6 us (4%)
  starting transfers between devices  23.9 us (3%)
    another operation x11, other arithmetic  521 us
    convert_element_type x1, other arithmetic, steering(): (weight * jnp.cos(phase)).astype(jnp.bfloat16)  64.1 us
    dot_general x8, matrix products, one_block(): jnp.einsum('cgj,gzj->cgz', beams_here, kernel, preferred_element_type=jnp...  58 us
    all_to_all x1, waiting for transfers between devices, on_device(): lax.all_to_all(outgoing, ('line', 'xline'), split_axis=0, concat_axis=0,...  51.1 us
    all_gather x1, blocking collectives, on_device(): amp_piece = lax.all_gather(amplitude, 'xline', axis=0, tiled=True)  25.8 us
    all_gather x1, blocking collectives, on_device(): time_piece = lax.all_gather(travel_time, 'xline', axis=0, tiled=True)  24.6 us
  transfers between devices with their start and end apart: 4, of which 1 were waited for; matrix products, arithmetic and copies ran while one was open for 84% of the time, Pallas kernels for 0%

commit v1 on v0

v1 whole, which is shorter than its diff:
```python
import functools
import math

import jax
import jax.numpy as jnp
import numpy as np
from jax import lax
from jax.experimental import pallas as pl
from jax.experimental.pallas import tpu as pltpu
from jax.sharding import PartitionSpec as P

X = 128
FINE = 128
SLOTS = 9


def iota(shape, dim):
    return lax.broadcasted_iota(jnp.int32, shape, dim)


def fold_matrix():
    half = FINE // 2
    plus = np.zeros((FINE, half), np.float32)
    minus = np.zeros((FINE, half), np.float32)
    for m in range(half):
        plus[half + m, m] = plus[half - 1 - m, m] = 1.0
        minus[half + m, m], minus[half - 1 - m, m] = 1.0, -1.0
    zero = np.zeros_like(plus)
    real = np.concatenate([plus, zero, zero, -minus], 1)
    imag = np.concatenate([zero, minus, plus, zero], 1)
    return np.concatenate([real, imag], 0)


def slant_kernel(before, own, after, tap, ray, flip, fold, out, combos, beams):
    freqs = combos.shape[0] * 128
    half = combos.shape[1]
    centres = combos.shape[2] // 4
    flat = combos.reshape(freqs // 128, half * 4 * centres, 128)
    for n in range(centres):
        start = n * half - half // 2
        if n == 0:
            low = jnp.concatenate([before[...], own[: half // 2]], 0)
        else:
            low = own[start : start + half]
        if n == centres - 1:
            high = jnp.concatenate([own[start + half :], after[...]], 0)
        else:
            high = own[start + half : start + 2 * half]
        turned = jnp.dot(flip[...], low, preferred_element_type=jnp.float32) * tap[0]
        high = high.astype(jnp.float32) * tap[1]
        total, diff = high + turned, high - turned
        for block in range(freqs // 128):
            for q in range(4):
                value = (total, diff)[q // 2]
                cut = (q % 2) * freqs + block * 128
                rows = pl.ds(q * centres + n, half, stride=4 * centres)
                flat[block, rows, :] = value[:, cut : cut + 128]

    rays = ray.shape[0]
    group = 2
    blocks = rays // (8 * group)

    def one_tile(tile, carry):
        block, first = tile // blocks, (tile % blocks) * 8 * group
        angular = (iota((8, 128), 1) + (block * 128 + 1)).astype(jnp.float32) * (math.pi / freqs)
        state = []
        steps = []
        for g in range(group):
            rows = pl.ds(pl.multiple_of(first + 8 * g, 8), 8)
            angle = ray[rows, :] * 0.5 * angular
            c, s = jnp.cos(angle), jnp.sin(angle)
            state += [c, s]
            steps += [(1.0 - 2.0 * s * s, 2.0 * s * c)]
        zero = jnp.zeros((8, 128), jnp.float32)
        sums = [zero] * (2 * group * centres)

        def one_offset(j, current):
            state, sums = list(current[0]), list(current[1])
            for n in range(centres):
                pr, pi, mr, mi = (
                    jnp.broadcast_to(combos[block, j, q * centres + n : q * centres + n + 1, :], (8, 128))
                    for q in range(4)
                )
                for g in range(group):
                    c, s = state[2 * g], state[2 * g + 1]
                    at = 2 * (g * centres + n)
                    sums[at] = sums[at] + (c * pr + s * mi)
                    sums[at + 1] = sums[at + 1] + (c * pi - s * mr)
            for g in range(group):
                c, s = state[2 * g], state[2 * g + 1]
                cs, ss = steps[g]
                state[2 * g], state[2 * g + 1] = c * cs - s * ss, s * cs + c * ss
            return tuple(state), tuple(sums)

        state, sums = lax.fori_loop(0, half, one_offset, (tuple(state), tuple(sums)), unroll=4)
        for g in range(group):
            for n in range(centres):
                at = 2 * (g * centres + n)
                row = pl.multiple_of((block * centres + n) * rays + first + 8 * g, 8)
                beams[pl.ds(row, 8), 0:128] = sums[at]
                beams[pl.ds(row, 8), 128:256] = sums[at + 1]
        return carry

    lax.fori_loop(0, (freqs // 128) * blocks, one_tile, 0)
    rows = centres * rays
    flat = out.reshape(rays * out.shape[1], 128)
    for block in range(freqs // 128):
        folded = jnp.dot(
            beams[block * rows : (block + 1) * rows].astype(jnp.bfloat16),
            fold[...],
            preferred_element_type=jnp.float32,
        )
        for n in range(centres):
            for v in range(2):
                row = (2 * block + v) * centres + n
                value = folded[n * rays : (n + 1) * rays, 128 * v : 128 * (v + 1)]
                flat[pl.ds(row, rays, stride=out.shape[1]), :] = value


def project_kernel(factor, coarse, centres, times, folded, rank, keys, out, fine, outer, proj):
    half = FINE // 2
    blocks = fine.shape[0]
    bases = times.shape[0]
    upper = iota((2 * centres, 128 * blocks), 0) < centres

    def one_group(base, r):
        c0s, s0s, c1s, s1s = [], [], [], []
        for zb in range(blocks):
            cols = slice(zb * 128, zb * 128 + 128)
            t = times[base, pl.ds(8 * r + zb, 8, stride=32), :]
            amp = times[base, pl.ds(16 + 8 * r + zb, 8, stride=32), :] * factor
            angle = t * (math.pi / (2 * coarse * FINE))
            c0, s0 = jnp.cos(angle), jnp.sin(angle)
            c1, s1 = 1.0 - 2.0 * s0 * s0, 2.0 * s0 * c0
            c, s = c1, s1
            for _ in range(6):
                c, s = 1.0 - 2.0 * s * s, 2.0 * s * c
            ca, sa = (c * c0 - s * s0) * amp, (s * c0 + c * s0) * amp
            cb, sb = 1.0 - 2.0 * s * s, 2.0 * s * c
            for a in range(coarse):
                outer[16 * a : 16 * a + 8, cols] = ca
                outer[16 * a + 8 : 16 * a + 16, cols] = sa
                ca, sa = ca * cb - sa * sb, sa * cb + ca * sb
            c0s, s0s, c1s, s1s = c0s + [c0], s0s + [s0], c1s + [c1], s1s + [s1]

        def one_step(m, state):
            cs, ss = state
            row, low = pl.multiple_of(m * 8, 8), pl.multiple_of((half + m) * 8, 8)
            for zb in range(blocks):
                fine[zb, pl.ds(row, 8), :] = cs[zb]
                fine[zb, pl.ds(low, 8), :] = ss[zb]
            turned = [
                (c * c1 - s * s1, s * c1 + c * s1) for c, s, c1, s1 in zip(cs, ss, c1s, s1s)
            ]
            return tuple(c for c, _ in turned), tuple(s for _, s in turned)

        lax.fori_loop(0, half, one_step, (tuple(c0s), tuple(s0s)), unroll=4)
        for i in range(8):
            p = base * 16 + 2 * i + r
            weights = jnp.concatenate(
                [fine[zb, pl.ds(i, FINE, stride=8), :].astype(jnp.bfloat16) for zb in range(blocks)],
                1,
            )
            rows = folded[p].astype(jnp.bfloat16)
            parts = jnp.dot(rows, weights, preferred_element_type=jnp.float32)
            total = jnp.zeros(upper.shape, jnp.float32)
            for a in range(coarse):
                turn = jnp.where(
                    upper,
                    jnp.broadcast_to(outer[16 * a + i : 16 * a + i + 1, :], upper.shape),
                    jnp.broadcast_to(outer[16 * a + 8 + i : 16 * a + 9 + i, :], upper.shape),
                )
                total = total + parts[2 * centres * a : 2 * centres * (a + 1)] * turn
            total = total + pltpu.roll(total, centres, 0)
            if i % 2 == 0:
                held = total
            else:
                proj[(r * bases + base) * 4 + i // 2] = jnp.where(upper, held, total)

    def one_base(base, carry):
        one_group(base, 0)
        one_group(base, 1)
        return carry

    lax.fori_loop(0, bases, one_base, 0)

    sends = proj[...].reshape(-1, 128 * blocks).astype(jnp.bfloat16)
    devices, rows = rank.shape
    ranks = jnp.broadcast_to(rank[...][:, None, :], (devices, 8, rows)).reshape(devices * 8, rows)
    lane8 = iota((devices * 8, rows), 0) % 8
    pick = (ranks == lane8.astype(jnp.float32)).astype(jnp.bfloat16)
    for k in range(4):
        y = jnp.dot(pick, sends[:, 256 * k : 256 * (k + 1)], preferred_element_type=jnp.float32)
        pair = [y[:, :128].reshape(devices, 8, 128), y[:, 128:].reshape(devices, 8, 128)]
        out[:, 16 * k : 16 * (k + 1), :] = jnp.concatenate(pair, 1).astype(jnp.bfloat16)
    last = jnp.zeros((devices * 8, 128), jnp.float32)
    for k in range(8):
        pick = ((ranks == 8.0) & (lane8 == k)).astype(jnp.bfloat16)
        last += jnp.dot(pick, sends[:, 128 * k : 128 * (k + 1)], preferred_element_type=jnp.float32)
    tags = jnp.broadcast_to(keys[...][:, None, :], (devices, 8, 128))
    pair = [last.reshape(devices, 8, 128), tags]
    out[:, 64:80, :] = jnp.concatenate(pair, 1).astype(jnp.bfloat16)


def route_kernel(reach, landing, earlier, rank, keys):
    devices, rows = rank.shape
    tile = iota((devices, rows), 0)
    named = jnp.zeros((devices, rows), jnp.float32)
    column = jnp.zeros((devices, rows), jnp.float32)
    for t in range(reach.shape[0]):
        hit = jnp.broadcast_to(reach[t : t + 1, :], (devices, rows)) == tile
        land = jnp.broadcast_to(landing[t : t + 1, :], (devices, rows)).astype(jnp.float32)
        named = named + jnp.where(hit, 1.0, 0.0)
        column = column + jnp.where(hit, land + 1.0, 0.0)
    count = jnp.dot(named.astype(jnp.bfloat16), earlier[...], preferred_element_type=jnp.float32)
    slot = jnp.where(named > 0.0, count, -1.0)
    rank[...] = slot
    lane = iota((devices, 128), 1)
    table = jnp.zeros((devices, 128), jnp.float32)
    for k in range(SLOTS):
        value = jnp.sum(jnp.where(slot == k, column, 0.0), axis=1, keepdims=True)
        table = jnp.where(lane == k, value, table)
    keys[...] = table - 1.0


def place_kernel(incoming, image):
    devices = incoming.shape[0]
    tags = incoming[:, 64:80, :].astype(jnp.float32)[:, 8:16, :]
    tags = jnp.concatenate([tags, tags], 1).reshape(devices * 16, 128)
    lane = iota((devices * 16, 128), 1)
    row = iota((devices * 16, 128), 0) % 16
    key = jnp.sum(jnp.where(lane == row % 8, tags, 0.0), axis=1, keepdims=True)
    key9 = jnp.sum(jnp.where(lane == 8, tags, 0.0), axis=1, keepdims=True)
    lanes = lane.astype(jnp.float32)
    hit = key == lanes
    both = jnp.concatenate(
        [
            (hit & (row < 8)).astype(jnp.bfloat16),
            (hit & (row >= 8)).astype(jnp.bfloat16),
        ],
        1,
    )
    hit9 = key9 == lanes
    contract = (((0,), (0,)), ((), ()))
    tail = incoming[:, 64:80, :].reshape(devices * 16, 128)
    for k in range(4):
        rows = incoming[:, 16 * k : 16 * (k + 1), :].reshape(devices * 16, 128)
        y = lax.dot_general(rows, both, contract, preferred_element_type=jnp.float32)
        nine = jnp.concatenate(
            [(hit9 & (row == 2 * k + q)).astype(jnp.bfloat16) for q in range(2)], 1
        )
        y += lax.dot_general(tail, nine, contract, preferred_element_type=jnp.float32)
        image[256 * k : 256 * k + 128, :] = y[:, :128]
        image[256 * k + 128 : 256 * (k + 1), :] = y[:, 128:]


def vmem(count):
    return [pl.BlockSpec(memory_space=pltpu.VMEM)] * count


def call(kernel, shapes, args, scratch=()):
    return pl.pallas_call(
        kernel,
        out_shape=shapes,
        in_specs=vmem(len(args)),
        out_specs=jax.tree.map(lambda _: pl.BlockSpec(memory_space=pltpu.VMEM), shapes),
        scratch_shapes=list(scratch),
        compiler_params=pltpu.CompilerParams(vmem_limit_bytes=56 * 1024 * 1024),
    )(*args)


def on_device(traces, taper, ray_param, reach, landing, travel_time, amplitude):
    f32, bf16 = jnp.float32, jnp.bfloat16
    freqs = traces.shape[2] // 2
    window = taper.shape[0]
    half = window // 2
    rays = ray_param.shape[0]
    rows = traces.shape[1]
    centres = rows // half
    depth = travel_time.shape[1]
    reach_count = reach.shape[2]
    line_count, size = lax.axis_size("line"), lax.axis_size("xline")
    devices = line_count * size
    coarse = freqs // FINE
    factor = 1.0 / math.sqrt(2.0 * freqs * centres * rays * reach_count / X)

    own = traces[0]
    up = [(i, i + 1) for i in range(size - 1)]
    down = [(j, i) for i, j in up]
    before = lax.ppermute(own[rows - half // 2 :], "xline", up)
    after = lax.ppermute(own[: half // 2], "xline", down)
    mine = jnp.concatenate([travel_time.reshape(-1, 128), amplitude.reshape(-1, 128)], 0)
    mine = jnp.broadcast_to(mine[None], (size,) + mine.shape)
    times = lax.all_to_all(mine, "xline", split_axis=0, concat_axis=0, tiled=True)
    times = times.reshape(size // 8, 8 * mine.shape[1], 128)

    def beam_order(table):
        table = table.reshape(centres, rays // 16, 4, 2, 2, reach_count)
        return table.transpose(5, 4, 1, 2, 3, 0).reshape(reach_count, centres * rays)


    beam_count = centres * rays
    earlier = np.triu(np.ones((beam_count, beam_count), np.float32), 1)
    rank, keys = call(
        route_kernel,
        (
            jax.ShapeDtypeStruct((devices, beam_count), f32),
            jax.ShapeDtypeStruct((devices, 128), f32),
        ),
        (beam_order(reach[0]), beam_order(landing[0]), jnp.asarray(earlier, bf16)),
    )

    weight = taper * (1.0 / math.sqrt(window))
    tap = jnp.stack([weight[:half][::-1], weight[half:]])[:, :, None]
    flip = jnp.asarray(np.eye(half, dtype=np.float32)[::-1], bf16)
    folded = call(
        slant_kernel,
        jax.ShapeDtypeStruct((rays, 2 * coarse * centres, FINE), f32),
        (before, own, after, tap, ray_param[:, None], flip, jnp.asarray(fold_matrix(), bf16)),
        [
            pltpu.VMEM((freqs // 128, half, 4 * centres, 128), f32),
            pltpu.VMEM((coarse * beam_count, 2 * FINE), f32),
        ],
    )
    outgoing = call(
        functools.partial(project_kernel, factor, coarse, centres),
        jax.ShapeDtypeStruct((devices, 80, 128), bf16),
        (times, folded, rank, keys),
        [
            pltpu.VMEM((depth // 128, 8 * FINE, 128), f32),
            pltpu.VMEM((16 * coarse, depth), f32),
            pltpu.VMEM((beam_count // (2 * centres), 2 * centres, depth), f32),
        ],
    )
    incoming = lax.all_to_all(
        outgoing, ("line", "xline"), split_axis=0, concat_axis=0, tiled=True
    )
    image = call(place_kernel, jax.ShapeDtypeStruct((depth, X), f32), (incoming,))
    return image[None]


def solution(mesh):
    placed = (
        P("line", "xline", None),
        P(),
        P(),
        P("line", "xline", None),
        P("line", "xline", None),
        P("xline", None),
        P("xline", None),
    )
    return jax.shard_map(
        on_device, mesh=mesh, in_specs=placed, out_specs=P("line", None, "xline"), check_vma=False
    )
```

time: 869 us -> 119 us (0.14)
  other arithmetic: 590 us -> 0.67 us
  matrix products: 114 us -> 0 us
  waiting for transfers between devices: 51.1 us -> 0.01 us
  Pallas kernels: 0 us -> 44.9 us
  local copies, waits for them, and re-layouts: 32.6 us -> 11.2 us
    another operation x11 -> x0, other arithmetic: 521 us -> none
    dot_general x17 -> x0, matrix products: 114 us -> none  [the longest x8 58 us: one_block(): jnp.einsum('cgj,gzj->cgz', beams_here, kernel, preferred_element_type=jnp...]
    convert_element_type x1 -> x0, other arithmetic: 64.1 us -> none  [steering(): (weight * jnp.cos(phase)).astype(jnp.bfloat16)]
    all_to_all x2 -> x1, waiting for transfers between devices: 51.1 us -> 0.01 us  [on_device(): lax.all_to_all(mine, 'xline', split_axis=0, concat_axis=0, tiled=True)]
    all_gather x2 -> x0, blocking collectives: 50.4 us -> none  [the longest x1 25.8 us: on_device(): amp_piece = lax.all_gather(amplitude, 'xline', axis=0, tiled=True)]
    all_to_all x0 -> x1, blocking collectives: none -> 45.6 us  [on_device(): lax.all_to_all(outgoing, ('line', 'xline'), split_axis=0, concat_axis=0,...]
    pallas_call x0 -> x4, Pallas kernels: none -> 44.9 us  [call(): pl.pallas_call(kernel, out_shape=shapes, in_specs=vmem(len(args)), out_sp...]
    scatter x2 -> x0, local copies, waits for them, and re-layouts: 18 us -> none  [the longest x1 13.6 us: on_device(): outgoing = jnp.zeros((devices * capacity, depth_count), jnp.bfloat16).at[...]
  transfers between devices with their start and end apart: 4 -> 3, of which waited for: 1 -> 0; matrix products, arithmetic and copies ran while one was open for 84% -> 8% of each run, Pallas kernels for 0% -> 16%
where the time goes in v1:
time: 119 us
  blocking collectives  45.6 us (38%)
  Pallas kernels  44.9 us (38%)
  starting transfers between devices  16.1 us (14%)
  local copies, waits for them, and re-layouts  11.2 us (9%)
    all_to_all x1, blocking collectives, on_device(): lax.all_to_all(outgoing, ('line', 'xline'), split_axis=0, concat_axis=0,...  45.6 us
    pallas_call x4, Pallas kernels, call(): pl.pallas_call(kernel, out_shape=shapes, in_specs=vmem(len(args)), out_sp...  44.9 us
    all_to_all x1, starting transfers between devices, on_device(): lax.all_to_all(mine, 'xline', split_axis=0, concat_axis=0, tiled=True)  9.69 us
    ppermute x1, starting transfers between devices, on_device(): after = lax.ppermute(own[:half // 2], 'xline', down)  3.33 us
    ppermute x1, starting transfers between devices, on_device(): before = lax.ppermute(own[rows - half // 2:], 'xline', up)  3.1 us
    unnamed x8, local copies, waits for them, and re-layouts  3.05 us
  transfers between devices with their start and end apart: 3, of which 0 were waited for; matrix products, arithmetic and copies ran while one was open for 8% of the time, Pallas kernels for 16%

profile of v1, /device:TPU:1, one launch (start us, length us, event | category | flops | bytes accessed | tf_op | source)
XLA Modules:
  0.0 118.7 jit_solution(7627305891887189117)
XLA Ops:
  0.0 0.9 slice_bitcast_fusion
  0.9 3.3 %collective-permute-start.1 = (bf16[32,1024]{1,0:T(8,128)(2,1)S(1)}, bf16[32,1024]{1,0:T(8,128)(2,1)S(1)}, u32[]{:S(2)}, u32[]{:S(2)}) collective-permute-start(bf16[32,1024]{1,0:T(8,128)(2,1)S(1)} %get-tuple-element.9), channel_id=1, source_target_pairs={{1,0},{2,1},{3,2},{4,3},{5,4},{6,5},{7,6},{8,7},{9,8},{10,9},{11,1... | collective-permute-start | bytes 196616 | tf_op jit(solution)/shard_map/ppermute | solution.py:291
  4.2 3.1 %collective-permute-start = (bf16[32,1024]{1,0:T(8,128)(2,1)S(1)}, bf16[32,1024]{1,0:T(8,128)(2,1)S(1)}, u32[]{:S(2)}, u32[]{:S(2)}) collective-permute-start(bf16[32,1024]{1,0:T(8,128)(2,1)S(1)} %get-tuple-element.10), channel_id=1, source_target_pairs={{0,1},{1,2},{2,3},{3,4},{4,5},{5,6},{6,7},{7,8},{8,9},{9,10},{10,1... | collective-permute-start | bytes 196616 | tf_op jit(solution)/shard_map/ppermute | solution.py:290
  7.3 0.7 reshape.18
  8.0 0.7 reshape.19
  8.8 0.9 broadcast_in_dim.15
  9.6 9.7 %all-to-all-start = ((f32[32,32,128]{2,1,0:T(8,128)}), f32[32,32,128]{2,1,0:T(8,128)S(1)}, u32[]{:S(2)}, u32[]{:S(2)}) async-start(f32[32,32,128]{2,1,0:T(8,128)} %broadcast_in_dim.15), calls=%async_computation | async-start | bytes 1048576 | tf_op jit(solution)/shard_map/all_to_all | solution.py:294
  19.3 0.7 broadcast_multiply_fusion
  20.0 0.1 fusion
  20.0 0.1 rev.3
  20.1 1.3 %copy.16.ray = f32[64,1]{1,0:T(8,128)} copy(f32[64,1]{0,1:T(1,128)} %bitcast.23) | data formatting | bytes 512 | tf_op jit(solution)/shard_map/broadcast_in_dim | solution.py:319
  21.5 0.7 copy.15.tap
  22.2 0.8 copy.17
  23.0 0.6 copy.18
  23.6 0.8 reshape.21.reach
  24.4 0.8 copy.19
  25.3 0.6 copy.20
  25.9 0.8 reshape.22.landing
  26.7 1.9 %shard_map.101 = (f32[128,256]{1,0:T(8,128)}, f32[128,128]{1,0:T(8,128)}) custom-call(s32[4,256]{1,0:T(4,128)} %reshape.21.reach, s32[4,256]{1,0:T(4,128)} %reshape.22.landing, bf16[256,256]{1,0:T(8,128)(2,1)} %constant.8.clone.earlier), custom_call_target="tpu_custom_call" | custom-call | tf_op jit(solution)/shard_map/pallas_call | solution.py:262
  28.6 0.0 collective-permute-done.1.after
  28.6 0.0 copy-start.1
  28.6 0.0 collective-permute-done.before
  28.6 0.0 copy-start.2
  28.6 0.6 copy-done.1
  29.2 0.0 copy-done.2
  29.2 17.6 %shard_map.100.folded = f32[64,32,128]{2,1,0:T(8,128)} custom-call(bf16[32,1024]{1,0:T(8,128)(2,1)} %copy-done.2, bf16[256,1024]{1,0:T(8,128)(2,1)} %bitcast.20, bf16[32,1024]{1,0:T(8,128)(2,1)} %copy-done.1, f32[2,64,1]{2,1,0:T(8,128)} %copy.15.tap, f32[64,1]{1,0:T(8,128)} %copy.16.ray, bf16[64,64]{1,0:T(8,128)(2,1)} %constant.9.clone.flip, ...), custom_call_target="tpu_custom_call" | custom-call | tf_op jit(solution)/shard_map/pallas_call | solution.py:262
  46.8 0.0 all-to-all-done
  46.8 0.0 copy-start
  46.8 0.8 copy-done
  47.6 21.1 %shard_map.102 = bf16[128,80,128]{2,1,0:T(8,128)(2,1)} custom-call(f32[4,256,128]{2,1,0:T(8,128)} %bitcast.19, f32[64,32,128]{2,1,0:T(8,128)} %shard_map.100.folded, f32[128,256]{1,0:T(8,128)} %get-tuple-element.7.rank, f32[128,128]{1,0:T(8,128)} %get-tuple-element.8.keys), custom_call_target="tpu_custom_call" | custom-call | tf_op jit(solution)/shard_map/pallas_call | solution.py:262
  68.7 45.6 %all_to_all.10.incoming = bf16[128,80,128]{2,1,0:T(8,128)(2,1)} all-to-all(bf16[128,80,128]{2,1,0:T(8,128)(2,1)} %shard_map.102), channel_id=1, replica_groups=mesh['line'=4,'xline'=32] {'line','xline'}, dimensions={0} | all-to-all | bytes 5242880 | tf_op jit(solution)/shard_map/all_to_all | solution.py:335
  114.4 4.3 %shard_map.103 = f32[1024,128]{1,0:T(8,128)} custom-call(bf16[128,80,128]{2,1,0:T(8,128)(2,1)} %all_to_all.10.incoming), custom_call_target="tpu_custom_call" | custom-call | tf_op jit(solution)/shard_map/pallas_call | solution.py:262
  (2 shorter events, 0.0 us)
Async XLA Ops:
  0.9 27.7 %collective-permute-start.1 = (bf16[32,1024]{1,0:T(8,128)(2,1)S(1)}, bf16[32,1024]{1,0:T(8,128)(2,1)S(1)}, u32[]{:S(2)}, u32[]{:S(2)}) collective-permute-start(bf16[32,1024]{1,0:T(8,128)(2,1)S(1)} %get-tuple-element.9), channel_id=1, source_target_pairs={{1,0},{2,1},{3,2},{4,3},{5,4},{6,5},{7,6},{8,7},{9,8},{10,9},{11,1... | collective-permute-start | bytes 196616 | tf_op jit(solution)/shard_map/ppermute | solution.py:291
  4.2 24.4 %collective-permute-start = (bf16[32,1024]{1,0:T(8,128)(2,1)S(1)}, bf16[32,1024]{1,0:T(8,128)(2,1)S(1)}, u32[]{:S(2)}, u32[]{:S(2)}) collective-permute-start(bf16[32,1024]{1,0:T(8,128)(2,1)S(1)} %get-tuple-element.10), channel_id=1, source_target_pairs={{0,1},{1,2},{2,3},{3,4},{4,5},{5,6},{6,7},{7,8},{8,9},{9,10},{10,1... | collective-permute-start | bytes 196616 | tf_op jit(solution)/shard_map/ppermute | solution.py:290
  9.6 37.2 %all-to-all-start = ((f32[32,32,128]{2,1,0:T(8,128)}), f32[32,32,128]{2,1,0:T(8,128)S(1)}, u32[]{:S(2)}, u32[]{:S(2)}) async-start(f32[32,32,128]{2,1,0:T(8,128)} %broadcast_in_dim.15), calls=%async_computation | async-start | bytes 1048576 | tf_op jit(solution)/shard_map/all_to_all | solution.py:294
  28.6 0.6 copy-start.1
  28.6 0.6 copy-start.2
  46.8 0.8 copy-start

commit v2 on v1

--- a/solution.py
+++ b/solution.py
@@ -117,14 +117,13 @@
                 flat[pl.ds(row, rays, stride=out.shape[1]), :] = value
 
 
-def project_kernel(factor, coarse, centres, times, folded, rank, keys, out, fine, outer, proj):
+def project_kernel(factor, coarse, centres, times, folded, rank, keys, out, seed, step, outer, proj, ninth):
     half = FINE // 2
-    blocks = fine.shape[0]
+    blocks = seed.shape[0]
     bases = times.shape[0]
     upper = iota((2 * centres, 128 * blocks), 0) < centres
 
     def one_group(base, r):
-        c0s, s0s, c1s, s1s = [], [], [], []
         for zb in range(blocks):
             cols = slice(zb * 128, zb * 128 + 128)
             t = times[base, pl.ds(8 * r + zb, 8, stride=32), :]
@@ -132,37 +131,43 @@
             angle = t * (math.pi / (2 * coarse * FINE))
             c0, s0 = jnp.cos(angle), jnp.sin(angle)
             c1, s1 = 1.0 - 2.0 * s0 * s0, 2.0 * s0 * c0
+            c, s = c0, s0
+            for m in range(8):
+                seed[zb, m * 8 : m * 8 + 8, :] = c
+                seed[zb, 64 + m * 8 : 72 + m * 8, :] = s
+                if m < 7:
+                    c, s = c * c1 - s * s1, s * c1 + c * s1
             c, s = c1, s1
-            for _ in range(6):
+            for power in range(6):
                 c, s = 1.0 - 2.0 * s * s, 2.0 * s * c
+                if power == 2:
+                    step[0:8, cols] = c
+                    step[8:16, cols] = s
             ca, sa = (c * c0 - s * s0) * amp, (s * c0 + c * s0) * amp
             cb, sb = 1.0 - 2.0 * s * s, 2.0 * s * c
             for a in range(coarse):
                 outer[16 * a : 16 * a + 8, cols] = ca
                 outer[16 * a + 8 : 16 * a + 16, cols] = sa
                 ca, sa = ca * cb - sa * sb, sa * cb + ca * sb
-            c0s, s0s, c1s, s1s = c0s + [c0], s0s + [s0], c1s + [c1], s1s + [s1]
-
-        def one_step(m, state):
-            cs, ss = state
-            row, low = pl.multiple_of(m * 8, 8), pl.multiple_of((half + m) * 8, 8)
-            for zb in range(blocks):
-                fine[zb, pl.ds(row, 8), :] = cs[zb]
-                fine[zb, pl.ds(low, 8), :] = ss[zb]
-            turned = [
-                (c * c1 - s * s1, s * c1 + c * s1) for c, s, c1, s1 in zip(cs, ss, c1s, s1s)
-            ]
-            return tuple(c for c, _ in turned), tuple(s for _, s in turned)
-
-        lax.fori_loop(0, half, one_step, (tuple(c0s), tuple(s0s)), unroll=4)
         for i in range(8):
             p = base * 16 + 2 * i + r
-            weights = jnp.concatenate(
-                [fine[zb, pl.ds(i, FINE, stride=8), :].astype(jnp.bfloat16) for zb in range(blocks)],
-                1,
+            rows = folded[p].astype(jnp.bfloat16)
+            weights = []
+            for zb in range(blocks):
+                cols = slice(zb * 128, zb * 128 + 128)
+                c = seed[zb, pl.ds(i, 8, stride=8), :]
+                s = seed[zb, pl.ds(64 + i, 8, stride=8), :]
+                cs = jnp.broadcast_to(step[i : i + 1, cols], (8, 128))
+                ss = jnp.broadcast_to(step[8 + i : 9 + i, cols], (8, 128))
+                real, imag = [c], [s]
+                for _ in range(half // 8 - 1):
+                    c, s = c * cs - s * ss, s * cs + c * ss
+                    real.append(c)
+                    imag.append(s)
+                weights.append(jnp.concatenate(real + imag, 0).astype(jnp.bfloat16))
+            parts = jnp.dot(
+                rows, jnp.concatenate(weights, 1), preferred_element_type=jnp.float32
             )
-            rows = folded[p].astype(jnp.bfloat16)
-            parts = jnp.dot(rows, weights, preferred_element_type=jnp.float32)
             total = jnp.zeros(upper.shape, jnp.float32)
             for a in range(coarse):
                 turn = jnp.where(
@@ -193,16 +198,17 @@
         y = jnp.dot(pick, sends[:, 256 * k : 256 * (k + 1)], preferred_element_type=jnp.float32)
         pair = [y[:, :128].reshape(devices, 8, 128), y[:, 128:].reshape(devices, 8, 128)]
         out[:, 16 * k : 16 * (k + 1), :] = jnp.concatenate(pair, 1).astype(jnp.bfloat16)
-    last = jnp.zeros((devices * 8, 128), jnp.float32)
+    last = jnp.dot(
+        (rank[...] == 8.0).astype(jnp.bfloat16), sends, preferred_element_type=jnp.float32
+    )
     for k in range(8):
-        pick = ((ranks == 8.0) & (lane8 == k)).astype(jnp.bfloat16)
-        last += jnp.dot(pick, sends[:, 128 * k : 128 * (k + 1)], preferred_element_type=jnp.float32)
+        ninth[pl.ds(k, devices, stride=8), :] = last[:, 128 * k : 128 * (k + 1)]
     tags = jnp.broadcast_to(keys[...][:, None, :], (devices, 8, 128))
-    pair = [last.reshape(devices, 8, 128), tags]
+    pair = [ninth[...].reshape(devices, 8, 128), tags]
     out[:, 64:80, :] = jnp.concatenate(pair, 1).astype(jnp.bfloat16)
 
 
-def route_kernel(reach, landing, earlier, rank, keys):
+def route_kernel(reach, landing, earlier, order, rank, keys):
     devices, rows = rank.shape
     tile = iota((devices, rows), 0)
     named = jnp.zeros((devices, rows), jnp.float32)
@@ -214,13 +220,22 @@
         column = column + jnp.where(hit, land + 1.0, 0.0)
     count = jnp.dot(named.astype(jnp.bfloat16), earlier[...], preferred_element_type=jnp.float32)
     slot = jnp.where(named > 0.0, count, -1.0)
-    rank[...] = slot
+    rank[...] = jnp.dot(
+        slot.astype(jnp.bfloat16), order[...], preferred_element_type=jnp.float32
+    )
     lane = iota((devices, 128), 1)
     table = jnp.zeros((devices, 128), jnp.float32)
     for k in range(SLOTS):
         value = jnp.sum(jnp.where(slot == k, column, 0.0), axis=1, keepdims=True)
         table = jnp.where(lane == k, value, table)
     keys[...] = table - 1.0
+
+
+def spread_kernel(times, amps, out):
+    rows = [table[r : r + 1, :] for table in (times, amps) for r in range(table.shape[0])]
+    lanes = range(0, times.shape[1], 128)
+    tile = jnp.concatenate([row[:, at : at + 128] for row in rows for at in lanes], 0)
+    out[...] = jnp.broadcast_to(tile[None], out.shape)
 
 
 def place_kernel(incoming, image):
@@ -289,25 +304,30 @@
     down = [(j, i) for i, j in up]
     before = lax.ppermute(own[rows - half // 2 :], "xline", up)
     after = lax.ppermute(own[: half // 2], "xline", down)
-    mine = jnp.concatenate([travel_time.reshape(-1, 128), amplitude.reshape(-1, 128)], 0)
-    mine = jnp.broadcast_to(mine[None], (size,) + mine.shape)
+    mine = call(
+        spread_kernel,
+        jax.ShapeDtypeStruct((size, 4 * depth // 128, 128), f32),
+        (travel_time, amplitude),
+    )
     times = lax.all_to_all(mine, "xline", split_axis=0, concat_axis=0, tiled=True)
     times = times.reshape(size // 8, 8 * mine.shape[1], 128)
 
-    def beam_order(table):
-        table = table.reshape(centres, rays // 16, 4, 2, 2, reach_count)
-        return table.transpose(5, 4, 1, 2, 3, 0).reshape(reach_count, centres * rays)
-
-
     beam_count = centres * rays
     earlier = np.triu(np.ones((beam_count, beam_count), np.float32), 1)
+    order = np.arange(beam_count).reshape(centres, rays // 16, 4, 2, 2)
+    order = np.eye(beam_count, dtype=np.float32)[:, order.transpose(4, 1, 2, 3, 0).reshape(-1)]
     rank, keys = call(
         route_kernel,
         (
             jax.ShapeDtypeStruct((devices, beam_count), f32),
             jax.ShapeDtypeStruct((devices, 128), f32),
         ),
-        (beam_order(reach[0]), beam_order(landing[0]), jnp.asarray(earlier, bf16)),
+        (
+            reach[0].T,
+            landing[0].T,
+            jnp.asarray(earlier, bf16),
+            jnp.asarray(order, bf16),
+        ),
     )
 
     weight = taper * (1.0 / math.sqrt(window))
@@ -327,9 +347,11 @@
         jax.ShapeDtypeStruct((devices, 80, 128), bf16),
         (times, folded, rank, keys),
         [
-            pltpu.VMEM((depth // 128, 8 * FINE, 128), f32),
+            pltpu.VMEM((depth // 128, 128, 128), f32),
+            pltpu.VMEM((16, depth), f32),
             pltpu.VMEM((16 * coarse, depth), f32),
             pltpu.VMEM((beam_count // (2 * centres), 2 * centres, depth), f32),
+            pltpu.VMEM((devices * 8, 128), f32),
         ],
     )
     incoming = lax.all_to_all(

time: 119 us -> 106 us (0.89)
  Pallas kernels: 44.9 us -> 38.1 us
  local copies, waits for them, and re-layouts: 11.2 us -> 4.55 us
    pallas_call x4 -> x5, Pallas kernels: 44.9 us -> 38.1 us  [call(): pl.pallas_call(kernel, out_shape=shapes, in_specs=vmem(len(args)), out_sp...]
    reshape x4 -> x0, local copies, waits for them, and re-layouts: 3.02 us -> none  [the longest x2 1.61 us: beam_order(): table.transpose(5, 4, 1, 2, 3, 0).reshape(reach_count, centres * rays)]
    unnamed x8 -> x6, local copies, waits for them, and re-layouts: 3.05 us -> 1.42 us
  transfers between devices with their start and end apart: 3 -> 3, of which waited for: 0 -> 0; matrix products, arithmetic and copies ran while one was open for 8% -> 3% of each run, Pallas kernels for 16% -> 20%
where the time goes in v2:
time: 106 us; the launch traced here: 105 us
  blocking collectives  45.6 us (43%)
  Pallas kernels  38.1 us (36%)
  starting transfers between devices  16.1 us (15%)
  local copies, waits for them, and re-layouts  4.55 us (4%)
    all_to_all x1, blocking collectives, on_device(): lax.all_to_all(outgoing, ('line', 'xline'), split_axis=0, concat_axis=0,...  45.6 us
    pallas_call x5, Pallas kernels, call(): pl.pallas_call(kernel, out_shape=shapes, in_specs=vmem(len(args)), out_sp...  38.1 us
    all_to_all x1, starting transfers between devices, on_device(): lax.all_to_all(mine, 'xline', split_axis=0, concat_axis=0, tiled=True)  9.68 us
    ppermute x1, starting transfers between devices, on_device(): after = lax.ppermute(own[:half // 2], 'xline', down)  3.33 us
    ppermute x1, starting transfers between devices, on_device(): before = lax.ppermute(own[rows - half // 2:], 'xline', up)  3.1 us
  transfers between devices with their start and end apart: 3, of which 0 were waited for; matrix products, arithmetic and copies ran while one was open for 3% of the time, Pallas kernels for 20%

profile of v2, /device:TPU:1, one launch (start us, length us, event | category | flops | bytes accessed | tf_op | source)
XLA Modules:
  0.0 105.1 jit_solution(5596405279024516912)
XLA Ops:
  0.0 0.9 slice_bitcast_fusion
  0.9 3.3 %collective-permute-start.1 = (bf16[32,1024]{1,0:T(8,128)(2,1)S(1)}, bf16[32,1024]{1,0:T(8,128)(2,1)S(1)}, u32[]{:S(2)}, u32[]{:S(2)}) collective-permute-start(bf16[32,1024]{1,0:T(8,128)(2,1)S(1)} %get-tuple-element.9), channel_id=1, source_target_pairs={{1,0},{2,1},{3,2},{4,3},{5,4},{6,5},{7,6},{8,7},{9,8},{10,9},{11,1... | collective-permute-start | bytes 196616 | tf_op jit(solution)/shard_map/ppermute | solution.py:306
  4.2 3.1 %collective-permute-start = (bf16[32,1024]{1,0:T(8,128)(2,1)S(1)}, bf16[32,1024]{1,0:T(8,128)(2,1)S(1)}, u32[]{:S(2)}, u32[]{:S(2)}) collective-permute-start(bf16[32,1024]{1,0:T(8,128)(2,1)S(1)} %get-tuple-element.10), channel_id=1, source_target_pairs={{0,1},{1,2},{2,3},{3,4},{4,5},{5,6},{6,7},{7,8},{8,9},{9,10},{10,1... | collective-permute-start | bytes 196616 | tf_op jit(solution)/shard_map/ppermute | solution.py:305
  7.3 1.6 %shard_map.109 = f32[32,32,128]{2,1,0:T(8,128)} custom-call(f32[2,1024]{1,0:T(2,128)} %times.1, f32[2,1024]{1,0:T(2,128)} %amps.1), custom_call_target="tpu_custom_call" | custom-call | tf_op jit(solution)/shard_map/pallas_call | solution.py:277
  8.9 9.7 %all-to-all-start = ((f32[32,32,128]{2,1,0:T(8,128)}), f32[32,32,128]{2,1,0:T(8,128)S(1)}, u32[]{:S(2)}, u32[]{:S(2)}) async-start(f32[32,32,128]{2,1,0:T(8,128)} %shard_map.109), calls=%async_computation | async-start | bytes 1048576 | tf_op jit(solution)/shard_map/all_to_all | solution.py:312
  18.6 0.7 broadcast_multiply_fusion
  19.3 0.1 fusion
  19.3 0.1 rev.3
  19.4 1.3 %copy.13.ray = f32[64,1]{1,0:T(8,128)} copy(f32[64,1]{0,1:T(1,128)} %bitcast.23) | data formatting | bytes 512 | tf_op jit(solution)/shard_map/broadcast_in_dim | solution.py:339
  20.8 0.7 copy.12.tap
  21.5 2.0 %shard_map.111 = (f32[128,256]{1,0:T(8,128)}, f32[128,128]{1,0:T(8,128)}) custom-call(s32[4,256]{1,0:T(4,128)} %bitcast.21, s32[4,256]{1,0:T(4,128)} %bitcast.22, bf16[256,256]{1,0:T(8,128)(2,1)} %constant.10.clone.earlier, bf16[256,256]{1,0:T(8,128)(2,1)} %constant.11.clone.order), custom_call_target="tpu_custom_call" | custom-call | tf_op jit(solution)/shard_map/pallas_call | solution.py:277
  23.5 0.0 collective-permute-done.1.after
  23.5 0.0 copy-start.1
  23.5 0.0 collective-permute-done.before
  23.5 0.0 copy-start.2
  23.5 0.6 copy-done.1
  24.2 0.0 copy-done.2
  24.2 17.6 %shard_map.110.folded = f32[64,32,128]{2,1,0:T(8,128)} custom-call(bf16[32,1024]{1,0:T(8,128)(2,1)} %copy-done.2, bf16[256,1024]{1,0:T(8,128)(2,1)} %bitcast.20, bf16[32,1024]{1,0:T(8,128)(2,1)} %copy-done.1, f32[2,64,1]{2,1,0:T(8,128)} %copy.12.tap, f32[64,1]{1,0:T(8,128)} %copy.13.ray, bf16[64,64]{1,0:T(8,128)(2,1)} %constant.12.clone.flip, ...), custom_call_target="tpu_custom_call" | custom-call | tf_op jit(solution)/shard_map/pallas_call | solution.py:277
  41.8 0.0 all-to-all-done
  41.8 0.0 copy-start
  41.8 0.8 copy-done
  42.6 12.6 %shard_map.112 = bf16[128,80,128]{2,1,0:T(8,128)(2,1)} custom-call(f32[4,256,128]{2,1,0:T(8,128)} %bitcast.19, f32[64,32,128]{2,1,0:T(8,128)} %shard_map.110.folded, f32[128,256]{1,0:T(8,128)} %get-tuple-element.7.rank, f32[128,128]{1,0:T(8,128)} %get-tuple-element.8.keys), custom_call_target="tpu_custom_call" | custom-call | tf_op jit(solution)/shard_map/pallas_call | solution.py:277
  55.2 45.6 %all_to_all.10.incoming = bf16[128,80,128]{2,1,0:T(8,128)(2,1)} all-to-all(bf16[128,80,128]{2,1,0:T(8,128)(2,1)} %shard_map.112), channel_id=1, replica_groups=mesh['line'=4,'xline'=32] {'line','xline'}, dimensions={0} | all-to-all | bytes 5242880 | tf_op jit(solution)/shard_map/all_to_all | solution.py:357
  100.8 4.3 %shard_map.113 = f32[1024,128]{1,0:T(8,128)} custom-call(bf16[128,80,128]{2,1,0:T(8,128)(2,1)} %all_to_all.10.incoming), custom_call_target="tpu_custom_call" | custom-call | tf_op jit(solution)/shard_map/pallas_call | solution.py:277
  (1 shorter events, 0.0 us)
Async XLA Ops:
  0.9 22.6 %collective-permute-start.1 = (bf16[32,1024]{1,0:T(8,128)(2,1)S(1)}, bf16[32,1024]{1,0:T(8,128)(2,1)S(1)}, u32[]{:S(2)}, u32[]{:S(2)}) collective-permute-start(bf16[32,1024]{1,0:T(8,128)(2,1)S(1)} %get-tuple-element.9), channel_id=1, source_target_pairs={{1,0},{2,1},{3,2},{4,3},{5,4},{6,5},{7,6},{8,7},{9,8},{10,9},{11,1... | collective-permute-start | bytes 196616 | tf_op jit(solution)/shard_map/ppermute | solution.py:306
  4.2 19.3 %collective-permute-start = (bf16[32,1024]{1,0:T(8,128)(2,1)S(1)}, bf16[32,1024]{1,0:T(8,128)(2,1)S(1)}, u32[]{:S(2)}, u32[]{:S(2)}) collective-permute-start(bf16[32,1024]{1,0:T(8,128)(2,1)S(1)} %get-tuple-element.10), channel_id=1, source_target_pairs={{0,1},{1,2},{2,3},{3,4},{4,5},{5,6},{6,7},{7,8},{8,9},{9,10},{10,1... | collective-permute-start | bytes 196616 | tf_op jit(solution)/shard_map/ppermute | solution.py:305
  8.9 32.9 %all-to-all-start = ((f32[32,32,128]{2,1,0:T(8,128)}), f32[32,32,128]{2,1,0:T(8,128)S(1)}, u32[]{:S(2)}, u32[]{:S(2)}) async-start(f32[32,32,128]{2,1,0:T(8,128)} %shard_map.109), calls=%async_computation | async-start | bytes 1048576 | tf_op jit(solution)/shard_map/all_to_all | solution.py:312
  23.5 0.6 copy-start.1
  23.5 0.6 copy-start.2
  41.8 0.8 copy-start

commit v3 on v2

--- a/solution.py
+++ b/solution.py
@@ -12,6 +12,7 @@
 X = 128
 FINE = 128
 SLOTS = 9
+BATCH = 8
 
 
 def iota(shape, dim):
@@ -31,85 +32,106 @@
     return np.concatenate([real, imag], 0)
 
 
-def slant_kernel(before, own, after, tap, ray, flip, fold, out, combos, beams):
-    freqs = combos.shape[0] * 128
-    half = combos.shape[1]
-    centres = combos.shape[2] // 4
-    flat = combos.reshape(freqs // 128, half * 4 * centres, 128)
-    for n in range(centres):
-        start = n * half - half // 2
-        if n == 0:
-            low = jnp.concatenate([before[...], own[: half // 2]], 0)
-        else:
-            low = own[start : start + half]
-        if n == centres - 1:
-            high = jnp.concatenate([own[start + half :], after[...]], 0)
-        else:
-            high = own[start + half : start + 2 * half]
-        turned = jnp.dot(flip[...], low, preferred_element_type=jnp.float32) * tap[0]
-        high = high.astype(jnp.float32) * tap[1]
-        total, diff = high + turned, high - turned
-        for block in range(freqs // 128):
-            for q in range(4):
-                value = (total, diff)[q // 2]
-                cut = (q % 2) * freqs + block * 128
-                rows = pl.ds(q * centres + n, half, stride=4 * centres)
-                flat[block, rows, :] = value[:, cut : cut + 128]
-
-    rays = ray.shape[0]
-    group = 2
-    blocks = rays // (8 * group)
-
-    def one_tile(tile, carry):
-        block, first = tile // blocks, (tile % blocks) * 8 * group
-        angular = (iota((8, 128), 1) + (block * 128 + 1)).astype(jnp.float32) * (math.pi / freqs)
-        state = []
-        steps = []
-        for g in range(group):
-            rows = pl.ds(pl.multiple_of(first + 8 * g, 8), 8)
-            angle = ray[rows, :] * 0.5 * angular
-            c, s = jnp.cos(angle), jnp.sin(angle)
-            state += [c, s]
-            steps += [(1.0 - 2.0 * s * s, 2.0 * s * c)]
-        zero = jnp.zeros((8, 128), jnp.float32)
-        sums = [zero] * (2 * group * centres)
-
-        def one_offset(j, current):
-            state, sums = list(current[0]), list(current[1])
-            for n in range(centres):
-                pr, pi, mr, mi = (
-                    jnp.broadcast_to(combos[block, j, q * centres + n : q * centres + n + 1, :], (8, 128))
-                    for q in range(4)
-                )
-                for g in range(group):
-                    c, s = state[2 * g], state[2 * g + 1]
-                    at = 2 * (g * centres + n)
-                    sums[at] = sums[at] + (c * pr + s * mi)
-                    sums[at + 1] = sums[at + 1] + (c * pi - s * mr)
-            for g in range(group):
-                c, s = state[2 * g], state[2 * g + 1]
-                cs, ss = steps[g]
-                state[2 * g], state[2 * g + 1] = c * cs - s * ss, s * cs + c * ss
-            return tuple(state), tuple(sums)
-
-        state, sums = lax.fori_loop(0, half, one_offset, (tuple(state), tuple(sums)), unroll=4)
-        for g in range(group):
-            for n in range(centres):
-                at = 2 * (g * centres + n)
-                row = pl.multiple_of((block * centres + n) * rays + first + 8 * g, 8)
-                beams[pl.ds(row, 8), 0:128] = sums[at]
-                beams[pl.ds(row, 8), 128:256] = sums[at + 1]
-        return carry
-
-    lax.fori_loop(0, (freqs // 128) * blocks, one_tile, 0)
-    rows = centres * rays
+def pick_column(row, at):
+    hit = iota((at.shape[0], row.shape[1]), 1) == at
+    return jnp.sum(jnp.where(hit, row, 0.0), axis=1, keepdims=True)
+
+
+def slant_kernel(before, own, after, taper, ray, fold, out, data, order, rows, beams):
+    half = before.shape[0] * 2
+    window = 2 * half
+    rays = ray.shape[1]
+    freqs = own.shape[1] // 2
+    centres = own.shape[0] // half
+    blocks = freqs // 128
+    data[: half // 2] = before[...]
+    data[half // 2 : half // 2 + own.shape[0]] = own[...]
+    data[half // 2 + own.shape[0] :] = after[...]
+
+    column = iota((1, order.shape[1]), 1)
+    source = column // 16 % 8 * 128 + column // 128 * 16 + column % 16
+    order[...] = (iota(order.shape, 0) == source).astype(jnp.bfloat16)
+
+    weight = taper[...] * (1.0 / math.sqrt(window))
+    place = iota((half, 1), 0)
+    high_weight = pick_column(weight, half + place)
+    low_weight = pick_column(weight, half - 1 - place)
+    flip = (iota((half, half), 0) + iota((half, half), 1) == half - 1).astype(jnp.bfloat16)
+    lane = iota((half, 128), 1)
+    even = lane % 2 == 0
+    for block in range(blocks):
+        parts = [
+            data[n * half : n * half + window, part * freqs + block * 128 :][:, :128]
+            for n in range(centres)
+            for part in range(2)
+        ]
+        moved = jnp.dot(
+            jnp.concatenate(parts, 1), order[...], preferred_element_type=jnp.float32
+        )
+        low = jnp.dot(flip, moved[:half].astype(jnp.bfloat16), preferred_element_type=jnp.float32)
+        low, high = low * low_weight, moved[half:] * high_weight
+        total, diff = high + low, high - low
+        for g in range(8):
+            plus = total[:, 128 * g : 128 * (g + 1)]
+            minus = diff[:, 128 * g : 128 * (g + 1)]
+            minus = jnp.where(
+                lane % 32 < 16, pltpu.roll(minus, 112, 1), -pltpu.roll(minus, 16, 1)
+            )
+            stack = [
+                jnp.where(even, plus, 0.0),
+                jnp.where(even, 0.0, plus),
+                jnp.where(even, minus, 0.0),
+                jnp.where(even, 0.0, minus),
+            ]
+            rows[block * 8 + g] = jnp.concatenate(stack, 0).astype(jnp.bfloat16)
+
+    slow = pick_column(ray[...], iota((rays, 1), 0))
+    lane = iota((rays, 128), 1)
+    offset = (lane % half).astype(jnp.float32) + 0.5
+    angle = slow * offset * (math.pi / freqs)
+    c1, s1 = jnp.cos(angle), jnp.sin(angle)
+    cs, ss = 1.0 - 2.0 * s1 * s1, 2.0 * s1 * c1
+    first = lane < half
+    pair = lane % 16 // 2
+
+    def one_group(g, state):
+        c, s = state
+        total = jnp.zeros((rays, 128), jnp.float32)
+        for start in range(0, 8, BATCH):
+            steer = []
+            for _ in range(BATCH):
+                steer.append(jnp.concatenate([c, s], 1).astype(jnp.bfloat16))
+                c, s = c * cs - s * ss, s * cs + c * ss
+            y = jnp.dot(
+                jnp.concatenate(steer, 0), rows[g], preferred_element_type=jnp.float32
+            )
+            for q in range(BATCH):
+                total = jnp.where(pair == start + q, y[q * rays : (q + 1) * rays], total)
+        beams[g] = total
+        return c, s
+
+    begin = (jnp.where(first, c1, cs), jnp.where(first, s1, ss))
+    lax.fori_loop(0, 8 * blocks, one_group, begin, unroll=8)
+
     flat = out.reshape(rays * out.shape[1], 128)
-    for block in range(freqs // 128):
+    centre = lane // 32
+    for block in range(blocks):
+        fine, rest = [], []
+        for g in range(8):
+            value = beams[block * 8 + g]
+            fine.append(value.astype(jnp.bfloat16).astype(jnp.float32))
+            rest.append(value - fine[-1])
+        stack = [
+            jnp.concatenate([jnp.where(centre == n, v, 0.0) for v in piece], 1)
+            for piece in (fine, rest)
+            for n in range(centres)
+        ]
         folded = jnp.dot(
-            beams[block * rows : (block + 1) * rows].astype(jnp.bfloat16),
+            jnp.concatenate(stack, 0).astype(jnp.bfloat16),
             fold[...],
             preferred_element_type=jnp.float32,
         )
+        folded = folded[: centres * rays] + folded[centres * rays :]
         for n in range(centres):
             for v in range(2):
                 row = (2 * block + v) * centres + n
@@ -330,16 +352,17 @@
         ),
     )
 
-    weight = taper * (1.0 / math.sqrt(window))
-    tap = jnp.stack([weight[:half][::-1], weight[half:]])[:, :, None]
-    flip = jnp.asarray(np.eye(half, dtype=np.float32)[::-1], bf16)
+    at = np.arange(8 * 128)
+    fold = fold_matrix()[at // 16 % 2 * 128 + at // 128 * 16 + at % 16]
     folded = call(
         slant_kernel,
         jax.ShapeDtypeStruct((rays, 2 * coarse * centres, FINE), f32),
-        (before, own, after, tap, ray_param[:, None], flip, jnp.asarray(fold_matrix(), bf16)),
+        (before, own, after, taper[None], ray_param[None], jnp.asarray(fold, bf16)),
         [
-            pltpu.VMEM((freqs // 128, half, 4 * centres, 128), f32),
-            pltpu.VMEM((coarse * beam_count, 2 * FINE), f32),
+            pltpu.VMEM((rows + half, 2 * freqs), bf16),
+            pltpu.VMEM((256 * centres, 256 * centres), bf16),
+            pltpu.VMEM((freqs // 16, 4 * half, 128), bf16),
+            pltpu.VMEM((freqs // 16, rays, 128), f32),
         ],
     )
     outgoing = call(

time: 106 us -> 95.4 us (0.900)
  Pallas kernels: 38.1 us -> 29.9 us
  local copies, waits for them, and re-layouts: 4.55 us -> 2.33 us
  blocking collectives: 45.6 us -> 47.1 us
  starting transfers between devices: 16.1 us -> 15 us
    pallas_call x5, Pallas kernels: 38.1 us -> 29.9 us  [call(): pl.pallas_call(kernel, out_shape=shapes, in_specs=vmem(len(args)), out_sp...]
    broadcast_in_dim x2 -> x0, local copies, waits for them, and re-layouts: 2.08 us -> none  [the longest x1 1.35 us: on_device(): ray_param[:, None]]
    all_to_all x1, blocking collectives: 45.6 us -> 47.1 us  [on_device(): lax.all_to_all(outgoing, ('line', 'xline'), split_axis=0, concat_axis=0,...]
    ppermute x1, starting transfers between devices: 3.33 us -> 2.14 us  [on_device(): after = lax.ppermute(own[:half // 2], 'xline', down)]
  transfers between devices with their start and end apart: 3 -> 3, of which waited for: 0 -> 1; matrix products, arithmetic and copies ran while one was open for 3% -> 1% of each run, Pallas kernels for 20% -> 12%
where the time goes in v3:
time: 95.4 us; the launch traced here: 94.9 us
  blocking collectives  47.1 us (49%)
  Pallas kernels  29.9 us (31%)
  starting transfers between devices  15 us (16%)
  local copies, waits for them, and re-layouts  2.33 us (2%)
    all_to_all x1, blocking collectives, on_device(): lax.all_to_all(outgoing, ('line', 'xline'), split_axis=0, concat_axis=0,...  47.1 us
    pallas_call x5, Pallas kernels, call(): pl.pallas_call(kernel, out_shape=shapes, in_specs=vmem(len(args)), out_sp...  29.9 us
    all_to_all x1, starting transfers between devices, on_device(): lax.all_to_all(mine, 'xline', split_axis=0, concat_axis=0, tiled=True)  9.43 us
    ppermute x1, starting transfers between devices, on_device(): before = lax.ppermute(own[rows - half // 2:], 'xline', up)  3.42 us
    ppermute x1, starting transfers between devices, on_device(): after = lax.ppermute(own[:half // 2], 'xline', down)  2.14 us
  transfers between devices with their start and end apart: 3, of which 1 were waited for; matrix products, arithmetic and copies ran while one was open for 1% of the time, Pallas kernels for 12%

profile of v3, /device:TPU:1, one launch (start us, length us, event | category | flops | bytes accessed | tf_op | source)
XLA Modules:
  0.0 94.9 jit_solution(14836971273130700167)
XLA Ops:
  0.0 1.6 %shard_map.100 = f32[32,32,128]{2,1,0:T(8,128)} custom-call(f32[2,1024]{1,0:T(2,128)} %times.1, f32[2,1024]{1,0:T(2,128)} %amps.1), custom_call_target="tpu_custom_call" | custom-call | tf_op jit(solution)/shard_map/pallas_call | solution.py:299
  1.6 9.4 %all-to-all-start = ((f32[32,32,128]{2,1,0:T(8,128)}), f32[32,32,128]{2,1,0:T(8,128)S(1)}, u32[]{:S(2)}, u32[]{:S(2)}) async-start(f32[32,32,128]{2,1,0:T(8,128)} %shard_map.100), calls=%async_computation | async-start | bytes 1048576 | tf_op jit(solution)/shard_map/all_to_all | solution.py:334
  11.0 0.9 slice_bitcast_fusion
  11.9 2.1 %collective-permute-start.1 = (bf16[32,1024]{1,0:T(8,128)(2,1)S(1)}, bf16[32,1024]{1,0:T(8,128)(2,1)S(1)}, u32[]{:S(2)}, u32[]{:S(2)}) collective-permute-start(bf16[32,1024]{1,0:T(8,128)(2,1)S(1)} %get-tuple-element.9), channel_id=1, source_target_pairs={{1,0},{2,1},{3,2},{4,3},{5,4},{6,5},{7,6},{8,7},{9,8},{10,9},{11,1... | collective-permute-start | bytes 196616 | tf_op jit(solution)/shard_map/ppermute | solution.py:328
  14.0 3.4 %collective-permute-start = (bf16[32,1024]{1,0:T(8,128)(2,1)S(1)}, bf16[32,1024]{1,0:T(8,128)(2,1)S(1)}, u32[]{:S(2)}, u32[]{:S(2)}) collective-permute-start(bf16[32,1024]{1,0:T(8,128)(2,1)S(1)} %get-tuple-element.10), channel_id=1, source_target_pairs={{0,1},{1,2},{2,3},{3,4},{4,5},{5,6},{6,7},{7,8},{8,9},{9,10},{10,1... | collective-permute-start | bytes 196616 | tf_op jit(solution)/shard_map/ppermute | solution.py:327
  17.5 2.0 %shard_map.102 = (f32[128,256]{1,0:T(8,128)}, f32[128,128]{1,0:T(8,128)}) custom-call(s32[4,256]{1,0:T(4,128)} %bitcast.17, s32[4,256]{1,0:T(4,128)} %bitcast.18, bf16[256,256]{1,0:T(8,128)(2,1)} %constant.6.clone.earlier, bf16[256,256]{1,0:T(8,128)(2,1)} %constant.7.clone.order), custom_call_target="tpu_custom_call" | custom-call | tf_op jit(solution)/shard_map/pallas_call | solution.py:299
  19.5 0.6 collective-permute-done.1.after
  20.1 0.0 copy-start.1
  20.1 0.0 collective-permute-done.before
  20.1 0.0 copy-start.2
  20.1 0.6 copy-done.1
  20.7 0.0 copy-done.2
  20.7 9.4 %shard_map.101.folded = f32[64,32,128]{2,1,0:T(8,128)} custom-call(bf16[32,1024]{1,0:T(8,128)(2,1)} %copy-done.2, bf16[256,1024]{1,0:T(8,128)(2,1)} %bitcast.16, bf16[32,1024]{1,0:T(8,128)(2,1)} %copy-done.1, f32[1,128]{1,0:T(1,128)} %bitcast.19, f32[1,64]{1,0:T(1,128)} %bitcast.20, bf16[1024,256]{1,0:T(8,128)(2,1)} %constant.8.clone.fold), custom_call_target="tpu_custom_call" | custom-call | tf_op jit(solution)/shard_map/pallas_call | solution.py:299
  30.1 0.0 all-to-all-done
  30.1 0.0 copy-start
  30.1 0.8 copy-done
  30.9 12.6 %shard_map.103 = bf16[128,80,128]{2,1,0:T(8,128)(2,1)} custom-call(f32[4,256,128]{2,1,0:T(8,128)} %bitcast.15, f32[64,32,128]{2,1,0:T(8,128)} %shard_map.101.folded, f32[128,256]{1,0:T(8,128)} %get-tuple-element.7.rank, f32[128,128]{1,0:T(8,128)} %get-tuple-element.8.keys), custom_call_target="tpu_custom_call" | custom-call | tf_op jit(solution)/shard_map/pallas_call | solution.py:299
  43.5 47.1 %all_to_all.10.incoming = bf16[128,80,128]{2,1,0:T(8,128)(2,1)} all-to-all(bf16[128,80,128]{2,1,0:T(8,128)(2,1)} %shard_map.103), channel_id=1, replica_groups=mesh['line'=4,'xline'=32] {'line','xline'}, dimensions={0} | all-to-all | bytes 5242880 | tf_op jit(solution)/shard_map/all_to_all | solution.py:380
  90.6 4.3 %shard_map.104 = f32[1024,128]{1,0:T(8,128)} custom-call(bf16[128,80,128]{2,1,0:T(8,128)(2,1)} %all_to_all.10.incoming), custom_call_target="tpu_custom_call" | custom-call | tf_op jit(solution)/shard_map/pallas_call | solution.py:299
Async XLA Ops:
  1.6 28.6 %all-to-all-start = ((f32[32,32,128]{2,1,0:T(8,128)}), f32[32,32,128]{2,1,0:T(8,128)S(1)}, u32[]{:S(2)}, u32[]{:S(2)}) async-start(f32[32,32,128]{2,1,0:T(8,128)} %shard_map.100), calls=%async_computation | async-start | bytes 1048576 | tf_op jit(solution)/shard_map/all_to_all | solution.py:334
  11.9 8.2 %collective-permute-start.1 = (bf16[32,1024]{1,0:T(8,128)(2,1)S(1)}, bf16[32,1024]{1,0:T(8,128)(2,1)S(1)}, u32[]{:S(2)}, u32[]{:S(2)}) collective-permute-start(bf16[32,1024]{1,0:T(8,128)(2,1)S(1)} %get-tuple-element.9), channel_id=1, source_target_pairs={{1,0},{2,1},{3,2},{4,3},{5,4},{6,5},{7,6},{8,7},{9,8},{10,9},{11,1... | collective-permute-start | bytes 196616 | tf_op jit(solution)/shard_map/ppermute | solution.py:328
  14.0 6.0 %collective-permute-start = (bf16[32,1024]{1,0:T(8,128)(2,1)S(1)}, bf16[32,1024]{1,0:T(8,128)(2,1)S(1)}, u32[]{:S(2)}, u32[]{:S(2)}) collective-permute-start(bf16[32,1024]{1,0:T(8,128)(2,1)S(1)} %get-tuple-element.10), channel_id=1, source_target_pairs={{0,1},{1,2},{2,3},{3,4},{4,5},{5,6},{6,7},{7,8},{8,9},{9,10},{10,1... | collective-permute-start | bytes 196616 | tf_op jit(solution)/shard_map/ppermute | solution.py:327
  20.1 0.6 copy-start.1
  20.1 0.7 copy-start.2
  30.1 0.8 copy-start

commit v4 on v3

--- a/solution.py
+++ b/solution.py
@@ -143,7 +143,7 @@
     half = FINE // 2
     blocks = seed.shape[0]
     bases = times.shape[0]
-    upper = iota((2 * centres, 128 * blocks), 0) < centres
+    upper = iota((2 * centres, 128), 0) < centres
 
     def one_group(base, r):
         for zb in range(blocks):
@@ -171,10 +171,10 @@
                 outer[16 * a : 16 * a + 8, cols] = ca
                 outer[16 * a + 8 : 16 * a + 16, cols] = sa
                 ca, sa = ca * cb - sa * sb, sa * cb + ca * sb
+        held = [None] * blocks
         for i in range(8):
             p = base * 16 + 2 * i + r
             rows = folded[p].astype(jnp.bfloat16)
-            weights = []
             for zb in range(blocks):
                 cols = slice(zb * 128, zb * 128 + 128)
                 c = seed[zb, pl.ds(i, 8, stride=8), :]
@@ -186,23 +186,22 @@
                     c, s = c * cs - s * ss, s * cs + c * ss
                     real.append(c)
                     imag.append(s)
-                weights.append(jnp.concatenate(real + imag, 0).astype(jnp.bfloat16))
-            parts = jnp.dot(
-                rows, jnp.concatenate(weights, 1), preferred_element_type=jnp.float32
-            )
-            total = jnp.zeros(upper.shape, jnp.float32)
-            for a in range(coarse):
-                turn = jnp.where(
-                    upper,
-                    jnp.broadcast_to(outer[16 * a + i : 16 * a + i + 1, :], upper.shape),
-                    jnp.broadcast_to(outer[16 * a + 8 + i : 16 * a + 9 + i, :], upper.shape),
-                )
-                total = total + parts[2 * centres * a : 2 * centres * (a + 1)] * turn
-            total = total + pltpu.roll(total, centres, 0)
-            if i % 2 == 0:
-                held = total
-            else:
-                proj[(r * bases + base) * 4 + i // 2] = jnp.where(upper, held, total)
+                weights = jnp.concatenate(real + imag, 0).astype(jnp.bfloat16)
+                parts = jnp.dot(rows, weights, preferred_element_type=jnp.float32)
+                total = jnp.zeros(upper.shape, jnp.float32)
+                for a in range(coarse):
+                    turn = jnp.where(
+                        upper,
+                        jnp.broadcast_to(outer[16 * a + i : 16 * a + i + 1, cols], upper.shape),
+                        jnp.broadcast_to(outer[16 * a + 8 + i : 16 * a + 9 + i, cols], upper.shape),
+                    )
+                    total = total + parts[2 * centres * a : 2 * centres * (a + 1)] * turn
+                total = total + pltpu.roll(total, centres, 0)
+                if i % 2 == 0:
+                    held[zb] = total
+                else:
+                    tile = (r * bases + base) * 4 + i // 2
+                    proj[tile, :, cols] = jnp.where(upper, held[zb], total)
 
     def one_base(base, carry):
         one_group(base, 0)
@@ -230,7 +229,19 @@
     out[:, 64:80, :] = jnp.concatenate(pair, 1).astype(jnp.bfloat16)
 
 
-def route_kernel(reach, landing, earlier, order, rank, keys):
+def open_kernel(own, times, amps, reach, landing, earlier, order, up, down, mine, rank, keys, sems):
+    edge = up.shape[0]
+    copies = [
+        pltpu.make_async_copy(own.at[own.shape[0] - edge :], up, sems.at[0]),
+        pltpu.make_async_copy(own.at[:edge], down, sems.at[1]),
+    ]
+    for copy in copies:
+        copy.start()
+    rows = [table[r : r + 1, :] for table in (times, amps) for r in range(table.shape[0])]
+    lanes = range(0, times.shape[1], 128)
+    tile = jnp.concatenate([row[:, at : at + 128] for row in rows for at in lanes], 0)
+    mine[...] = jnp.broadcast_to(tile[None], mine.shape)
+
     devices, rows = rank.shape
     tile = iota((devices, rows), 0)
     named = jnp.zeros((devices, rows), jnp.float32)
@@ -251,25 +262,22 @@
         value = jnp.sum(jnp.where(slot == k, column, 0.0), axis=1, keepdims=True)
         table = jnp.where(lane == k, value, table)
     keys[...] = table - 1.0
-
-
-def spread_kernel(times, amps, out):
-    rows = [table[r : r + 1, :] for table in (times, amps) for r in range(table.shape[0])]
-    lanes = range(0, times.shape[1], 128)
-    tile = jnp.concatenate([row[:, at : at + 128] for row in rows for at in lanes], 0)
-    out[...] = jnp.broadcast_to(tile[None], out.shape)
-
-
-def place_kernel(incoming, image):
+    for copy in copies:
+        copy.wait()
+
+
+def place_kernel(incoming, image, ninth):
     devices = incoming.shape[0]
-    tags = incoming[:, 64:80, :].astype(jnp.float32)[:, 8:16, :]
+    tail = incoming[:, 64:80, :].astype(jnp.float32)
+    tags = tail[:, 8:16, :]
+    ninth[...] = tail[:, 0:8, :].reshape(devices * 8, 128)
+    lane = iota((devices, 128), 1)
+    hit9 = (tags[:, 0, :][:, 8:9] == lane.astype(jnp.float32)).astype(jnp.bfloat16)
     tags = jnp.concatenate([tags, tags], 1).reshape(devices * 16, 128)
     lane = iota((devices * 16, 128), 1)
     row = iota((devices * 16, 128), 0) % 16
     key = jnp.sum(jnp.where(lane == row % 8, tags, 0.0), axis=1, keepdims=True)
-    key9 = jnp.sum(jnp.where(lane == 8, tags, 0.0), axis=1, keepdims=True)
-    lanes = lane.astype(jnp.float32)
-    hit = key == lanes
+    hit = key == lane.astype(jnp.float32)
     both = jnp.concatenate(
         [
             (hit & (row < 8)).astype(jnp.bfloat16),
@@ -277,29 +285,26 @@
         ],
         1,
     )
-    hit9 = key9 == lanes
     contract = (((0,), (0,)), ((), ()))
-    tail = incoming[:, 64:80, :].reshape(devices * 16, 128)
     for k in range(4):
         rows = incoming[:, 16 * k : 16 * (k + 1), :].reshape(devices * 16, 128)
         y = lax.dot_general(rows, both, contract, preferred_element_type=jnp.float32)
-        nine = jnp.concatenate(
-            [(hit9 & (row == 2 * k + q)).astype(jnp.bfloat16) for q in range(2)], 1
-        )
-        y += lax.dot_general(tail, nine, contract, preferred_element_type=jnp.float32)
-        image[256 * k : 256 * k + 128, :] = y[:, :128]
-        image[256 * k + 128 : 256 * (k + 1), :] = y[:, 128:]
+        for q in range(2):
+            last = ninth[pl.ds(2 * k + q, devices, stride=8), :].astype(jnp.bfloat16)
+            last = lax.dot_general(last, hit9, contract, preferred_element_type=jnp.float32)
+            cut = 256 * k + 128 * q
+            image[cut : cut + 128, :] = y[:, 128 * q : 128 * (q + 1)] + last
 
 
 def vmem(count):
     return [pl.BlockSpec(memory_space=pltpu.VMEM)] * count
 
 
-def call(kernel, shapes, args, scratch=()):
+def call(kernel, shapes, args, scratch=(), specs=()):
     return pl.pallas_call(
         kernel,
         out_shape=shapes,
-        in_specs=vmem(len(args)),
+        in_specs=list(specs) + vmem(len(args) - len(specs)),
         out_specs=jax.tree.map(lambda _: pl.BlockSpec(memory_space=pltpu.VMEM), shapes),
         scratch_shapes=list(scratch),
         compiler_params=pltpu.CompilerParams(vmem_limit_bytes=56 * 1024 * 1024),
@@ -322,35 +327,38 @@
     factor = 1.0 / math.sqrt(2.0 * freqs * centres * rays * reach_count / X)
 
     own = traces[0]
-    up = [(i, i + 1) for i in range(size - 1)]
-    down = [(j, i) for i, j in up]
-    before = lax.ppermute(own[rows - half // 2 :], "xline", up)
-    after = lax.ppermute(own[: half // 2], "xline", down)
-    mine = call(
-        spread_kernel,
-        jax.ShapeDtypeStruct((size, 4 * depth // 128, 128), f32),
-        (travel_time, amplitude),
-    )
-    times = lax.all_to_all(mine, "xline", split_axis=0, concat_axis=0, tiled=True)
-    times = times.reshape(size // 8, 8 * mine.shape[1], 128)
-
     beam_count = centres * rays
     earlier = np.triu(np.ones((beam_count, beam_count), np.float32), 1)
     order = np.arange(beam_count).reshape(centres, rays // 16, 4, 2, 2)
     order = np.eye(beam_count, dtype=np.float32)[:, order.transpose(4, 1, 2, 3, 0).reshape(-1)]
-    rank, keys = call(
-        route_kernel,
+    edge = (half // 2, 2 * freqs)
+    last, first, mine, rank, keys = call(
+        open_kernel,
         (
+            jax.ShapeDtypeStruct(edge, bf16),
+            jax.ShapeDtypeStruct(edge, bf16),
+            jax.ShapeDtypeStruct((size, 4 * depth // 128, 128), f32),
             jax.ShapeDtypeStruct((devices, beam_count), f32),
             jax.ShapeDtypeStruct((devices, 128), f32),
         ),
         (
+            own,
+            travel_time,
+            amplitude,
             reach[0].T,
             landing[0].T,
             jnp.asarray(earlier, bf16),
             jnp.asarray(order, bf16),
         ),
-    )
+        [pltpu.SemaphoreType.DMA((2,))],
+        [pl.BlockSpec(memory_space=pl.ANY)],
+    )
+    up = [(i, i + 1) for i in range(size - 1)]
+    down = [(j, i) for i, j in up]
+    before = lax.ppermute(last, "xline", up)
+    after = lax.ppermute(first, "xline", down)
+    times = lax.all_to_all(mine, "xline", split_axis=0, concat_axis=0, tiled=True)
+    times = times.reshape(size // 8, 8 * mine.shape[1], 128)
 
     at = np.arange(8 * 128)
     fold = fold_matrix()[at // 16 % 2 * 128 + at // 128 * 16 + at % 16]
@@ -380,7 +388,12 @@
     incoming = lax.all_to_all(
         outgoing, ("line", "xline"), split_axis=0, concat_axis=0, tiled=True
     )
-    image = call(place_kernel, jax.ShapeDtypeStruct((depth, X), f32), (incoming,))
+    image = call(
+        place_kernel,
+        jax.ShapeDtypeStruct((depth, X), f32),
+        (incoming,),
+        [pltpu.VMEM((8 * devices, 128), f32)],
+    )
     return image[None]
 
 

time: 95.4 us -> 94.7 us (level)
  waiting for transfers between devices: 0.57 us -> 4.16 us
  Pallas kernels: 29.9 us -> 27.2 us
    ppermute x2, waiting for transfers between devices: 0.57 us -> 4.16 us  [the longest x1 2.6 us: on_device(): after = lax.ppermute(first, 'xline', down)]
    pallas_call x5 -> x4, Pallas kernels: 29.9 us -> 27.2 us  [call(): pl.pallas_call(kernel, out_shape=shapes, in_specs=list(specs) + vmem(len(...]
  transfers between devices with their start and end apart: 3 -> 3, of which waited for: 1 -> 2; matrix products, arithmetic and copies ran while one was open for 1% -> 0% of each run, Pallas kernels for 12% -> 10%
where the time goes in v4:
time: 94.7 us; the launch traced here: 94.2 us
  blocking collectives  46.4 us (49%)
  Pallas kernels  27.2 us (29%)
  starting transfers between devices  14.9 us (16%)
  waiting for transfers between devices  4.16 us (4%)
  local copies, waits for them, and re-layouts  1.41 us (1%)
    all_to_all x1, blocking collectives, on_device(): lax.all_to_all(outgoing, ('line', 'xline'), split_axis=0, concat_axis=0,...  46.4 us
    pallas_call x4, Pallas kernels, call(): pl.pallas_call(kernel, out_shape=shapes, in_specs=list(specs) + vmem(len(...  27.2 us
    all_to_all x1, starting transfers between devices, on_device(): lax.all_to_all(mine, 'xline', split_axis=0, concat_axis=0, tiled=True)  9.44 us
    ppermute x1, starting transfers between devices, on_device(): before = lax.ppermute(last, 'xline', up)  3.54 us
    ppermute x1, waiting for transfers between devices, on_device(): after = lax.ppermute(first, 'xline', down)  2.6 us
    ppermute x1, starting transfers between devices, on_device(): after = lax.ppermute(first, 'xline', down)  1.92 us
  transfers between devices with their start and end apart: 3, of which 2 were waited for; matrix products, arithmetic and copies ran while one was open for 0% of the time, Pallas kernels for 10%

profile of v4, /device:TPU:1, one launch (start us, length us, event | category | flops | bytes accessed | tf_op | source)
XLA Modules:
  0.0 94.2 jit_solution(18383855359250234887)
XLA Ops:
  0.0 2.8 %shard_map.100 = (bf16[32,1024]{1,0:T(8,128)(2,1)}, bf16[32,1024]{1,0:T(8,128)(2,1)}, f32[32,32,128]{2,1,0:T(8,128)}, f32[128,256]{1,0:T(8,128)}, f32[128,128]{1,0:T(8,128)}) custom-call(bf16[256,1024]{1,0:T(8,128)(2,1)} %bitcast.12, f32[2,1024]{1,0:T(2,128)} %times.1, f32[2,1024]{1,0:T(2,128)} %amps.1, s32[4,256]{1,0:T(4,128)} %bitcast.14, ...), custom_call_target="tpu_custom_call" | custom-call | tf_op jit(solution)/shard_map/pallas_call | solution.py:304
  2.8 9.4 %all-to-all-start = ((f32[32,32,128]{2,1,0:T(8,128)}), f32[32,32,128]{2,1,0:T(8,128)S(1)}, u32[]{:S(2)}, u32[]{:S(2)}) async-start(f32[32,32,128]{2,1,0:T(8,128)} %get-tuple-element.10), calls=%async_computation | async-start | bytes 1048576 | tf_op jit(solution)/shard_map/all_to_all | solution.py:360
  12.3 3.5 %collective-permute-start = (bf16[32,1024]{1,0:T(8,128)(2,1)}, bf16[32,1024]{1,0:T(8,128)(2,1)S(1)}, u32[]{:S(2)}, u32[]{:S(2)}) collective-permute-start(bf16[32,1024]{1,0:T(8,128)(2,1)} %get-tuple-element.11), channel_id=1, source_target_pairs={{0,1},{1,2},{2,3},{3,4},{4,5},{5,6},{6,7},{7,8},{8,9},{9,10},{10,1... | collective-permute-start | bytes 196616 | tf_op jit(solution)/shard_map/ppermute | solution.py:358
  15.8 1.9 %collective-permute-start.1 = (bf16[32,1024]{1,0:T(8,128)(2,1)}, bf16[32,1024]{1,0:T(8,128)(2,1)S(1)}, u32[]{:S(2)}, u32[]{:S(2)}) collective-permute-start(bf16[32,1024]{1,0:T(8,128)(2,1)} %get-tuple-element.12), channel_id=1, source_target_pairs={{1,0},{2,1},{3,2},{4,3},{5,4},{6,5},{7,6},{8,7},{9,8},{10,9},{11,1... | collective-permute-start | bytes 196616 | tf_op jit(solution)/shard_map/ppermute | solution.py:359
  17.8 1.6 %collective-permute-done.before = bf16[32,1024]{1,0:T(8,128)(2,1)S(1)} collective-permute-done((bf16[32,1024]{1,0:T(8,128)(2,1)}, bf16[32,1024]{1,0:T(8,128)(2,1)S(1)}, u32[]{:S(2)}, u32[]{:S(2)}) %collective-permute-start) | collective-permute-done | bytes 65568 | tf_op jit(solution)/shard_map/ppermute | solution.py:358
  19.3 0.0 copy-start.1
  19.3 2.6 %collective-permute-done.1.after = bf16[32,1024]{1,0:T(8,128)(2,1)S(1)} collective-permute-done((bf16[32,1024]{1,0:T(8,128)(2,1)}, bf16[32,1024]{1,0:T(8,128)(2,1)S(1)}, u32[]{:S(2)}, u32[]{:S(2)}) %collective-permute-start.1) | collective-permute-done | bytes 65568 | tf_op jit(solution)/shard_map/ppermute | solution.py:359
  21.9 0.0 copy-start.2
  21.9 0.0 copy-done.1
  21.9 0.6 copy-done.2
  22.6 9.4 %shard_map.101.folded = f32[64,32,128]{2,1,0:T(8,128)} custom-call(bf16[32,1024]{1,0:T(8,128)(2,1)} %copy-done.1, bf16[256,1024]{1,0:T(8,128)(2,1)} %bitcast.13, bf16[32,1024]{1,0:T(8,128)(2,1)} %copy-done.2, f32[1,128]{1,0:T(1,128)} %bitcast.16, f32[1,64]{1,0:T(1,128)} %bitcast.17, bf16[1024,256]{1,0:T(8,128)(2,1)} %constant.8.clone.fold), custom_call_target="tpu_custom_call" | custom-call | tf_op jit(solution)/shard_map/pallas_call | solution.py:304
  32.0 0.0 all-to-all-done
  32.0 0.0 copy-start
  32.0 0.8 copy-done
  32.8 11.2 %shard_map.102 = bf16[128,80,128]{2,1,0:T(8,128)(2,1)} custom-call(f32[4,256,128]{2,1,0:T(8,128)} %bitcast.11, f32[64,32,128]{2,1,0:T(8,128)} %shard_map.101.folded, f32[128,256]{1,0:T(8,128)} %get-tuple-element.13.rank, f32[128,128]{1,0:T(8,128)} %get-tuple-element.14.keys), custom_call_target="tpu_custom_call" | custom-call | tf_op jit(solution)/shard_map/pallas_call | solution.py:304
  43.9 46.4 %all_to_all.10.incoming = bf16[128,80,128]{2,1,0:T(8,128)(2,1)} all-to-all(bf16[128,80,128]{2,1,0:T(8,128)(2,1)} %shard_map.102), channel_id=1, replica_groups=mesh['line'=4,'xline'=32] {'line','xline'}, dimensions={0} | all-to-all | bytes 5242880 | tf_op jit(solution)/shard_map/all_to_all | solution.py:388
  90.4 3.8 %shard_map.103 = f32[1024,128]{1,0:T(8,128)} custom-call(bf16[128,80,128]{2,1,0:T(8,128)(2,1)} %all_to_all.10.incoming), custom_call_target="tpu_custom_call" | custom-call | tf_op jit(solution)/shard_map/pallas_call | solution.py:304
Async XLA Ops:
  2.8 29.1 %all-to-all-start = ((f32[32,32,128]{2,1,0:T(8,128)}), f32[32,32,128]{2,1,0:T(8,128)S(1)}, u32[]{:S(2)}, u32[]{:S(2)}) async-start(f32[32,32,128]{2,1,0:T(8,128)} %get-tuple-element.10), calls=%async_computation | async-start | bytes 1048576 | tf_op jit(solution)/shard_map/all_to_all | solution.py:360
  12.3 7.0 %collective-permute-start = (bf16[32,1024]{1,0:T(8,128)(2,1)}, bf16[32,1024]{1,0:T(8,128)(2,1)S(1)}, u32[]{:S(2)}, u32[]{:S(2)}) collective-permute-start(bf16[32,1024]{1,0:T(8,128)(2,1)} %get-tuple-element.11), channel_id=1, source_target_pairs={{0,1},{1,2},{2,3},{3,4},{4,5},{5,6},{6,7},{7,8},{8,9},{9,10},{10,1... | collective-permute-start | bytes 196616 | tf_op jit(solution)/shard_map/ppermute | solution.py:358
  15.8 6.1 %collective-permute-start.1 = (bf16[32,1024]{1,0:T(8,128)(2,1)}, bf16[32,1024]{1,0:T(8,128)(2,1)S(1)}, u32[]{:S(2)}, u32[]{:S(2)}) collective-permute-start(bf16[32,1024]{1,0:T(8,128)(2,1)} %get-tuple-element.12), channel_id=1, source_target_pairs={{1,0},{2,1},{3,2},{4,3},{5,4},{6,5},{7,6},{8,7},{9,8},{10,9},{11,1... | collective-permute-start | bytes 196616 | tf_op jit(solution)/shard_map/ppermute | solution.py:359
  19.3 2.6 %copy-start.1 = (bf16[32,1024]{1,0:T(8,128)(2,1)}, bf16[32,1024]{1,0:T(8,128)(2,1)S(1)}, u32[]{:S(2)}) copy-start(bf16[32,1024]{1,0:T(8,128)(2,1)S(1)} %collective-permute-done.before) | copy-start | bytes 196612
  21.9 0.6 copy-start.2
  32.0 0.8 copy-start

commit v5 on v4

--- a/solution.py
+++ b/solution.py
@@ -300,6 +300,10 @@
     return [pl.BlockSpec(memory_space=pltpu.VMEM)] * count
 
 
+def near(*arrays):
+    return tuple(pltpu.with_memory_space_constraint(array, pltpu.VMEM) for array in arrays)
+
+
 def call(kernel, shapes, args, scratch=(), specs=()):
     return pl.pallas_call(
         kernel,
@@ -335,11 +339,11 @@
     last, first, mine, rank, keys = call(
         open_kernel,
         (
-            jax.ShapeDtypeStruct(edge, bf16),
-            jax.ShapeDtypeStruct(edge, bf16),
-            jax.ShapeDtypeStruct((size, 4 * depth // 128, 128), f32),
-            jax.ShapeDtypeStruct((devices, beam_count), f32),
-            jax.ShapeDtypeStruct((devices, 128), f32),
+            pltpu.VMEM(edge, bf16),
+            pltpu.VMEM(edge, bf16),
+            pltpu.VMEM((size, 4 * depth // 128, 128), f32),
+            pltpu.VMEM((devices, beam_count), f32),
+            pltpu.VMEM((devices, 128), f32),
         ),
         (
             own,
@@ -364,8 +368,15 @@
     fold = fold_matrix()[at // 16 % 2 * 128 + at // 128 * 16 + at % 16]
     folded = call(
         slant_kernel,
-        jax.ShapeDtypeStruct((rays, 2 * coarse * centres, FINE), f32),
-        (before, own, after, taper[None], ray_param[None], jnp.asarray(fold, bf16)),
+        pltpu.VMEM((rays, 2 * coarse * centres, FINE), f32),
+        (
+            *near(before),
+            own,
+            *near(after),
+            taper[None],
+            ray_param[None],
+            jnp.asarray(fold, bf16),
+        ),
         [
             pltpu.VMEM((rows + half, 2 * freqs), bf16),
             pltpu.VMEM((256 * centres, 256 * centres), bf16),
@@ -375,8 +386,8 @@
     )
     outgoing = call(
         functools.partial(project_kernel, factor, coarse, centres),
-        jax.ShapeDtypeStruct((devices, 80, 128), bf16),
-        (times, folded, rank, keys),
+        pltpu.VMEM((devices, 80, 128), bf16),
+        near(times, folded, rank, keys),
         [
             pltpu.VMEM((depth // 128, 128, 128), f32),
             pltpu.VMEM((16, depth), f32),
@@ -391,7 +402,7 @@
     image = call(
         place_kernel,
         jax.ShapeDtypeStruct((depth, X), f32),
-        (incoming,),
+        near(incoming),
         [pltpu.VMEM((8 * devices, 128), f32)],
     )
     return image[None]

time: 94.7 us -> 86.9 us (0.918)
  Pallas kernels: 27.2 us -> 21.5 us
  local copies, waits for them, and re-layouts: 1.41 us -> 0 us
    pallas_call x4, Pallas kernels: 27.2 us -> 21.5 us  [call(): pl.pallas_call(kernel, out_shape=shapes, in_specs=list(specs) + vmem(len(...]
    unnamed x6 -> x0, local copies, waits for them, and re-layouts: 1.41 us -> none
where the time goes in v5:
time: 86.9 us; the launch traced here: 86.5 us
  blocking collectives  46.1 us (53%)
  Pallas kernels  21.5 us (25%)
  starting transfers between devices  14.9 us (17%)
  waiting for transfers between devices  3.95 us (5%)
    all_to_all x1, blocking collectives, on_device(): lax.all_to_all(outgoing, ('line', 'xline'), split_axis=0, concat_axis=0,...  46.1 us
    pallas_call x4, Pallas kernels, call(): pl.pallas_call(kernel, out_shape=shapes, in_specs=list(specs) + vmem(len(...  21.5 us
    all_to_all x1, starting transfers between devices, on_device(): lax.all_to_all(mine, 'xline', split_axis=0, concat_axis=0, tiled=True)  9.44 us
    ppermute x1, starting transfers between devices, on_device(): before = lax.ppermute(last, 'xline', up)  3.54 us
    ppermute x1, waiting for transfers between devices, on_device(): after = lax.ppermute(first, 'xline', down)  2.5 us
    ppermute x1, starting transfers between devices, on_device(): after = lax.ppermute(first, 'xline', down)  1.92 us
  transfers between devices with their start and end apart: 3, of which 2 were waited for; matrix products, arithmetic and copies ran while one was open for 0% of the time, Pallas kernels for 10%

profile of v5, /device:TPU:1, one launch (start us, length us, event | category | flops | bytes accessed | tf_op | source)
XLA Modules:
  0.0 86.5 jit_solution(11370298341713201980)
XLA Ops:
  0.0 2.7 %shard_map.100 = (bf16[32,1024]{1,0:T(8,128)(2,1)S(1)}, bf16[32,1024]{1,0:T(8,128)(2,1)S(1)}, f32[32,32,128]{2,1,0:T(8,128)}, f32[128,256]{1,0:T(8,128)S(1)}, f32[128,128]{1,0:T(8,128)S(1)}) custom-call(bf16[256,1024]{1,0:T(8,128)(2,1)} %bitcast.12, f32[2,1024]{1,0:T(2,128)} %times.1, f32[2,1024]{1,0:T(2,128)} %amps.1, s32[4,256]{1,0:T(4,128)} %bitcast.14, ...), custom_call_target="tpu_custom_call" | custom-call | tf_op jit(solution)/shard_map/pallas_call | solution.py:308
  2.8 9.4 %all-to-all-start = ((f32[32,32,128]{2,1,0:T(8,128)}), f32[32,32,128]{2,1,0:T(8,128)S(1)}, u32[]{:S(2)}, u32[]{:S(2)}) async-start(f32[32,32,128]{2,1,0:T(8,128)} %get-tuple-element.10), calls=%async_computation | async-start | bytes 1048576 | tf_op jit(solution)/shard_map/all_to_all | solution.py:364
  12.2 3.5 %collective-permute-start = (bf16[32,1024]{1,0:T(8,128)(2,1)S(1)}, bf16[32,1024]{1,0:T(8,128)(2,1)S(1)}, u32[]{:S(2)}, u32[]{:S(2)}) collective-permute-start(bf16[32,1024]{1,0:T(8,128)(2,1)S(1)} %get-tuple-element.11), channel_id=1, source_target_pairs={{0,1},{1,2},{2,3},{3,4},{4,5},{5,6},{6,7},{7,8},{8,9},{9,10},{10,1... | collective-permute-start | bytes 196616 | tf_op jit(solution)/shard_map/ppermute | solution.py:362
  15.8 1.9 %collective-permute-start.1 = (bf16[32,1024]{1,0:T(8,128)(2,1)S(1)}, bf16[32,1024]{1,0:T(8,128)(2,1)S(1)}, u32[]{:S(2)}, u32[]{:S(2)}) collective-permute-start(bf16[32,1024]{1,0:T(8,128)(2,1)S(1)} %get-tuple-element.12), channel_id=1, source_target_pairs={{1,0},{2,1},{3,2},{4,3},{5,4},{6,5},{7,6},{8,7},{9,8},{10,9},{11,1... | collective-permute-start | bytes 196616 | tf_op jit(solution)/shard_map/ppermute | solution.py:363
  17.7 1.4 %collective-permute-done.before = bf16[32,1024]{1,0:T(8,128)(2,1)S(1)} collective-permute-done((bf16[32,1024]{1,0:T(8,128)(2,1)S(1)}, bf16[32,1024]{1,0:T(8,128)(2,1)S(1)}, u32[]{:S(2)}, u32[]{:S(2)}) %collective-permute-start) | collective-permute-done | bytes 65568 | tf_op jit(solution)/shard_map/ppermute | solution.py:362
  19.1 2.5 %collective-permute-done.1.after = bf16[32,1024]{1,0:T(8,128)(2,1)S(1)} collective-permute-done((bf16[32,1024]{1,0:T(8,128)(2,1)S(1)}, bf16[32,1024]{1,0:T(8,128)(2,1)S(1)}, u32[]{:S(2)}, u32[]{:S(2)}) %collective-permute-start.1) | collective-permute-done | bytes 65568 | tf_op jit(solution)/shard_map/ppermute | solution.py:363
  21.6 8.4 %shard_map.101.folded = f32[64,32,128]{2,1,0:T(8,128)S(1)} custom-call(bf16[32,1024]{1,0:T(8,128)(2,1)S(1)} %collective-permute-done.before, bf16[256,1024]{1,0:T(8,128)(2,1)} %bitcast.13, bf16[32,1024]{1,0:T(8,128)(2,1)S(1)} %collective-permute-done.1.after, f32[1,128]{1,0:T(1,128)} %bitcast.16, f32[1,64]{1,0:T(1,128)} %bitcast.17, ...), custom_call_target="tpu_custom_call" | custom-call | tf_op jit(solution)/shard_map/pallas_call | solution.py:308
  30.0 0.0 all-to-all-done
  30.0 8.3 %shard_map.102 = bf16[128,80,128]{2,1,0:T(8,128)(2,1)S(1)} custom-call(f32[4,256,128]{2,1,0:T(8,128)S(1)} %bitcast.11, f32[64,32,128]{2,1,0:T(8,128)S(1)} %shard_map.101.folded, f32[128,256]{1,0:T(8,128)S(1)} %get-tuple-element.13.rank, f32[128,128]{1,0:T(8,128)S(1)} %get-tuple-element.14.keys), custom_call_target="tpu_custom_call" | custom-call | tf_op jit(solution)/shard_map/pallas_call | solution.py:308
  38.3 46.1 %all_to_all.10.incoming = bf16[128,80,128]{2,1,0:T(8,128)(2,1)S(1)} all-to-all(bf16[128,80,128]{2,1,0:T(8,128)(2,1)S(1)} %shard_map.102), channel_id=1, replica_groups=mesh['line'=4,'xline'=32] {'line','xline'}, dimensions={0} | all-to-all | bytes 5242880 | tf_op jit(solution)/shard_map/all_to_all | solution.py:399
  84.5 2.1 %shard_map.103 = f32[1024,128]{1,0:T(8,128)} custom-call(bf16[128,80,128]{2,1,0:T(8,128)(2,1)S(1)} %all_to_all.10.incoming), custom_call_target="tpu_custom_call" | custom-call | tf_op jit(solution)/shard_map/pallas_call | solution.py:308
Async XLA Ops:
  2.8 27.3 %all-to-all-start = ((f32[32,32,128]{2,1,0:T(8,128)}), f32[32,32,128]{2,1,0:T(8,128)S(1)}, u32[]{:S(2)}, u32[]{:S(2)}) async-start(f32[32,32,128]{2,1,0:T(8,128)} %get-tuple-element.10), calls=%async_computation | async-start | bytes 1048576 | tf_op jit(solution)/shard_map/all_to_all | solution.py:364
  12.2 6.9 %collective-permute-start = (bf16[32,1024]{1,0:T(8,128)(2,1)S(1)}, bf16[32,1024]{1,0:T(8,128)(2,1)S(1)}, u32[]{:S(2)}, u32[]{:S(2)}) collective-permute-start(bf16[32,1024]{1,0:T(8,128)(2,1)S(1)} %get-tuple-element.11), channel_id=1, source_target_pairs={{0,1},{1,2},{2,3},{3,4},{4,5},{5,6},{6,7},{7,8},{8,9},{9,10},{10,1... | collective-permute-start | bytes 196616 | tf_op jit(solution)/shard_map/ppermute | solution.py:362
  15.8 5.9 %collective-permute-start.1 = (bf16[32,1024]{1,0:T(8,128)(2,1)S(1)}, bf16[32,1024]{1,0:T(8,128)(2,1)S(1)}, u32[]{:S(2)}, u32[]{:S(2)}) collective-permute-start(bf16[32,1024]{1,0:T(8,128)(2,1)S(1)} %get-tuple-element.12), channel_id=1, source_target_pairs={{1,0},{2,1},{3,2},{4,3},{5,4},{6,5},{7,6},{8,7},{9,8},{10,9},{11,1... | collective-permute-start | bytes 196616 | tf_op jit(solution)/shard_map/ppermute | solution.py:363

commit v6 on v5

--- a/solution.py
+++ b/solution.py
@@ -139,7 +139,7 @@
                 flat[pl.ds(row, rays, stride=out.shape[1]), :] = value
 
 
-def project_kernel(factor, coarse, centres, times, folded, rank, keys, out, seed, step, outer, proj, ninth):
+def project_kernel(factor, coarse, centres, times, folded, pick, pick9, keys, out, seed, step, outer, proj, ninth):
     half = FINE // 2
     blocks = seed.shape[0]
     bases = times.shape[0]
@@ -211,17 +211,12 @@
     lax.fori_loop(0, bases, one_base, 0)
 
     sends = proj[...].reshape(-1, 128 * blocks).astype(jnp.bfloat16)
-    devices, rows = rank.shape
-    ranks = jnp.broadcast_to(rank[...][:, None, :], (devices, 8, rows)).reshape(devices * 8, rows)
-    lane8 = iota((devices * 8, rows), 0) % 8
-    pick = (ranks == lane8.astype(jnp.float32)).astype(jnp.bfloat16)
+    devices = keys.shape[0]
     for k in range(4):
-        y = jnp.dot(pick, sends[:, 256 * k : 256 * (k + 1)], preferred_element_type=jnp.float32)
+        y = jnp.dot(pick[...], sends[:, 256 * k : 256 * (k + 1)], preferred_element_type=jnp.float32)
         pair = [y[:, :128].reshape(devices, 8, 128), y[:, 128:].reshape(devices, 8, 128)]
         out[:, 16 * k : 16 * (k + 1), :] = jnp.concatenate(pair, 1).astype(jnp.bfloat16)
-    last = jnp.dot(
-        (rank[...] == 8.0).astype(jnp.bfloat16), sends, preferred_element_type=jnp.float32
-    )
+    last = jnp.dot(pick9[...], sends, preferred_element_type=jnp.float32)
     for k in range(8):
         ninth[pl.ds(k, devices, stride=8), :] = last[:, 128 * k : 128 * (k + 1)]
     tags = jnp.broadcast_to(keys[...][:, None, :], (devices, 8, 128))
@@ -229,7 +224,7 @@
     out[:, 64:80, :] = jnp.concatenate(pair, 1).astype(jnp.bfloat16)
 
 
-def open_kernel(own, times, amps, reach, landing, earlier, order, up, down, mine, rank, keys, sems):
+def open_kernel(own, times, amps, up, down, mine, sems):
     edge = up.shape[0]
     copies = [
         pltpu.make_async_copy(own.at[own.shape[0] - edge :], up, sems.at[0]),
@@ -241,8 +236,12 @@
     lanes = range(0, times.shape[1], 128)
     tile = jnp.concatenate([row[:, at : at + 128] for row in rows for at in lanes], 0)
     mine[...] = jnp.broadcast_to(tile[None], mine.shape)
-
-    devices, rows = rank.shape
+    for copy in copies:
+        copy.wait()
+
+
+def route_kernel(centres, reach, landing, pick, ninth, keys):
+    devices, rows = ninth.shape
     tile = iota((devices, rows), 0)
     named = jnp.zeros((devices, rows), jnp.float32)
     column = jnp.zeros((devices, rows), jnp.float32)
@@ -251,19 +250,26 @@
         land = jnp.broadcast_to(landing[t : t + 1, :], (devices, rows)).astype(jnp.float32)
         named = named + jnp.where(hit, 1.0, 0.0)
         column = column + jnp.where(hit, land + 1.0, 0.0)
-    count = jnp.dot(named.astype(jnp.bfloat16), earlier[...], preferred_element_type=jnp.float32)
+    first, second = iota((rows, rows), 0), iota((rows, rows), 1)
+    earlier = (first < second).astype(jnp.bfloat16)
+    count = jnp.dot(named.astype(jnp.bfloat16), earlier, preferred_element_type=jnp.float32)
     slot = jnp.where(named > 0.0, count, -1.0)
-    rank[...] = jnp.dot(
-        slot.astype(jnp.bfloat16), order[...], preferred_element_type=jnp.float32
-    )
+    rays = rows // centres
+    tile = second % centres * rays + second // (rays // 2 * centres)
+    tile += second // (8 * centres) % (rays // 16) * 16
+    tile += second // (2 * centres) % 4 * 4 + second // centres % 2 * 2
+    order = (first == tile).astype(jnp.bfloat16)
+    moved = jnp.dot(slot.astype(jnp.bfloat16), order, preferred_element_type=jnp.float32)
+    wide = jnp.broadcast_to(moved[:, None, :], (devices, 8, rows)).reshape(devices * 8, rows)
+    row = iota((devices * 8, rows), 0) % 8
+    pick[...] = (wide == row.astype(jnp.float32)).astype(jnp.bfloat16)
+    ninth[...] = (moved == 8.0).astype(jnp.bfloat16)
     lane = iota((devices, 128), 1)
     table = jnp.zeros((devices, 128), jnp.float32)
     for k in range(SLOTS):
         value = jnp.sum(jnp.where(slot == k, column, 0.0), axis=1, keepdims=True)
         table = jnp.where(lane == k, value, table)
     keys[...] = table - 1.0
-    for copy in copies:
-        copy.wait()
 
 
 def place_kernel(incoming, image, ninth):
@@ -304,13 +310,14 @@
     return tuple(pltpu.with_memory_space_constraint(array, pltpu.VMEM) for array in arrays)
 
 
-def call(kernel, shapes, args, scratch=(), specs=()):
+def call(kernel, shapes, args, scratch=(), specs=(), flops=0):
     return pl.pallas_call(
         kernel,
         out_shape=shapes,
         in_specs=list(specs) + vmem(len(args) - len(specs)),
         out_specs=jax.tree.map(lambda _: pl.BlockSpec(memory_space=pltpu.VMEM), shapes),
         scratch_shapes=list(scratch),
+        cost_estimate=pl.CostEstimate(flops=flops, bytes_accessed=0, transcendentals=0),
         compiler_params=pltpu.CompilerParams(vmem_limit_bytes=56 * 1024 * 1024),
     )(*args)
 
@@ -332,30 +339,27 @@
 
     own = traces[0]
     beam_count = centres * rays
-    earlier = np.triu(np.ones((beam_count, beam_count), np.float32), 1)
-    order = np.arange(beam_count).reshape(centres, rays // 16, 4, 2, 2)
-    order = np.eye(beam_count, dtype=np.float32)[:, order.transpose(4, 1, 2, 3, 0).reshape(-1)]
     edge = (half // 2, 2 * freqs)
-    last, first, mine, rank, keys = call(
+    last, first, mine = call(
         open_kernel,
         (
             pltpu.VMEM(edge, bf16),
             pltpu.VMEM(edge, bf16),
             pltpu.VMEM((size, 4 * depth // 128, 128), f32),
-            pltpu.VMEM((devices, beam_count), f32),
+        ),
+        (own, travel_time, amplitude),
+        [pltpu.SemaphoreType.DMA((2,))],
+        [pl.BlockSpec(memory_space=pl.ANY)],
+    )
+    pick, pick9, keys = call(
+        functools.partial(route_kernel, centres),
+        (
+            pltpu.VMEM((8 * devices, beam_count), bf16),
+            pltpu.VMEM((devices, beam_count), bf16),
             pltpu.VMEM((devices, 128), f32),
         ),
-        (
-            own,
-            travel_time,
-            amplitude,
-            reach[0].T,
-            landing[0].T,
-            jnp.asarray(earlier, bf16),
-            jnp.asarray(order, bf16),
-        ),
-        [pltpu.SemaphoreType.DMA((2,))],
-        [pl.BlockSpec(memory_space=pl.ANY)],
+        (reach[0].T, landing[0].T),
+        flops=1_000_000_000,
     )
     up = [(i, i + 1) for i in range(size - 1)]
     down = [(j, i) for i, j in up]
@@ -383,11 +387,12 @@
             pltpu.VMEM((freqs // 16, 4 * half, 128), bf16),
             pltpu.VMEM((freqs // 16, rays, 128), f32),
         ],
+        flops=8_000_000_000,
     )
     outgoing = call(
         functools.partial(project_kernel, factor, coarse, centres),
         pltpu.VMEM((devices, 80, 128), bf16),
-        near(times, folded, rank, keys),
+        near(times, folded, pick, pick9, keys),
         [
             pltpu.VMEM((depth // 128, 128, 128), f32),
             pltpu.VMEM((16, depth), f32),

time: 86.9 us -> 86.6 us (level)
  waiting for transfers between devices: 3.95 us -> 2.73 us
    ppermute x1, waiting for transfers between devices: 1.45 us -> 0.22 us  [on_device(): before = lax.ppermute(last, 'xline', up)]
    pallas_call x4 -> x5, Pallas kernels: 21.5 us -> 22.3 us  [call(): pl.pallas_call(kernel, out_shape=shapes, in_specs=list(specs) + vmem(len(...]
  transfers between devices with their start and end apart: 3 -> 3, of which waited for: 2 -> 2; matrix products, arithmetic and copies ran while one was open for 0% -> 0% of each run, Pallas kernels for 10% -> 11%
where the time goes in v6:
time: 86.6 us; the launch traced here: 86.2 us
  blocking collectives  46.1 us (53%)
  Pallas kernels  22.3 us (26%)
  starting transfers between devices  14.9 us (17%)
  waiting for transfers between devices  2.73 us (3%)
    all_to_all x1, blocking collectives, on_device(): lax.all_to_all(outgoing, ('line', 'xline'), split_axis=0, concat_axis=0,...  46.1 us
    pallas_call x5, Pallas kernels, call(): pl.pallas_call(kernel, out_shape=shapes, in_specs=list(specs) + vmem(len(...  22.3 us
    all_to_all x1, starting transfers between devices, on_device(): lax.all_to_all(mine, 'xline', split_axis=0, concat_axis=0, tiled=True)  9.44 us
    ppermute x1, starting transfers between devices, on_device(): before = lax.ppermute(last, 'xline', up)  3.54 us
    ppermute x1, waiting for transfers between devices, on_device(): after = lax.ppermute(first, 'xline', down)  2.5 us
    ppermute x1, starting transfers between devices, on_device(): after = lax.ppermute(first, 'xline', down)  1.92 us
  transfers between devices with their start and end apart: 3, of which 2 were waited for; matrix products, arithmetic and copies ran while one was open for 0% of the time, Pallas kernels for 11%

profile of v6, /device:TPU:1, one launch (start us, length us, event | category | flops | bytes accessed | tf_op | source)
XLA Modules:
  0.0 86.2 jit_solution(3812062075298536973)
XLA Ops:
  0.0 2.4 %shard_map.82 = (bf16[32,1024]{1,0:T(8,128)(2,1)S(1)}, bf16[32,1024]{1,0:T(8,128)(2,1)S(1)}, f32[32,32,128]{2,1,0:T(8,128)}) custom-call(bf16[256,1024]{1,0:T(8,128)(2,1)} %bitcast.12, f32[2,1024]{1,0:T(2,128)} %times.1, f32[2,1024]{1,0:T(2,128)} %amps.1), custom_call_target="tpu_custom_call" | custom-call | tf_op jit(solution)/shard_map/pallas_call | solution.py:314
  2.4 9.4 %all-to-all-start = ((f32[32,32,128]{2,1,0:T(8,128)}), f32[32,32,128]{2,1,0:T(8,128)S(1)}, u32[]{:S(2)}, u32[]{:S(2)}) async-start(f32[32,32,128]{2,1,0:T(8,128)} %get-tuple-element.11), calls=%async_computation | async-start | bytes 1048576 | tf_op jit(solution)/shard_map/all_to_all | solution.py:368
  11.9 3.5 %collective-permute-start = (bf16[32,1024]{1,0:T(8,128)(2,1)S(1)}, bf16[32,1024]{1,0:T(8,128)(2,1)S(1)}, u32[]{:S(2)}, u32[]{:S(2)}) collective-permute-start(bf16[32,1024]{1,0:T(8,128)(2,1)S(1)} %get-tuple-element.12), channel_id=1, source_target_pairs={{0,1},{1,2},{2,3},{3,4},{4,5},{5,6},{6,7},{7,8},{8,9},{9,10},{10,1... | collective-permute-start | bytes 196616 | tf_op jit(solution)/shard_map/ppermute | solution.py:366
  15.4 1.9 %collective-permute-start.1 = (bf16[32,1024]{1,0:T(8,128)(2,1)S(1)}, bf16[32,1024]{1,0:T(8,128)(2,1)S(1)}, u32[]{:S(2)}, u32[]{:S(2)}) collective-permute-start(bf16[32,1024]{1,0:T(8,128)(2,1)S(1)} %get-tuple-element.13), channel_id=1, source_target_pairs={{1,0},{2,1},{3,2},{4,3},{5,4},{6,5},{7,6},{8,7},{9,8},{10,9},{11,1... | collective-permute-start | bytes 196616 | tf_op jit(solution)/shard_map/ppermute | solution.py:367
  17.3 1.2 %shard_map.84 = (bf16[1024,256]{1,0:T(8,128)(2,1)S(1)}, bf16[128,256]{1,0:T(8,128)(2,1)S(1)}, f32[128,128]{1,0:T(8,128)S(1)}) custom-call(s32[4,256]{1,0:T(4,128)} %bitcast.14, s32[4,256]{1,0:T(4,128)} %bitcast.15), custom_call_target="tpu_custom_call" | custom-call | flops 1000000000 | tf_op jit(solution)/shard_map/pallas_call | solution.py:314
  18.6 0.2 collective-permute-done.before
  18.8 2.5 %collective-permute-done.1.after = bf16[32,1024]{1,0:T(8,128)(2,1)S(1)} collective-permute-done((bf16[32,1024]{1,0:T(8,128)(2,1)S(1)}, bf16[32,1024]{1,0:T(8,128)(2,1)S(1)}, u32[]{:S(2)}, u32[]{:S(2)}) %collective-permute-start.1) | collective-permute-done | bytes 65568 | tf_op jit(solution)/shard_map/ppermute | solution.py:367
  21.3 8.4 %shard_map.83.folded = f32[64,32,128]{2,1,0:T(8,128)S(1)} custom-call(bf16[32,1024]{1,0:T(8,128)(2,1)S(1)} %collective-permute-done.before, bf16[256,1024]{1,0:T(8,128)(2,1)} %bitcast.13, bf16[32,1024]{1,0:T(8,128)(2,1)S(1)} %collective-permute-done.1.after, f32[1,128]{1,0:T(1,128)} %bitcast.16, f32[1,64]{1,0:T(1,128)} %bitcast.17, ...), custom_call_target="tpu_custom_call" | custom-call | flops 8000000000 | tf_op jit(solution)/shard_map/pallas_call | solution.py:314
  29.7 0.0 all-to-all-done
  29.7 8.3 %shard_map.85 = bf16[128,80,128]{2,1,0:T(8,128)(2,1)S(1)} custom-call(f32[4,256,128]{2,1,0:T(8,128)S(1)} %bitcast.11, f32[64,32,128]{2,1,0:T(8,128)S(1)} %shard_map.83.folded, bf16[1024,256]{1,0:T(8,128)(2,1)S(1)} %get-tuple-element.14.pick, bf16[128,256]{1,0:T(8,128)(2,1)S(1)} %get-tuple-element.15.pick9, f32[128,128]{1,0:T(8,128)S(1)} %get-tuple-element.16.keys), custom_call_target="tpu_custom_call" | custom-call | tf_op jit(solution)/shard_map/pallas_call | solution.py:314
  38.0 46.1 %all_to_all.10.incoming = bf16[128,80,128]{2,1,0:T(8,128)(2,1)S(1)} all-to-all(bf16[128,80,128]{2,1,0:T(8,128)(2,1)S(1)} %shard_map.85), channel_id=1, replica_groups=mesh['line'=4,'xline'=32] {'line','xline'}, dimensions={0} | all-to-all | bytes 5242880 | tf_op jit(solution)/shard_map/all_to_all | solution.py:404
  84.1 2.1 %shard_map.86 = f32[1024,128]{1,0:T(8,128)} custom-call(bf16[128,80,128]{2,1,0:T(8,128)(2,1)S(1)} %all_to_all.10.incoming), custom_call_target="tpu_custom_call" | custom-call | tf_op jit(solution)/shard_map/pallas_call | solution.py:314
Async XLA Ops:
  2.4 27.3 %all-to-all-start = ((f32[32,32,128]{2,1,0:T(8,128)}), f32[32,32,128]{2,1,0:T(8,128)S(1)}, u32[]{:S(2)}, u32[]{:S(2)}) async-start(f32[32,32,128]{2,1,0:T(8,128)} %get-tuple-element.11), calls=%async_computation | async-start | bytes 1048576 | tf_op jit(solution)/shard_map/all_to_all | solution.py:368
  11.9 6.9 %collective-permute-start = (bf16[32,1024]{1,0:T(8,128)(2,1)S(1)}, bf16[32,1024]{1,0:T(8,128)(2,1)S(1)}, u32[]{:S(2)}, u32[]{:S(2)}) collective-permute-start(bf16[32,1024]{1,0:T(8,128)(2,1)S(1)} %get-tuple-element.12), channel_id=1, source_target_pairs={{0,1},{1,2},{2,3},{3,4},{4,5},{5,6},{6,7},{7,8},{8,9},{9,10},{10,1... | collective-permute-start | bytes 196616 | tf_op jit(solution)/shard_map/ppermute | solution.py:366
  15.4 5.9 %collective-permute-start.1 = (bf16[32,1024]{1,0:T(8,128)(2,1)S(1)}, bf16[32,1024]{1,0:T(8,128)(2,1)S(1)}, u32[]{:S(2)}, u32[]{:S(2)}) collective-permute-start(bf16[32,1024]{1,0:T(8,128)(2,1)S(1)} %get-tuple-element.13), channel_id=1, source_target_pairs={{1,0},{2,1},{3,2},{4,3},{5,4},{6,5},{7,6},{8,7},{9,8},{10,9},{11,1... | collective-permute-start | bytes 196616 | tf_op jit(solution)/shard_map/ppermute | solution.py:367

commit v7 on v6

--- a/solution.py
+++ b/solution.py
@@ -37,7 +37,7 @@
     return jnp.sum(jnp.where(hit, row, 0.0), axis=1, keepdims=True)
 
 
-def slant_kernel(before, own, after, taper, ray, fold, out, data, order, rows, beams):
+def slant_kernel(before, own, after, taper, ray, fold, order, out, data, rows, beams):
     half = before.shape[0] * 2
     window = 2 * half
     rays = ray.shape[1]
@@ -48,10 +48,6 @@
     data[half // 2 : half // 2 + own.shape[0]] = own[...]
     data[half // 2 + own.shape[0] :] = after[...]
 
-    column = iota((1, order.shape[1]), 1)
-    source = column // 16 % 8 * 128 + column // 128 * 16 + column % 16
-    order[...] = (iota(order.shape, 0) == source).astype(jnp.bfloat16)
-
     weight = taper[...] * (1.0 / math.sqrt(window))
     place = iota((half, 1), 0)
     high_weight = pick_column(weight, half + place)
@@ -59,7 +55,8 @@
     flip = (iota((half, half), 0) + iota((half, half), 1) == half - 1).astype(jnp.bfloat16)
     lane = iota((half, 128), 1)
     even = lane % 2 == 0
-    for block in range(blocks):
+    side = lane % 32 < 16
+    def prepare(block):
         parts = [
             data[n * half : n * half + window, part * freqs + block * 128 :][:, :128]
             for n in range(centres)
@@ -75,7 +72,7 @@
             plus = total[:, 128 * g : 128 * (g + 1)]
             minus = diff[:, 128 * g : 128 * (g + 1)]
             minus = jnp.where(
-                lane % 32 < 16, pltpu.roll(minus, 112, 1), -pltpu.roll(minus, 16, 1)
+                side, pltpu.roll(minus, 112, 1), -pltpu.roll(minus, 16, 1)
             )
             stack = [
                 jnp.where(even, plus, 0.0),
@@ -110,12 +107,9 @@
         beams[g] = total
         return c, s
 
-    begin = (jnp.where(first, c1, cs), jnp.where(first, s1, ss))
-    lax.fori_loop(0, 8 * blocks, one_group, begin, unroll=8)
-
     flat = out.reshape(rays * out.shape[1], 128)
     centre = lane // 32
-    for block in range(blocks):
+    def finish(block):
         fine, rest = [], []
         for g in range(8):
             value = beams[block * 8 + g]
@@ -138,8 +132,19 @@
                 value = folded[n * rays : (n + 1) * rays, 128 * v : 128 * (v + 1)]
                 flat[pl.ds(row, rays, stride=out.shape[1]), :] = value
 
-
-def project_kernel(factor, coarse, centres, times, folded, pick, pick9, keys, out, seed, step, outer, proj, ninth):
+    state = (jnp.where(first, c1, cs), jnp.where(first, s1, ss))
+    prepare(0)
+    for block in range(blocks):
+        if block + 1 < blocks:
+            prepare(block + 1)
+        for g in range(8):
+            state = one_group(block * 8 + g, state)
+        if block > 0:
+            finish(block - 1)
+    finish(blocks - 1)
+
+
+def project_kernel(coarse, centres, times, folded, pick, pick9, keys, out, seed, step, outer, proj, ninth):
     half = FINE // 2
     blocks = seed.shape[0]
     bases = times.shape[0]
@@ -148,10 +153,9 @@
     def one_group(base, r):
         for zb in range(blocks):
             cols = slice(zb * 128, zb * 128 + 128)
-            t = times[base, pl.ds(8 * r + zb, 8, stride=32), :]
-            amp = times[base, pl.ds(16 + 8 * r + zb, 8, stride=32), :] * factor
-            angle = t * (math.pi / (2 * coarse * FINE))
-            c0, s0 = jnp.cos(angle), jnp.sin(angle)
+            s0 = times[base, pl.ds(8 * r + zb, 8, stride=32), :]
+            amp = times[base, pl.ds(16 + 8 * r + zb, 8, stride=32), :]
+            c0 = jnp.sqrt(1.0 - s0 * s0)
             c1, s1 = 1.0 - 2.0 * s0 * s0, 2.0 * s0 * c0
             c, s = c0, s0
             for m in range(8):
@@ -224,23 +228,29 @@
     out[:, 64:80, :] = jnp.concatenate(pair, 1).astype(jnp.bfloat16)
 
 
-def open_kernel(own, times, amps, up, down, mine, sems):
+def open_kernel(scale, factor, own, times, amps, up, down, mine, held, sems):
     edge = up.shape[0]
-    copies = [
-        pltpu.make_async_copy(own.at[own.shape[0] - edge :], up, sems.at[0]),
-        pltpu.make_async_copy(own.at[:edge], down, sems.at[1]),
+    pairs = [
+        (times, held.at[0]),
+        (amps, held.at[1]),
+        (own.at[own.shape[0] - edge :], up),
+        (own.at[:edge], down),
     ]
+    copies = [pltpu.make_async_copy(x, y, sems.at[k]) for k, (x, y) in enumerate(pairs)]
     for copy in copies:
         copy.start()
-    rows = [table[r : r + 1, :] for table in (times, amps) for r in range(table.shape[0])]
-    lanes = range(0, times.shape[1], 128)
+    copies[0].wait()
+    copies[1].wait()
+    tables = (jnp.sin(held[0] * scale), held[1] * factor)
+    rows = [table[r : r + 1, :] for table in tables for r in range(held.shape[1])]
+    lanes = range(0, held.shape[2], 128)
     tile = jnp.concatenate([row[:, at : at + 128] for row in rows for at in lanes], 0)
     mine[...] = jnp.broadcast_to(tile[None], mine.shape)
-    for copy in copies:
-        copy.wait()
-
-
-def route_kernel(centres, reach, landing, pick, ninth, keys):
+    copies[2].wait()
+    copies[3].wait()
+
+
+def route_kernel(centres, reach, landing, pick, ninth, keys, lanes):
     devices, rows = ninth.shape
     tile = iota((devices, rows), 0)
     named = jnp.zeros((devices, rows), jnp.float32)
@@ -270,6 +280,9 @@
         value = jnp.sum(jnp.where(slot == k, column, 0.0), axis=1, keepdims=True)
         table = jnp.where(lane == k, value, table)
     keys[...] = table - 1.0
+    column = iota((1, lanes.shape[1]), 1)
+    source = column // 16 % 8 * 128 + column // 128 * 16 + column % 16
+    lanes[...] = (iota(lanes.shape, 0) == source).astype(jnp.bfloat16)
 
 
 def place_kernel(incoming, image, ninth):
@@ -341,22 +354,23 @@
     beam_count = centres * rays
     edge = (half // 2, 2 * freqs)
     last, first, mine = call(
-        open_kernel,
+        functools.partial(open_kernel, math.pi / (2 * freqs), factor),
         (
             pltpu.VMEM(edge, bf16),
             pltpu.VMEM(edge, bf16),
             pltpu.VMEM((size, 4 * depth // 128, 128), f32),
         ),
         (own, travel_time, amplitude),
-        [pltpu.SemaphoreType.DMA((2,))],
-        [pl.BlockSpec(memory_space=pl.ANY)],
-    )
-    pick, pick9, keys = call(
+        [pltpu.VMEM((2,) + travel_time.shape, f32), pltpu.SemaphoreType.DMA((4,))],
+        [pl.BlockSpec(memory_space=pl.ANY)] * 3,
+    )
+    pick, pick9, keys, order = call(
         functools.partial(route_kernel, centres),
         (
             pltpu.VMEM((8 * devices, beam_count), bf16),
             pltpu.VMEM((devices, beam_count), bf16),
             pltpu.VMEM((devices, 128), f32),
+            pltpu.VMEM((256 * centres, 256 * centres), bf16),
         ),
         (reach[0].T, landing[0].T),
         flops=1_000_000_000,
@@ -380,17 +394,17 @@
             taper[None],
             ray_param[None],
             jnp.asarray(fold, bf16),
+            *near(order),
         ),
         [
             pltpu.VMEM((rows + half, 2 * freqs), bf16),
-            pltpu.VMEM((256 * centres, 256 * centres), bf16),
             pltpu.VMEM((freqs // 16, 4 * half, 128), bf16),
             pltpu.VMEM((freqs // 16, rays, 128), f32),
         ],
         flops=8_000_000_000,
     )
     outgoing = call(
-        functools.partial(project_kernel, factor, coarse, centres),
+        functools.partial(project_kernel, coarse, centres),
         pltpu.VMEM((devices, 80, 128), bf16),
         near(times, folded, pick, pick9, keys),
         [

time: 86.6 us -> 83.9 us (0.969)
  Pallas kernels: 22.3 us -> 20.3 us
    pallas_call x5, Pallas kernels: 22.3 us -> 20.3 us  [call(): pl.pallas_call(kernel, out_shape=shapes, in_specs=list(specs) + vmem(len(...]
  transfers between devices with their start and end apart: 3 -> 3, of which waited for: 2 -> 1; matrix products, arithmetic and copies ran while one was open for 0% -> 0% of each run, Pallas kernels for 11% -> 11%
where the time goes in v7:
time: 83.9 us; the launch traced here: 83.6 us
  blocking collectives  46.1 us (55%)
  Pallas kernels  20.3 us (24%)
  starting transfers between devices  14.9 us (18%)
  waiting for transfers between devices  2.13 us (3%)
    all_to_all x1, blocking collectives, on_device(): lax.all_to_all(outgoing, ('line', 'xline'), split_axis=0, concat_axis=0,...  46.1 us
    pallas_call x5, Pallas kernels, call(): pl.pallas_call(kernel, out_shape=shapes, in_specs=list(specs) + vmem(len(...  20.3 us
    all_to_all x1, starting transfers between devices, on_device(): lax.all_to_all(mine, 'xline', split_axis=0, concat_axis=0, tiled=True)  9.44 us
    ppermute x1, starting transfers between devices, on_device(): before = lax.ppermute(last, 'xline', up)  3.54 us
    ppermute x1, waiting for transfers between devices, on_device(): after = lax.ppermute(first, 'xline', down)  2.12 us
    ppermute x1, starting transfers between devices, on_device(): after = lax.ppermute(first, 'xline', down)  1.92 us
  transfers between devices with their start and end apart: 3, of which 1 were waited for; matrix products, arithmetic and copies ran while one was open for 0% of the time, Pallas kernels for 11%

profile of v7, /device:TPU:1, one launch (start us, length us, event | category | flops | bytes accessed | tf_op | source)
XLA Modules:
  0.0 83.6 jit_solution(9764405825600869527)
XLA Ops:
  0.0 1.7 %shard_map.82 = (bf16[32,1024]{1,0:T(8,128)(2,1)S(1)}, bf16[32,1024]{1,0:T(8,128)(2,1)S(1)}, f32[32,32,128]{2,1,0:T(8,128)}) custom-call(bf16[256,1024]{1,0:T(8,128)(2,1)} %bitcast.12, f32[2,1024]{1,0:T(2,128)} %times.1, f32[2,1024]{1,0:T(2,128)} %amps.1), custom_call_target="tpu_custom_call" | custom-call | tf_op jit(solution)/shard_map/pallas_call | solution.py:327
  1.7 9.4 %all-to-all-start = ((f32[32,32,128]{2,1,0:T(8,128)}), f32[32,32,128]{2,1,0:T(8,128)S(1)}, u32[]{:S(2)}, u32[]{:S(2)}) async-start(f32[32,32,128]{2,1,0:T(8,128)} %get-tuple-element.12), calls=%async_computation | async-start | bytes 1048576 | tf_op jit(solution)/shard_map/all_to_all | solution.py:382
  11.2 3.5 %collective-permute-start = (bf16[32,1024]{1,0:T(8,128)(2,1)S(1)}, bf16[32,1024]{1,0:T(8,128)(2,1)S(1)}, u32[]{:S(2)}, u32[]{:S(2)}) collective-permute-start(bf16[32,1024]{1,0:T(8,128)(2,1)S(1)} %get-tuple-element.13), channel_id=1, source_target_pairs={{0,1},{1,2},{2,3},{3,4},{4,5},{5,6},{6,7},{7,8},{8,9},{9,10},{10,1... | collective-permute-start | bytes 196616 | tf_op jit(solution)/shard_map/ppermute | solution.py:380
  14.7 1.9 %collective-permute-start.1 = (bf16[32,1024]{1,0:T(8,128)(2,1)S(1)}, bf16[32,1024]{1,0:T(8,128)(2,1)S(1)}, u32[]{:S(2)}, u32[]{:S(2)}) collective-permute-start(bf16[32,1024]{1,0:T(8,128)(2,1)S(1)} %get-tuple-element.14), channel_id=1, source_target_pairs={{1,0},{2,1},{3,2},{4,3},{5,4},{6,5},{7,6},{8,7},{9,8},{10,9},{11,1... | collective-permute-start | bytes 196616 | tf_op jit(solution)/shard_map/ppermute | solution.py:381
  16.7 1.8 %shard_map.83 = (bf16[1024,256]{1,0:T(8,128)(2,1)S(1)}, bf16[128,256]{1,0:T(8,128)(2,1)S(1)}, f32[128,128]{1,0:T(8,128)S(1)}, bf16[1024,1024]{1,0:T(8,128)(2,1)S(1)}) custom-call(s32[4,256]{1,0:T(4,128)} %bitcast.14, s32[4,256]{1,0:T(4,128)} %bitcast.15), custom_call_target="tpu_custom_call" | custom-call | flops 1000000000 | tf_op jit(solution)/shard_map/pallas_call | solution.py:327
  18.5 0.0 collective-permute-done.before
  18.5 2.1 %collective-permute-done.1.after = bf16[32,1024]{1,0:T(8,128)(2,1)S(1)} collective-permute-done((bf16[32,1024]{1,0:T(8,128)(2,1)S(1)}, bf16[32,1024]{1,0:T(8,128)(2,1)S(1)}, u32[]{:S(2)}, u32[]{:S(2)}) %collective-permute-start.1) | collective-permute-done | bytes 65568 | tf_op jit(solution)/shard_map/ppermute | solution.py:381
  20.6 7.3 %shard_map.84.folded = f32[64,32,128]{2,1,0:T(8,128)S(1)} custom-call(bf16[32,1024]{1,0:T(8,128)(2,1)S(1)} %collective-permute-done.before, bf16[256,1024]{1,0:T(8,128)(2,1)} %bitcast.13, bf16[32,1024]{1,0:T(8,128)(2,1)S(1)} %collective-permute-done.1.after, f32[1,128]{1,0:T(1,128)} %bitcast.16, f32[1,64]{1,0:T(1,128)} %bitcast.17, ...), custom_call_target="tpu_custom_call" | custom-call | flops 8000000000 | tf_op jit(solution)/shard_map/pallas_call | solution.py:327
  27.9 0.0 all-to-all-done
  27.9 7.4 %shard_map.85 = bf16[128,80,128]{2,1,0:T(8,128)(2,1)S(1)} custom-call(f32[4,256,128]{2,1,0:T(8,128)S(1)} %bitcast.11, f32[64,32,128]{2,1,0:T(8,128)S(1)} %shard_map.84.folded, bf16[1024,256]{1,0:T(8,128)(2,1)S(1)} %get-tuple-element.16.pick, bf16[128,256]{1,0:T(8,128)(2,1)S(1)} %get-tuple-element.17.pick9, f32[128,128]{1,0:T(8,128)S(1)} %get-tuple-element.18.keys), custom_call_target="tpu_custom_call" | custom-call | tf_op jit(solution)/shard_map/pallas_call | solution.py:327
  35.4 46.1 %all_to_all.10.incoming = bf16[128,80,128]{2,1,0:T(8,128)(2,1)S(1)} all-to-all(bf16[128,80,128]{2,1,0:T(8,128)(2,1)S(1)} %shard_map.85), channel_id=1, replica_groups=mesh['line'=4,'xline'=32] {'line','xline'}, dimensions={0} | all-to-all | bytes 5242880 | tf_op jit(solution)/shard_map/all_to_all | solution.py:418
  81.5 2.1 %shard_map.86 = f32[1024,128]{1,0:T(8,128)} custom-call(bf16[128,80,128]{2,1,0:T(8,128)(2,1)S(1)} %all_to_all.10.incoming), custom_call_target="tpu_custom_call" | custom-call | tf_op jit(solution)/shard_map/pallas_call | solution.py:327
Async XLA Ops:
  1.7 26.2 %all-to-all-start = ((f32[32,32,128]{2,1,0:T(8,128)}), f32[32,32,128]{2,1,0:T(8,128)S(1)}, u32[]{:S(2)}, u32[]{:S(2)}) async-start(f32[32,32,128]{2,1,0:T(8,128)} %get-tuple-element.12), calls=%async_computation | async-start | bytes 1048576 | tf_op jit(solution)/shard_map/all_to_all | solution.py:382
  11.2 7.3 %collective-permute-start = (bf16[32,1024]{1,0:T(8,128)(2,1)S(1)}, bf16[32,1024]{1,0:T(8,128)(2,1)S(1)}, u32[]{:S(2)}, u32[]{:S(2)}) collective-permute-start(bf16[32,1024]{1,0:T(8,128)(2,1)S(1)} %get-tuple-element.13), channel_id=1, source_target_pairs={{0,1},{1,2},{2,3},{3,4},{4,5},{5,6},{6,7},{7,8},{8,9},{9,10},{10,1... | collective-permute-start | bytes 196616 | tf_op jit(solution)/shard_map/ppermute | solution.py:380
  14.7 5.9 %collective-permute-start.1 = (bf16[32,1024]{1,0:T(8,128)(2,1)S(1)}, bf16[32,1024]{1,0:T(8,128)(2,1)S(1)}, u32[]{:S(2)}, u32[]{:S(2)}) collective-permute-start(bf16[32,1024]{1,0:T(8,128)(2,1)S(1)} %get-tuple-element.14), channel_id=1, source_target_pairs={{1,0},{2,1},{3,2},{4,3},{5,4},{6,5},{7,6},{8,7},{9,8},{10,9},{11,1... | collective-permute-start | bytes 196616 | tf_op jit(solution)/shard_map/ppermute | solution.py:381

commit v8 on v7

--- a/solution.py
+++ b/solution.py
@@ -37,7 +37,7 @@
     return jnp.sum(jnp.where(hit, row, 0.0), axis=1, keepdims=True)
 
 
-def slant_kernel(before, own, after, taper, ray, fold, order, out, data, rows, beams):
+def slant_kernel(before, own, after, taper, ray, fold, out, data, rows, beams):
     half = before.shape[0] * 2
     window = 2 * half
     rays = ray.shape[1]
@@ -56,23 +56,37 @@
     lane = iota((half, 128), 1)
     even = lane % 2 == 0
     side = lane % 32 < 16
+    column = iota((1, 256), 1)
+    source = column // 16 % 2 * 128 + column // 32 * 16 + column % 16
+    order = (iota((256, 256), 0) == source).astype(jnp.bfloat16)
+
     def prepare(block):
-        parts = [
-            data[n * half : n * half + window, part * freqs + block * 128 :][:, :128]
-            for n in range(centres)
-            for part in range(2)
-        ]
-        moved = jnp.dot(
-            jnp.concatenate(parts, 1), order[...], preferred_element_type=jnp.float32
-        )
-        low = jnp.dot(flip, moved[:half].astype(jnp.bfloat16), preferred_element_type=jnp.float32)
-        low, high = low * low_weight, moved[half:] * high_weight
-        total, diff = high + low, high - low
+        sums, turns = [], []
+        for n in range(centres):
+            parts = [
+                data[n * half : n * half + window, part * freqs + block * 128 :][:, :128]
+                for part in range(2)
+            ]
+            moved = jnp.dot(
+                jnp.concatenate(parts, 1), order, preferred_element_type=jnp.float32
+            )
+            low = moved[:half].astype(jnp.bfloat16)
+            low = jnp.dot(flip, low, preferred_element_type=jnp.float32) * low_weight
+            high = moved[half:] * high_weight
+            for value, into in ((high + low, sums), (high - low, turns)):
+                for cut in (0, 128):
+                    tile = value[:, cut : cut + 128]
+                    if into is turns:
+                        tile = jnp.where(side, pltpu.roll(tile, 112, 1), -pltpu.roll(tile, 16, 1))
+                    into.append(pltpu.roll(tile, 32 * n, 1) if n else tile)
         for g in range(8):
-            plus = total[:, 128 * g : 128 * (g + 1)]
-            minus = diff[:, 128 * g : 128 * (g + 1)]
-            minus = jnp.where(
-                side, pltpu.roll(minus, 112, 1), -pltpu.roll(minus, 16, 1)
+            plus, minus = (
+                functools.reduce(
+                    lambda x, c: jnp.where(lane // 32 == c, table[(c - g) % centres * 2 + g // 4], x),
+                    range(1, centres),
+                    table[-g % centres * 2 + g // 4],
+                )
+                for table in (sums, turns)
             )
             stack = [
                 jnp.where(even, plus, 0.0),
@@ -83,13 +97,13 @@
             rows[block * 8 + g] = jnp.concatenate(stack, 0).astype(jnp.bfloat16)
 
     slow = pick_column(ray[...], iota((rays, 1), 0))
-    lane = iota((rays, 128), 1)
-    offset = (lane % half).astype(jnp.float32) + 0.5
+    lanes = iota((rays, 128), 1)
+    offset = (lanes % half).astype(jnp.float32) + 0.5
     angle = slow * offset * (math.pi / freqs)
     c1, s1 = jnp.cos(angle), jnp.sin(angle)
     cs, ss = 1.0 - 2.0 * s1 * s1, 2.0 * s1 * c1
-    first = lane < half
-    pair = lane % 16 // 2
+    first = lanes < half
+    pair = lanes % 16 // 2
 
     def one_group(g, state):
         c, s = state
@@ -108,20 +122,20 @@
         return c, s
 
     flat = out.reshape(rays * out.shape[1], 128)
-    centre = lane // 32
     def finish(block):
         fine, rest = [], []
-        for g in range(8):
-            value = beams[block * 8 + g]
+        for n in range(centres):
+            tiles = []
+            for first_group in (block * 8, block * 8 + 4):
+                tile = beams[first_group + -n % centres]
+                for c in range(1, centres):
+                    tile = jnp.where(lanes // 32 == c, beams[first_group + (c - n) % centres], tile)
+                tiles.append(pltpu.roll(tile, 128 - 32 * n, 1) if n else tile)
+            value = jnp.concatenate(tiles, 1)
             fine.append(value.astype(jnp.bfloat16).astype(jnp.float32))
             rest.append(value - fine[-1])
-        stack = [
-            jnp.concatenate([jnp.where(centre == n, v, 0.0) for v in piece], 1)
-            for piece in (fine, rest)
-            for n in range(centres)
-        ]
         folded = jnp.dot(
-            jnp.concatenate(stack, 0).astype(jnp.bfloat16),
+            jnp.concatenate(fine + rest, 0).astype(jnp.bfloat16),
             fold[...],
             preferred_element_type=jnp.float32,
         )
@@ -250,7 +264,7 @@
     copies[3].wait()
 
 
-def route_kernel(centres, reach, landing, pick, ninth, keys, lanes):
+def route_kernel(centres, reach, landing, pick, ninth, keys):
     devices, rows = ninth.shape
     tile = iota((devices, rows), 0)
     named = jnp.zeros((devices, rows), jnp.float32)
@@ -280,9 +294,6 @@
         value = jnp.sum(jnp.where(slot == k, column, 0.0), axis=1, keepdims=True)
         table = jnp.where(lane == k, value, table)
     keys[...] = table - 1.0
-    column = iota((1, lanes.shape[1]), 1)
-    source = column // 16 % 8 * 128 + column // 128 * 16 + column % 16
-    lanes[...] = (iota(lanes.shape, 0) == source).astype(jnp.bfloat16)
 
 
 def place_kernel(incoming, image, ninth):
@@ -364,13 +375,12 @@
         [pltpu.VMEM((2,) + travel_time.shape, f32), pltpu.SemaphoreType.DMA((4,))],
         [pl.BlockSpec(memory_space=pl.ANY)] * 3,
     )
-    pick, pick9, keys, order = call(
+    pick, pick9, keys = call(
         functools.partial(route_kernel, centres),
         (
             pltpu.VMEM((8 * devices, beam_count), bf16),
             pltpu.VMEM((devices, beam_count), bf16),
             pltpu.VMEM((devices, 128), f32),
-            pltpu.VMEM((256 * centres, 256 * centres), bf16),
         ),
         (reach[0].T, landing[0].T),
         flops=1_000_000_000,
@@ -382,8 +392,8 @@
     times = lax.all_to_all(mine, "xline", split_axis=0, concat_axis=0, tiled=True)
     times = times.reshape(size // 8, 8 * mine.shape[1], 128)
 
-    at = np.arange(8 * 128)
-    fold = fold_matrix()[at // 16 % 2 * 128 + at // 128 * 16 + at % 16]
+    at = np.arange(256)
+    fold = fold_matrix()[at // 16 % 2 * 128 + at // 32 * 16 + at % 16]
     folded = call(
         slant_kernel,
         pltpu.VMEM((rays, 2 * coarse * centres, FINE), f32),
@@ -394,7 +404,6 @@
             taper[None],
             ray_param[None],
             jnp.asarray(fold, bf16),
-            *near(order),
         ),
         [
             pltpu.VMEM((rows + half, 2 * freqs), bf16),

time: 83.9 us -> 83.4 us (level)
  Pallas kernels: 20.3 us -> 19.2 us
    pallas_call x5, Pallas kernels: 20.3 us -> 19.2 us  [call(): pl.pallas_call(kernel, out_shape=shapes, in_specs=list(specs) + vmem(len(...]
  transfers between devices with their start and end apart: 3 -> 3, of which waited for: 1 -> 2; matrix products, arithmetic and copies ran while one was open for 0% -> 0% of each run, Pallas kernels for 11% -> 10%
where the time goes in v8:
time: 83.4 us; the launch traced here: 83 us
  blocking collectives  46.1 us (55%)
  Pallas kernels  19.2 us (23%)
  starting transfers between devices  14.9 us (18%)
  waiting for transfers between devices  2.73 us (3%)
    all_to_all x1, blocking collectives, on_device(): lax.all_to_all(outgoing, ('line', 'xline'), split_axis=0, concat_axis=0,...  46.1 us
    pallas_call x5, Pallas kernels, call(): pl.pallas_call(kernel, out_shape=shapes, in_specs=list(specs) + vmem(len(...  19.2 us
    all_to_all x1, starting transfers between devices, on_device(): lax.all_to_all(mine, 'xline', split_axis=0, concat_axis=0, tiled=True)  9.44 us
    ppermute x1, starting transfers between devices, on_device(): before = lax.ppermute(last, 'xline', up)  3.54 us
    ppermute x1, waiting for transfers between devices, on_device(): after = lax.ppermute(first, 'xline', down)  2.5 us
    ppermute x1, starting transfers between devices, on_device(): after = lax.ppermute(first, 'xline', down)  1.92 us
  transfers between devices with their start and end apart: 3, of which 2 were waited for; matrix products, arithmetic and copies ran while one was open for 0% of the time, Pallas kernels for 10%

profile of v8, /device:TPU:1, one launch (start us, length us, event | category | flops | bytes accessed | tf_op | source)
XLA Modules:
  0.0 83.0 jit_solution(2345987038835453497)
XLA Ops:
  0.0 1.7 %shard_map.82 = (bf16[32,1024]{1,0:T(8,128)(2,1)S(1)}, bf16[32,1024]{1,0:T(8,128)(2,1)S(1)}, f32[32,32,128]{2,1,0:T(8,128)}) custom-call(bf16[256,1024]{1,0:T(8,128)(2,1)} %bitcast.12, f32[2,1024]{1,0:T(2,128)} %times.1, f32[2,1024]{1,0:T(2,128)} %amps.1), custom_call_target="tpu_custom_call" | custom-call | tf_op jit(solution)/shard_map/pallas_call | solution.py:338
  1.7 9.4 %all-to-all-start = ((f32[32,32,128]{2,1,0:T(8,128)}), f32[32,32,128]{2,1,0:T(8,128)S(1)}, u32[]{:S(2)}, u32[]{:S(2)}) async-start(f32[32,32,128]{2,1,0:T(8,128)} %get-tuple-element.11), calls=%async_computation | async-start | bytes 1048576 | tf_op jit(solution)/shard_map/all_to_all | solution.py:392
  11.2 3.5 %collective-permute-start = (bf16[32,1024]{1,0:T(8,128)(2,1)S(1)}, bf16[32,1024]{1,0:T(8,128)(2,1)S(1)}, u32[]{:S(2)}, u32[]{:S(2)}) collective-permute-start(bf16[32,1024]{1,0:T(8,128)(2,1)S(1)} %get-tuple-element.12), channel_id=1, source_target_pairs={{0,1},{1,2},{2,3},{3,4},{4,5},{5,6},{6,7},{7,8},{8,9},{9,10},{10,1... | collective-permute-start | bytes 196616 | tf_op jit(solution)/shard_map/ppermute | solution.py:390
  14.7 1.9 %collective-permute-start.1 = (bf16[32,1024]{1,0:T(8,128)(2,1)S(1)}, bf16[32,1024]{1,0:T(8,128)(2,1)S(1)}, u32[]{:S(2)}, u32[]{:S(2)}) collective-permute-start(bf16[32,1024]{1,0:T(8,128)(2,1)S(1)} %get-tuple-element.13), channel_id=1, source_target_pairs={{1,0},{2,1},{3,2},{4,3},{5,4},{6,5},{7,6},{8,7},{9,8},{10,9},{11,1... | collective-permute-start | bytes 196616 | tf_op jit(solution)/shard_map/ppermute | solution.py:391
  16.7 1.2 %shard_map.84 = (bf16[1024,256]{1,0:T(8,128)(2,1)S(1)}, bf16[128,256]{1,0:T(8,128)(2,1)S(1)}, f32[128,128]{1,0:T(8,128)S(1)}) custom-call(s32[4,256]{1,0:T(4,128)} %bitcast.14, s32[4,256]{1,0:T(4,128)} %bitcast.15), custom_call_target="tpu_custom_call" | custom-call | flops 1000000000 | tf_op jit(solution)/shard_map/pallas_call | solution.py:338
  17.9 0.2 collective-permute-done.before
  18.1 2.5 %collective-permute-done.1.after = bf16[32,1024]{1,0:T(8,128)(2,1)S(1)} collective-permute-done((bf16[32,1024]{1,0:T(8,128)(2,1)S(1)}, bf16[32,1024]{1,0:T(8,128)(2,1)S(1)}, u32[]{:S(2)}, u32[]{:S(2)}) %collective-permute-start.1) | collective-permute-done | bytes 65568 | tf_op jit(solution)/shard_map/ppermute | solution.py:391
  20.6 6.7 %shard_map.83.folded = f32[64,32,128]{2,1,0:T(8,128)S(1)} custom-call(bf16[32,1024]{1,0:T(8,128)(2,1)S(1)} %collective-permute-done.before, bf16[256,1024]{1,0:T(8,128)(2,1)} %bitcast.13, bf16[32,1024]{1,0:T(8,128)(2,1)S(1)} %collective-permute-done.1.after, f32[1,128]{1,0:T(1,128)} %bitcast.16, f32[1,64]{1,0:T(1,128)} %bitcast.17, ...), custom_call_target="tpu_custom_call" | custom-call | flops 8000000000 | tf_op jit(solution)/shard_map/pallas_call | solution.py:338
  27.4 0.0 all-to-all-done
  27.4 7.4 %shard_map.85 = bf16[128,80,128]{2,1,0:T(8,128)(2,1)S(1)} custom-call(f32[4,256,128]{2,1,0:T(8,128)S(1)} %bitcast.11, f32[64,32,128]{2,1,0:T(8,128)S(1)} %shard_map.83.folded, bf16[1024,256]{1,0:T(8,128)(2,1)S(1)} %get-tuple-element.14.pick, bf16[128,256]{1,0:T(8,128)(2,1)S(1)} %get-tuple-element.15.pick9, f32[128,128]{1,0:T(8,128)S(1)} %get-tuple-element.16.keys), custom_call_target="tpu_custom_call" | custom-call | tf_op jit(solution)/shard_map/pallas_call | solution.py:338
  34.8 46.1 %all_to_all.10.incoming = bf16[128,80,128]{2,1,0:T(8,128)(2,1)S(1)} all-to-all(bf16[128,80,128]{2,1,0:T(8,128)(2,1)S(1)} %shard_map.85), channel_id=1, replica_groups=mesh['line'=4,'xline'=32] {'line','xline'}, dimensions={0} | all-to-all | bytes 5242880 | tf_op jit(solution)/shard_map/all_to_all | solution.py:427
  80.9 2.1 %shard_map.86 = f32[1024,128]{1,0:T(8,128)} custom-call(bf16[128,80,128]{2,1,0:T(8,128)(2,1)S(1)} %all_to_all.10.incoming), custom_call_target="tpu_custom_call" | custom-call | tf_op jit(solution)/shard_map/pallas_call | solution.py:338
Async XLA Ops:
  1.7 25.6 %all-to-all-start = ((f32[32,32,128]{2,1,0:T(8,128)}), f32[32,32,128]{2,1,0:T(8,128)S(1)}, u32[]{:S(2)}, u32[]{:S(2)}) async-start(f32[32,32,128]{2,1,0:T(8,128)} %get-tuple-element.11), calls=%async_computation | async-start | bytes 1048576 | tf_op jit(solution)/shard_map/all_to_all | solution.py:392
  11.2 6.9 %collective-permute-start = (bf16[32,1024]{1,0:T(8,128)(2,1)S(1)}, bf16[32,1024]{1,0:T(8,128)(2,1)S(1)}, u32[]{:S(2)}, u32[]{:S(2)}) collective-permute-start(bf16[32,1024]{1,0:T(8,128)(2,1)S(1)} %get-tuple-element.12), channel_id=1, source_target_pairs={{0,1},{1,2},{2,3},{3,4},{4,5},{5,6},{6,7},{7,8},{8,9},{9,10},{10,1... | collective-permute-start | bytes 196616 | tf_op jit(solution)/shard_map/ppermute | solution.py:390
  14.7 5.9 %collective-permute-start.1 = (bf16[32,1024]{1,0:T(8,128)(2,1)S(1)}, bf16[32,1024]{1,0:T(8,128)(2,1)S(1)}, u32[]{:S(2)}, u32[]{:S(2)}) collective-permute-start(bf16[32,1024]{1,0:T(8,128)(2,1)S(1)} %get-tuple-element.13), channel_id=1, source_target_pairs={{1,0},{2,1},{3,2},{4,3},{5,4},{6,5},{7,6},{8,7},{9,8},{10,9},{11,1... | collective-permute-start | bytes 196616 | tf_op jit(solution)/shard_map/ppermute | solution.py:391

commit v9 on v8

--- a/solution.py
+++ b/solution.py
@@ -383,7 +383,7 @@
             pltpu.VMEM((devices, 128), f32),
         ),
         (reach[0].T, landing[0].T),
-        flops=1_000_000_000,
+        flops=100_000_000,
     )
     up = [(i, i + 1) for i in range(size - 1)]
     down = [(j, i) for i, j in up]

time: 83.4 us -> 80 us (0.959)
  blocking collectives: 46.1 us -> 41.8 us
    all_to_all x1, blocking collectives: 46.1 us -> 41.8 us  [on_device(): lax.all_to_all(outgoing, ('line', 'xline'), split_axis=0, concat_axis=0,...]
    all_to_all x1, waiting for transfers between devices: 0.01 us -> 3.55 us  [on_device(): lax.all_to_all(mine, 'xline', split_axis=0, concat_axis=0, tiled=True)]
    ppermute x1, waiting for transfers between devices: 2.5 us -> 0.01 us  [on_device(): after = lax.ppermute(first, 'xline', down)]
    ppermute x1, starting transfers between devices: 3.54 us -> 4.51 us  [on_device(): before = lax.ppermute(last, 'xline', up)]
    all_to_all x1, starting transfers between devices: 9.44 us -> 8.57 us  [on_device(): lax.all_to_all(mine, 'xline', split_axis=0, concat_axis=0, tiled=True)]
  transfers between devices with their start and end apart: 3 -> 3, of which waited for: 2 -> 1; matrix products, arithmetic and copies ran while one was open for 0% -> 0% of each run, Pallas kernels for 10% -> 10%
where the time goes in v9:
time: 80 us; the launch traced here: 79.6 us
  blocking collectives  41.8 us (52%)
  Pallas kernels  19.2 us (24%)
  starting transfers between devices  15 us (19%)
  waiting for transfers between devices  3.56 us (4%)
    all_to_all x1, blocking collectives, on_device(): lax.all_to_all(outgoing, ('line', 'xline'), split_axis=0, concat_axis=0,...  41.8 us
    pallas_call x5, Pallas kernels, call(): pl.pallas_call(kernel, out_shape=shapes, in_specs=list(specs) + vmem(len(...  19.2 us
    all_to_all x1, starting transfers between devices, on_device(): lax.all_to_all(mine, 'xline', split_axis=0, concat_axis=0, tiled=True)  8.57 us
    ppermute x1, starting transfers between devices, on_device(): before = lax.ppermute(last, 'xline', up)  4.51 us
    all_to_all x1, waiting for transfers between devices, on_device(): lax.all_to_all(mine, 'xline', split_axis=0, concat_axis=0, tiled=True)  3.55 us
    ppermute x1, starting transfers between devices, on_device(): after = lax.ppermute(first, 'xline', down)  1.92 us
  transfers between devices with their start and end apart: 3, of which 1 were waited for; matrix products, arithmetic and copies ran while one was open for 0% of the time, Pallas kernels for 10%

profile of v9, /device:TPU:1, one launch (start us, length us, event | category | flops | bytes accessed | tf_op | source)
XLA Modules:
  0.0 79.6 jit_solution(4033849160709345484)
XLA Ops:
  0.0 1.7 %shard_map.82 = (bf16[32,1024]{1,0:T(8,128)(2,1)S(1)}, bf16[32,1024]{1,0:T(8,128)(2,1)S(1)}, f32[32,32,128]{2,1,0:T(8,128)}) custom-call(bf16[256,1024]{1,0:T(8,128)(2,1)} %bitcast.12, f32[2,1024]{1,0:T(2,128)} %times.1, f32[2,1024]{1,0:T(2,128)} %amps.1), custom_call_target="tpu_custom_call" | custom-call | tf_op jit(solution)/shard_map/pallas_call | solution.py:338
  1.7 4.5 %collective-permute-start = (bf16[32,1024]{1,0:T(8,128)(2,1)S(1)}, bf16[32,1024]{1,0:T(8,128)(2,1)S(1)}, u32[]{:S(2)}, u32[]{:S(2)}) collective-permute-start(bf16[32,1024]{1,0:T(8,128)(2,1)S(1)} %get-tuple-element.12), channel_id=1, source_target_pairs={{0,1},{1,2},{2,3},{3,4},{4,5},{5,6},{6,7},{7,8},{8,9},{9,10},{10,1... | collective-permute-start | bytes 196616 | tf_op jit(solution)/shard_map/ppermute | solution.py:390
  6.3 1.9 %collective-permute-start.1 = (bf16[32,1024]{1,0:T(8,128)(2,1)S(1)}, bf16[32,1024]{1,0:T(8,128)(2,1)S(1)}, u32[]{:S(2)}, u32[]{:S(2)}) collective-permute-start(bf16[32,1024]{1,0:T(8,128)(2,1)S(1)} %get-tuple-element.13), channel_id=1, source_target_pairs={{1,0},{2,1},{3,2},{4,3},{5,4},{6,5},{7,6},{8,7},{9,8},{10,9},{11,1... | collective-permute-start | bytes 196616 | tf_op jit(solution)/shard_map/ppermute | solution.py:391
  8.2 8.6 %all-to-all-start = ((f32[32,32,128]{2,1,0:T(8,128)}), f32[32,32,128]{2,1,0:T(8,128)S(1)}, u32[]{:S(2)}, u32[]{:S(2)}) async-start(f32[32,32,128]{2,1,0:T(8,128)} %get-tuple-element.11), calls=%async_computation | async-start | bytes 1048576 | tf_op jit(solution)/shard_map/all_to_all | solution.py:392
  16.8 1.2 %shard_map.84 = (bf16[1024,256]{1,0:T(8,128)(2,1)S(1)}, bf16[128,256]{1,0:T(8,128)(2,1)S(1)}, f32[128,128]{1,0:T(8,128)S(1)}) custom-call(s32[4,256]{1,0:T(4,128)} %bitcast.14, s32[4,256]{1,0:T(4,128)} %bitcast.15), custom_call_target="tpu_custom_call" | custom-call | flops 100000000 | tf_op jit(solution)/shard_map/pallas_call | solution.py:338
  18.0 0.0 collective-permute-done.before
  18.0 0.0 collective-permute-done.1.after
  18.0 6.7 %shard_map.83.folded = f32[64,32,128]{2,1,0:T(8,128)S(1)} custom-call(bf16[32,1024]{1,0:T(8,128)(2,1)S(1)} %collective-permute-done.before, bf16[256,1024]{1,0:T(8,128)(2,1)} %bitcast.13, bf16[32,1024]{1,0:T(8,128)(2,1)S(1)} %collective-permute-done.1.after, f32[1,128]{1,0:T(1,128)} %bitcast.16, f32[1,64]{1,0:T(1,128)} %bitcast.17, ...), custom_call_target="tpu_custom_call" | custom-call | flops 8000000000 | tf_op jit(solution)/shard_map/pallas_call | solution.py:338
  24.8 3.6 %all-to-all-done = f32[32,32,128]{2,1,0:T(8,128)S(1)} async-done(((f32[32,32,128]{2,1,0:T(8,128)}), f32[32,32,128]{2,1,0:T(8,128)S(1)}, u32[]{:S(2)}, u32[]{:S(2)}) %all-to-all-start) | async-done | bytes 524320 | tf_op jit(solution)/shard_map/all_to_all | solution.py:392
  28.3 7.4 %shard_map.85 = bf16[128,80,128]{2,1,0:T(8,128)(2,1)S(1)} custom-call(f32[4,256,128]{2,1,0:T(8,128)S(1)} %bitcast.11, f32[64,32,128]{2,1,0:T(8,128)S(1)} %shard_map.83.folded, bf16[1024,256]{1,0:T(8,128)(2,1)S(1)} %get-tuple-element.14.pick, bf16[128,256]{1,0:T(8,128)(2,1)S(1)} %get-tuple-element.15.pick9, f32[128,128]{1,0:T(8,128)S(1)} %get-tuple-element.16.keys), custom_call_target="tpu_custom_call" | custom-call | tf_op jit(solution)/shard_map/pallas_call | solution.py:338
  35.7 41.8 %all_to_all.10.incoming = bf16[128,80,128]{2,1,0:T(8,128)(2,1)S(1)} all-to-all(bf16[128,80,128]{2,1,0:T(8,128)(2,1)S(1)} %shard_map.85), channel_id=1, replica_groups=mesh['line'=4,'xline'=32] {'line','xline'}, dimensions={0} | all-to-all | bytes 5242880 | tf_op jit(solution)/shard_map/all_to_all | solution.py:427
  77.5 2.1 %shard_map.86 = f32[1024,128]{1,0:T(8,128)} custom-call(bf16[128,80,128]{2,1,0:T(8,128)(2,1)S(1)} %all_to_all.10.incoming), custom_call_target="tpu_custom_call" | custom-call | tf_op jit(solution)/shard_map/pallas_call | solution.py:338
Async XLA Ops:
  1.7 16.3 %collective-permute-start = (bf16[32,1024]{1,0:T(8,128)(2,1)S(1)}, bf16[32,1024]{1,0:T(8,128)(2,1)S(1)}, u32[]{:S(2)}, u32[]{:S(2)}) collective-permute-start(bf16[32,1024]{1,0:T(8,128)(2,1)S(1)} %get-tuple-element.12), channel_id=1, source_target_pairs={{0,1},{1,2},{2,3},{3,4},{4,5},{5,6},{6,7},{7,8},{8,9},{9,10},{10,1... | collective-permute-start | bytes 196616 | tf_op jit(solution)/shard_map/ppermute | solution.py:390
  6.3 11.7 %collective-permute-start.1 = (bf16[32,1024]{1,0:T(8,128)(2,1)S(1)}, bf16[32,1024]{1,0:T(8,128)(2,1)S(1)}, u32[]{:S(2)}, u32[]{:S(2)}) collective-permute-start(bf16[32,1024]{1,0:T(8,128)(2,1)S(1)} %get-tuple-element.13), channel_id=1, source_target_pairs={{1,0},{2,1},{3,2},{4,3},{5,4},{6,5},{7,6},{8,7},{9,8},{10,9},{11,1... | collective-permute-start | bytes 196616 | tf_op jit(solution)/shard_map/ppermute | solution.py:391
  8.2 20.1 %all-to-all-start = ((f32[32,32,128]{2,1,0:T(8,128)}), f32[32,32,128]{2,1,0:T(8,128)S(1)}, u32[]{:S(2)}, u32[]{:S(2)}) async-start(f32[32,32,128]{2,1,0:T(8,128)} %get-tuple-element.11), calls=%async_computation | async-start | bytes 1048576 | tf_op jit(solution)/shard_map/all_to_all | solution.py:392

commit v10 on v9

--- a/solution.py
+++ b/solution.py
@@ -160,7 +160,7 @@
 
 def project_kernel(coarse, centres, times, folded, pick, pick9, keys, out, seed, step, outer, proj, ninth):
     half = FINE // 2
-    blocks = seed.shape[0]
+    blocks = seed.shape[1]
     bases = times.shape[0]
     upper = iota((2 * centres, 128), 0) < centres
 
@@ -173,21 +173,21 @@
             c1, s1 = 1.0 - 2.0 * s0 * s0, 2.0 * s0 * c0
             c, s = c0, s0
             for m in range(8):
-                seed[zb, m * 8 : m * 8 + 8, :] = c
-                seed[zb, 64 + m * 8 : 72 + m * 8, :] = s
+                seed[r, zb, m * 8 : m * 8 + 8, :] = c
+                seed[r, zb, 64 + m * 8 : 72 + m * 8, :] = s
                 if m < 7:
                     c, s = c * c1 - s * s1, s * c1 + c * s1
             c, s = c1, s1
             for power in range(6):
                 c, s = 1.0 - 2.0 * s * s, 2.0 * s * c
                 if power == 2:
-                    step[0:8, cols] = c
-                    step[8:16, cols] = s
+                    step[r, 0:8, cols] = c
+                    step[r, 8:16, cols] = s
             ca, sa = (c * c0 - s * s0) * amp, (s * c0 + c * s0) * amp
             cb, sb = 1.0 - 2.0 * s * s, 2.0 * s * c
             for a in range(coarse):
-                outer[16 * a : 16 * a + 8, cols] = ca
-                outer[16 * a + 8 : 16 * a + 16, cols] = sa
+                outer[r, 16 * a : 16 * a + 8, cols] = ca
+                outer[r, 16 * a + 8 : 16 * a + 16, cols] = sa
                 ca, sa = ca * cb - sa * sb, sa * cb + ca * sb
         held = [None] * blocks
         for i in range(8):
@@ -195,10 +195,10 @@
             rows = folded[p].astype(jnp.bfloat16)
             for zb in range(blocks):
                 cols = slice(zb * 128, zb * 128 + 128)
-                c = seed[zb, pl.ds(i, 8, stride=8), :]
-                s = seed[zb, pl.ds(64 + i, 8, stride=8), :]
-                cs = jnp.broadcast_to(step[i : i + 1, cols], (8, 128))
-                ss = jnp.broadcast_to(step[8 + i : 9 + i, cols], (8, 128))
+                c = seed[r, zb, pl.ds(i, 8, stride=8), :]
+                s = seed[r, zb, pl.ds(64 + i, 8, stride=8), :]
+                cs = jnp.broadcast_to(step[r, i : i + 1, cols], (8, 128))
+                ss = jnp.broadcast_to(step[r, 8 + i : 9 + i, cols], (8, 128))
                 real, imag = [c], [s]
                 for _ in range(half // 8 - 1):
                     c, s = c * cs - s * ss, s * cs + c * ss
@@ -210,8 +210,8 @@
                 for a in range(coarse):
                     turn = jnp.where(
                         upper,
-                        jnp.broadcast_to(outer[16 * a + i : 16 * a + i + 1, cols], upper.shape),
-                        jnp.broadcast_to(outer[16 * a + 8 + i : 16 * a + 9 + i, cols], upper.shape),
+                        jnp.broadcast_to(outer[r, 16 * a + i : 16 * a + i + 1, cols], upper.shape),
+                        jnp.broadcast_to(outer[r, 16 * a + 8 + i : 16 * a + 9 + i, cols], upper.shape),
                     )
                     total = total + parts[2 * centres * a : 2 * centres * (a + 1)] * turn
                 total = total + pltpu.roll(total, centres, 0)
@@ -417,9 +417,9 @@
         pltpu.VMEM((devices, 80, 128), bf16),
         near(times, folded, pick, pick9, keys),
         [
-            pltpu.VMEM((depth // 128, 128, 128), f32),
-            pltpu.VMEM((16, depth), f32),
-            pltpu.VMEM((16 * coarse, depth), f32),
+            pltpu.VMEM((2, depth // 128, 128, 128), f32),
+            pltpu.VMEM((2, 16, depth), f32),
+            pltpu.VMEM((2, 16 * coarse, depth), f32),
             pltpu.VMEM((beam_count // (2 * centres), 2 * centres, depth), f32),
             pltpu.VMEM((devices * 8, 128), f32),
         ],

time: 80 us -> 80.2 us (level)
  no operation moved by 1% of the time
where the time goes in v10:
time: 80.2 us; the launch traced here: 79.8 us
  blocking collectives  41.8 us (52%)
  Pallas kernels  19.3 us (24%)
  starting transfers between devices  15 us (19%)
  waiting for transfers between devices  3.56 us (4%)
    all_to_all x1, blocking collectives, on_device(): lax.all_to_all(outgoing, ('line', 'xline'), split_axis=0, concat_axis=0,...  41.8 us
    pallas_call x5, Pallas kernels, call(): pl.pallas_call(kernel, out_shape=shapes, in_specs=list(specs) + vmem(len(...  19.3 us
    all_to_all x1, starting transfers between devices, on_device(): lax.all_to_all(mine, 'xline', split_axis=0, concat_axis=0, tiled=True)  8.57 us
    ppermute x1, starting transfers between devices, on_device(): before = lax.ppermute(last, 'xline', up)  4.51 us
    all_to_all x1, waiting for transfers between devices, on_device(): lax.all_to_all(mine, 'xline', split_axis=0, concat_axis=0, tiled=True)  3.55 us
    ppermute x1, starting transfers between devices, on_device(): after = lax.ppermute(first, 'xline', down)  1.92 us
  transfers between devices with their start and end apart: 3, of which 1 were waited for; matrix products, arithmetic and copies ran while one was open for 0% of the time, Pallas kernels for 10%

profile of v10, /device:TPU:1, one launch (start us, length us, event | category | flops | bytes accessed | tf_op | source)
XLA Modules:
  0.0 79.8 jit_solution(2689423716072891241)
XLA Ops:
  0.0 1.7 %shard_map.82 = (bf16[32,1024]{1,0:T(8,128)(2,1)S(1)}, bf16[32,1024]{1,0:T(8,128)(2,1)S(1)}, f32[32,32,128]{2,1,0:T(8,128)}) custom-call(bf16[256,1024]{1,0:T(8,128)(2,1)} %bitcast.12, f32[2,1024]{1,0:T(2,128)} %times.1, f32[2,1024]{1,0:T(2,128)} %amps.1), custom_call_target="tpu_custom_call" | custom-call | tf_op jit(solution)/shard_map/pallas_call | solution.py:338
  1.7 4.5 %collective-permute-start = (bf16[32,1024]{1,0:T(8,128)(2,1)S(1)}, bf16[32,1024]{1,0:T(8,128)(2,1)S(1)}, u32[]{:S(2)}, u32[]{:S(2)}) collective-permute-start(bf16[32,1024]{1,0:T(8,128)(2,1)S(1)} %get-tuple-element.12), channel_id=1, source_target_pairs={{0,1},{1,2},{2,3},{3,4},{4,5},{5,6},{6,7},{7,8},{8,9},{9,10},{10,1... | collective-permute-start | bytes 196616 | tf_op jit(solution)/shard_map/ppermute | solution.py:390
  6.3 1.9 %collective-permute-start.1 = (bf16[32,1024]{1,0:T(8,128)(2,1)S(1)}, bf16[32,1024]{1,0:T(8,128)(2,1)S(1)}, u32[]{:S(2)}, u32[]{:S(2)}) collective-permute-start(bf16[32,1024]{1,0:T(8,128)(2,1)S(1)} %get-tuple-element.13), channel_id=1, source_target_pairs={{1,0},{2,1},{3,2},{4,3},{5,4},{6,5},{7,6},{8,7},{9,8},{10,9},{11,1... | collective-permute-start | bytes 196616 | tf_op jit(solution)/shard_map/ppermute | solution.py:391
  8.2 8.6 %all-to-all-start = ((f32[32,32,128]{2,1,0:T(8,128)}), f32[32,32,128]{2,1,0:T(8,128)S(1)}, u32[]{:S(2)}, u32[]{:S(2)}) async-start(f32[32,32,128]{2,1,0:T(8,128)} %get-tuple-element.11), calls=%async_computation | async-start | bytes 1048576 | tf_op jit(solution)/shard_map/all_to_all | solution.py:392
  16.8 1.2 %shard_map.84 = (bf16[1024,256]{1,0:T(8,128)(2,1)S(1)}, bf16[128,256]{1,0:T(8,128)(2,1)S(1)}, f32[128,128]{1,0:T(8,128)S(1)}) custom-call(s32[4,256]{1,0:T(4,128)} %bitcast.14, s32[4,256]{1,0:T(4,128)} %bitcast.15), custom_call_target="tpu_custom_call" | custom-call | flops 100000000 | tf_op jit(solution)/shard_map/pallas_call | solution.py:338
  18.0 0.0 collective-permute-done.before
  18.0 0.0 collective-permute-done.1.after
  18.0 6.7 %shard_map.83.folded = f32[64,32,128]{2,1,0:T(8,128)S(1)} custom-call(bf16[32,1024]{1,0:T(8,128)(2,1)S(1)} %collective-permute-done.before, bf16[256,1024]{1,0:T(8,128)(2,1)} %bitcast.13, bf16[32,1024]{1,0:T(8,128)(2,1)S(1)} %collective-permute-done.1.after, f32[1,128]{1,0:T(1,128)} %bitcast.16, f32[1,64]{1,0:T(1,128)} %bitcast.17, ...), custom_call_target="tpu_custom_call" | custom-call | flops 8000000000 | tf_op jit(solution)/shard_map/pallas_call | solution.py:338
  24.8 3.6 %all-to-all-done = f32[32,32,128]{2,1,0:T(8,128)S(1)} async-done(((f32[32,32,128]{2,1,0:T(8,128)}), f32[32,32,128]{2,1,0:T(8,128)S(1)}, u32[]{:S(2)}, u32[]{:S(2)}) %all-to-all-start) | async-done | bytes 524320 | tf_op jit(solution)/shard_map/all_to_all | solution.py:392
  28.3 7.6 %shard_map.85 = bf16[128,80,128]{2,1,0:T(8,128)(2,1)S(1)} custom-call(f32[4,256,128]{2,1,0:T(8,128)S(1)} %bitcast.11, f32[64,32,128]{2,1,0:T(8,128)S(1)} %shard_map.83.folded, bf16[1024,256]{1,0:T(8,128)(2,1)S(1)} %get-tuple-element.14.pick, bf16[128,256]{1,0:T(8,128)(2,1)S(1)} %get-tuple-element.15.pick9, f32[128,128]{1,0:T(8,128)S(1)} %get-tuple-element.16.keys), custom_call_target="tpu_custom_call" | custom-call | tf_op jit(solution)/shard_map/pallas_call | solution.py:338
  35.9 41.8 %all_to_all.10.incoming = bf16[128,80,128]{2,1,0:T(8,128)(2,1)S(1)} all-to-all(bf16[128,80,128]{2,1,0:T(8,128)(2,1)S(1)} %shard_map.85), channel_id=1, replica_groups=mesh['line'=4,'xline'=32] {'line','xline'}, dimensions={0} | all-to-all | bytes 5242880 | tf_op jit(solution)/shard_map/all_to_all | solution.py:427
  77.7 2.1 %shard_map.86 = f32[1024,128]{1,0:T(8,128)} custom-call(bf16[128,80,128]{2,1,0:T(8,128)(2,1)S(1)} %all_to_all.10.incoming), custom_call_target="tpu_custom_call" | custom-call | tf_op jit(solution)/shard_map/pallas_call | solution.py:338
Async XLA Ops:
  1.7 16.3 %collective-permute-start = (bf16[32,1024]{1,0:T(8,128)(2,1)S(1)}, bf16[32,1024]{1,0:T(8,128)(2,1)S(1)}, u32[]{:S(2)}, u32[]{:S(2)}) collective-permute-start(bf16[32,1024]{1,0:T(8,128)(2,1)S(1)} %get-tuple-element.12), channel_id=1, source_target_pairs={{0,1},{1,2},{2,3},{3,4},{4,5},{5,6},{6,7},{7,8},{8,9},{9,10},{10,1... | collective-permute-start | bytes 196616 | tf_op jit(solution)/shard_map/ppermute | solution.py:390
  6.3 11.7 %collective-permute-start.1 = (bf16[32,1024]{1,0:T(8,128)(2,1)S(1)}, bf16[32,1024]{1,0:T(8,128)(2,1)S(1)}, u32[]{:S(2)}, u32[]{:S(2)}) collective-permute-start(bf16[32,1024]{1,0:T(8,128)(2,1)S(1)} %get-tuple-element.13), channel_id=1, source_target_pairs={{1,0},{2,1},{3,2},{4,3},{5,4},{6,5},{7,6},{8,7},{9,8},{10,9},{11,1... | collective-permute-start | bytes 196616 | tf_op jit(solution)/shard_map/ppermute | solution.py:391
  8.2 20.1 %all-to-all-start = ((f32[32,32,128]{2,1,0:T(8,128)}), f32[32,32,128]{2,1,0:T(8,128)S(1)}, u32[]{:S(2)}, u32[]{:S(2)}) async-start(f32[32,32,128]{2,1,0:T(8,128)} %get-tuple-element.11), calls=%async_computation | async-start | bytes 1048576 | tf_op jit(solution)/shard_map/all_to_all | solution.py:392

commit v11 on v9

--- a/solution.py
+++ b/solution.py
@@ -226,7 +226,7 @@
         one_group(base, 1)
         return carry
 
-    lax.fori_loop(0, bases, one_base, 0)
+    lax.fori_loop(0, bases, one_base, 0, unroll=4)
 
     sends = proj[...].reshape(-1, 128 * blocks).astype(jnp.bfloat16)
     devices = keys.shape[0]

time: 80 us -> 80.1 us (level)
  no operation moved by 1% of the time
where the time goes in v11:
time: 80.1 us; the launch traced here: 79.7 us
  blocking collectives  41.8 us (52%)
  Pallas kernels  19.3 us (24%)
  starting transfers between devices  15 us (19%)
  waiting for transfers between devices  3.55 us (4%)
    all_to_all x1, blocking collectives, on_device(): lax.all_to_all(outgoing, ('line', 'xline'), split_axis=0, concat_axis=0,...  41.8 us
    pallas_call x5, Pallas kernels, call(): pl.pallas_call(kernel, out_shape=shapes, in_specs=list(specs) + vmem(len(...  19.3 us
    all_to_all x1, starting transfers between devices, on_device(): lax.all_to_all(mine, 'xline', split_axis=0, concat_axis=0, tiled=True)  8.57 us
    ppermute x1, starting transfers between devices, on_device(): before = lax.ppermute(last, 'xline', up)  4.51 us
    all_to_all x1, waiting for transfers between devices, on_device(): lax.all_to_all(mine, 'xline', split_axis=0, concat_axis=0, tiled=True)  3.55 us
    ppermute x1, starting transfers between devices, on_device(): after = lax.ppermute(first, 'xline', down)  1.92 us
  transfers between devices with their start and end apart: 3, of which 1 were waited for; matrix products, arithmetic and copies ran while one was open for 0% of the time, Pallas kernels for 10%

profile of v11, /device:TPU:1, one launch (start us, length us, event | category | flops | bytes accessed | tf_op | source)
XLA Modules:
  0.0 79.7 jit_solution(634099527784299478)
XLA Ops:
  0.0 1.7 %shard_map.82 = (bf16[32,1024]{1,0:T(8,128)(2,1)S(1)}, bf16[32,1024]{1,0:T(8,128)(2,1)S(1)}, f32[32,32,128]{2,1,0:T(8,128)}) custom-call(bf16[256,1024]{1,0:T(8,128)(2,1)} %bitcast.12, f32[2,1024]{1,0:T(2,128)} %times.1, f32[2,1024]{1,0:T(2,128)} %amps.1), custom_call_target="tpu_custom_call" | custom-call | tf_op jit(solution)/shard_map/pallas_call | solution.py:338
  1.7 4.5 %collective-permute-start = (bf16[32,1024]{1,0:T(8,128)(2,1)S(1)}, bf16[32,1024]{1,0:T(8,128)(2,1)S(1)}, u32[]{:S(2)}, u32[]{:S(2)}) collective-permute-start(bf16[32,1024]{1,0:T(8,128)(2,1)S(1)} %get-tuple-element.12), channel_id=1, source_target_pairs={{0,1},{1,2},{2,3},{3,4},{4,5},{5,6},{6,7},{7,8},{8,9},{9,10},{10,1... | collective-permute-start | bytes 196616 | tf_op jit(solution)/shard_map/ppermute | solution.py:390
  6.3 1.9 %collective-permute-start.1 = (bf16[32,1024]{1,0:T(8,128)(2,1)S(1)}, bf16[32,1024]{1,0:T(8,128)(2,1)S(1)}, u32[]{:S(2)}, u32[]{:S(2)}) collective-permute-start(bf16[32,1024]{1,0:T(8,128)(2,1)S(1)} %get-tuple-element.13), channel_id=1, source_target_pairs={{1,0},{2,1},{3,2},{4,3},{5,4},{6,5},{7,6},{8,7},{9,8},{10,9},{11,1... | collective-permute-start | bytes 196616 | tf_op jit(solution)/shard_map/ppermute | solution.py:391
  8.2 8.6 %all-to-all-start = ((f32[32,32,128]{2,1,0:T(8,128)}), f32[32,32,128]{2,1,0:T(8,128)S(1)}, u32[]{:S(2)}, u32[]{:S(2)}) async-start(f32[32,32,128]{2,1,0:T(8,128)} %get-tuple-element.11), calls=%async_computation | async-start | bytes 1048576 | tf_op jit(solution)/shard_map/all_to_all | solution.py:392
  16.8 1.2 %shard_map.84 = (bf16[1024,256]{1,0:T(8,128)(2,1)S(1)}, bf16[128,256]{1,0:T(8,128)(2,1)S(1)}, f32[128,128]{1,0:T(8,128)S(1)}) custom-call(s32[4,256]{1,0:T(4,128)} %bitcast.14, s32[4,256]{1,0:T(4,128)} %bitcast.15), custom_call_target="tpu_custom_call" | custom-call | flops 100000000 | tf_op jit(solution)/shard_map/pallas_call | solution.py:338
  18.0 0.0 collective-permute-done.before
  18.0 0.0 collective-permute-done.1.after
  18.0 6.8 %shard_map.83.folded = f32[64,32,128]{2,1,0:T(8,128)S(1)} custom-call(bf16[32,1024]{1,0:T(8,128)(2,1)S(1)} %collective-permute-done.before, bf16[256,1024]{1,0:T(8,128)(2,1)} %bitcast.13, bf16[32,1024]{1,0:T(8,128)(2,1)S(1)} %collective-permute-done.1.after, f32[1,128]{1,0:T(1,128)} %bitcast.16, f32[1,64]{1,0:T(1,128)} %bitcast.17, ...), custom_call_target="tpu_custom_call" | custom-call | flops 8000000000 | tf_op jit(solution)/shard_map/pallas_call | solution.py:338
  24.8 3.5 %all-to-all-done = f32[32,32,128]{2,1,0:T(8,128)S(1)} async-done(((f32[32,32,128]{2,1,0:T(8,128)}), f32[32,32,128]{2,1,0:T(8,128)S(1)}, u32[]{:S(2)}, u32[]{:S(2)}) %all-to-all-start) | async-done | bytes 524320 | tf_op jit(solution)/shard_map/all_to_all | solution.py:392
  28.3 7.5 %shard_map.85 = bf16[128,80,128]{2,1,0:T(8,128)(2,1)S(1)} custom-call(f32[4,256,128]{2,1,0:T(8,128)S(1)} %bitcast.11, f32[64,32,128]{2,1,0:T(8,128)S(1)} %shard_map.83.folded, bf16[1024,256]{1,0:T(8,128)(2,1)S(1)} %get-tuple-element.14.pick, bf16[128,256]{1,0:T(8,128)(2,1)S(1)} %get-tuple-element.15.pick9, f32[128,128]{1,0:T(8,128)S(1)} %get-tuple-element.16.keys), custom_call_target="tpu_custom_call" | custom-call | tf_op jit(solution)/shard_map/pallas_call | solution.py:338
  35.8 41.8 %all_to_all.10.incoming = bf16[128,80,128]{2,1,0:T(8,128)(2,1)S(1)} all-to-all(bf16[128,80,128]{2,1,0:T(8,128)(2,1)S(1)} %shard_map.85), channel_id=1, replica_groups=mesh['line'=4,'xline'=32] {'line','xline'}, dimensions={0} | all-to-all | bytes 5242880 | tf_op jit(solution)/shard_map/all_to_all | solution.py:427
  77.7 2.1 %shard_map.86 = f32[1024,128]{1,0:T(8,128)} custom-call(bf16[128,80,128]{2,1,0:T(8,128)(2,1)S(1)} %all_to_all.10.incoming), custom_call_target="tpu_custom_call" | custom-call | tf_op jit(solution)/shard_map/pallas_call | solution.py:338
Async XLA Ops:
  1.7 16.3 %collective-permute-start = (bf16[32,1024]{1,0:T(8,128)(2,1)S(1)}, bf16[32,1024]{1,0:T(8,128)(2,1)S(1)}, u32[]{:S(2)}, u32[]{:S(2)}) collective-permute-start(bf16[32,1024]{1,0:T(8,128)(2,1)S(1)} %get-tuple-element.12), channel_id=1, source_target_pairs={{0,1},{1,2},{2,3},{3,4},{4,5},{5,6},{6,7},{7,8},{8,9},{9,10},{10,1... | collective-permute-start | bytes 196616 | tf_op jit(solution)/shard_map/ppermute | solution.py:390
  6.3 11.7 %collective-permute-start.1 = (bf16[32,1024]{1,0:T(8,128)(2,1)S(1)}, bf16[32,1024]{1,0:T(8,128)(2,1)S(1)}, u32[]{:S(2)}, u32[]{:S(2)}) collective-permute-start(bf16[32,1024]{1,0:T(8,128)(2,1)S(1)} %get-tuple-element.13), channel_id=1, source_target_pairs={{1,0},{2,1},{3,2},{4,3},{5,4},{6,5},{7,6},{8,7},{9,8},{10,9},{11,1... | collective-permute-start | bytes 196616 | tf_op jit(solution)/shard_map/ppermute | solution.py:391
  8.2 20.1 %all-to-all-start = ((f32[32,32,128]{2,1,0:T(8,128)}), f32[32,32,128]{2,1,0:T(8,128)S(1)}, u32[]{:S(2)}, u32[]{:S(2)}) async-start(f32[32,32,128]{2,1,0:T(8,128)} %get-tuple-element.11), calls=%async_computation | async-start | bytes 1048576 | tf_op jit(solution)/shard_map/all_to_all | solution.py:392
